TPU v7x, 512 devices: a whole 4x8x8 slice. The times are simulated.
512 devices in a mesh: sec: 64 (over x, z, core), op: 8 (over y).
Axes of the slice: x: 4, y: 8, z: 8, core: 2. Of those that a mesh axis runs over, the one named last changes fastest.
Arguments:
- wavefunction: bfloat16 [4096, 32, 384], P('sec'), may hold values from -6 to 6
- left_environment: bfloat16 [1024, 16, 32, 32], P('sec', 'op'), may hold values from -1 to 1
- right_environment: bfloat16 [128, 16, 384, 384], P('sec', 'op'), may hold values from -0.078125 to 0.078125
- left_table: int32 [4096, 3], P('sec'), may hold values from 0 to 63, as said below
- right_table: int32 [8192], P('sec'), may hold values from -1 to 1, as said below
Outputs:
- sigma: bfloat16 [4096, 32, 384], P('sec', None, 'op')
Inputs may be any that keep to these rules, and one draw needn't show every extreme that they name: `left_table`: row g: column 0 is a left sector of the block's owner (below 16), column 1 the right owner along sec, column 2 a slot below 2; no two blocks of one left owner share columns 1 and 2; every left owner sends exactly 2 blocks to some right owner. `right_table`: entry p * 2 + c of right owner d's 128 entries is the right sector (below 2) of the block that left owner p sends to d in slot c, and -1 where p sends none there; it agrees with left_table.
All inputs are finite; a program needn't handle non-finite values.
Results may differ from a plain program's by a relative error of at most 0.017.
Values may be sent and summed in bfloat16 or wider, within the bound.
No kernel may reach another device: no remote copies, remote signals or barrier semaphores. Data moves between devices by JAX's collectives and lax.ppermute only.
A program may use at most 64 MiB of HBM per device.

v0:
```python
import math

import jax
import jax.numpy as jnp
from jax import lax
from jax.sharding import PartitionSpec as P


def contract_left(wavefunction, left_sector, left_environment):
    item_count, row_count, col_count = wavefunction.shape
    terms_here = left_environment.shape[1]
    group_size = math.gcd(item_count, 16)

    def one_group(members):
        block_data, sector_ids = members
        chosen = jnp.take(left_environment, sector_ids, axis=0)
        return jnp.einsum(
            "jkab,jbc->jkac", chosen, block_data, preferred_element_type=jnp.float32
        ).astype(jnp.bfloat16)

    result = lax.map(
        one_group,
        (
            wavefunction.reshape(item_count // group_size, group_size, row_count, col_count),
            left_sector.reshape(item_count // group_size, group_size),
        ),
    )
    return result.reshape(item_count, terms_here, row_count, col_count)


def contract_right(products, sector_ids, live_weight, right_environment):
    item_count, terms_here, row_count, col_count = products.shape
    group_size = math.gcd(item_count, 8)

    def one_group(members):
        block_data, group_ids, group_live = members
        chosen = jnp.take(right_environment, group_ids, axis=0)
        summed = jnp.einsum(
            "jkab,jkbc->jac", block_data, chosen, preferred_element_type=jnp.float32
        )
        return (summed * group_live[:, None, None]).astype(jnp.bfloat16)

    result = lax.map(
        one_group,
        (
            products.reshape(
                item_count // group_size, group_size, terms_here, row_count, col_count
            ),
            sector_ids.reshape(item_count // group_size, group_size),
            live_weight.reshape(item_count // group_size, group_size),
        ),
    )
    return result.reshape(item_count, row_count, col_count)


def per_device(wavefunction, left_environment, right_environment, left_table, right_table):
    owners = lax.axis_size("sec")
    slot_count = right_table.shape[0]
    capacity = slot_count // owners
    row_count = wavefunction.shape[1]
    col_count = wavefunction.shape[2]
    left_sector = left_table[:, 0]
    target = left_table[:, 1] * capacity + left_table[:, 2]
    slot_live = (right_table >= 0).astype(jnp.float32)
    slot_sector = jnp.maximum(right_table, 0)
    products = contract_left(wavefunction, left_sector, left_environment)
    terms_here = products.shape[1]
    send_buffer = (
        jnp.zeros((slot_count, terms_here, row_count, col_count), jnp.bfloat16)
        .at[target]
        .set(products)
    )
    partial_value = contract_right(
        lax.all_to_all(send_buffer, "sec", split_axis=0, concat_axis=0, tiled=True),
        slot_sector,
        slot_live,
        right_environment,
    )
    returned = lax.all_to_all(partial_value, "sec", split_axis=0, concat_axis=0, tiled=True)
    own_blocks = jnp.take(returned, target, axis=0)
    summed = lax.psum_scatter(
        own_blocks.astype(jnp.float32).astype(jnp.bfloat16), "op", scatter_dimension=2, tiled=True
    )
    return summed


def solution(mesh):
    in_specs = (
        P("sec", None, None),
        P("sec", "op", None, None),
        P("sec", "op", None, None),
        P("sec", None),
        P("sec"),
    )
    out_specs = P("sec", None, "op")
    return jax.shard_map(
        per_device, mesh=mesh, in_specs=in_specs, out_specs=out_specs, check_vma=False
    )
```

profile of v0, /device:TPU:1, one launch (start us, length us, event | category | flops | bytes accessed | tf_op | source)
XLA Modules:
  0.0 452.0 jit_solution(8047811733091863679)
XLA Ops:
  8.1 12.3 %while.20 = (s32[]{:T(128)}, bf16[4,16,2,32,384]{4,3,2,1,0:T(8,128)(2,1)S(1)}, s32[4,16]{1,0:T(4,128)S(1)}, bf16[16,2,32,32]{3,2,1,0:T(8,128)(2,1)}, bf16[4,16,32,384]{3,2,1,0:T(8,128)(2,1)}, /*index=5*/s32[]{:T(128)}) while((s32[]{:T(128)}, bf16[4,16,2,32,384]{4,3,2,1,0:T(8,128)(2,1)S(1)}, s32[4,16]{1,0:T(4,128)S(1)}, ...), condition=%wide.region_1.2_spmd, body=%wide.region_0.1_spmd.sunk | while | flops 25592976 | bytes 1578909 | solution.py:21
  24.1 9.6 %scatter_fusion = bf16[128,2,32,384]{3,2,1,0:T(8,128)(2,1)} fusion(bf16[128,2,32,384]{3,2,1,0:T(8,128)(2,1)} %broadcast_in_dim.51, s32[64]{0:T(128)S(1)} %bitcast.76, bf16[64,2,32,384]{3,2,1,0:T(8,128)(2,1)S(1)} %bitcast.74), kind=kCustom, calls=%fused_computation.3 | custom fusion | bytes 9437440 | tf_op jit(solution)/shard_map/scatter | solution.py:71
  33.7 15.1 %all-to-all-start = ((bf16[128,2,32,384]{3,2,1,0:T(8,128)(2,1)}), bf16[128,2,32,384]{3,2,1,0:T(8,128)(2,1)}, u32[]{:S(2)}, u32[]{:S(2)}) async-start(bf16[128,2,32,384]{3,2,1,0:T(8,128)(2,1)} %scatter_fusion), calls=%async_computation | async-start | bytes 12582912 | tf_op jit(solution)/shard_map/all_to_all | solution.py:74
  49.0 140.6 %all-to-all-done = bf16[128,2,32,384]{3,2,1,0:T(8,128)(2,1)} async-done(((bf16[128,2,32,384]{3,2,1,0:T(8,128)(2,1)}), bf16[128,2,32,384]{3,2,1,0:T(8,128)(2,1)}, u32[]{:S(2)}, u32[]{:S(2)}) %all-to-all-start) | async-done | bytes 6291488 | tf_op jit(solution)/shard_map/all_to_all | solution.py:74
  189.6 121.3 %while.21 = (s32[]{:T(128)}, bf16[16,8,32,384]{3,2,1,0:T(8,128)(2,1)}, bf16[16,8,2,32,384]{4,3,2,1,0:T(8,128)(2,1)}, s32[16,8]{1,0:T(8,128)S(1)}, bf16[2,2,384,3...) while((s32[]{:T(128)}, bf16[16,8,32,384]{3,2,1,0:T(8,128)(2,1)}, ...), condition=%wide.region_4.5_spmd, body=%wide.region_3.4_spmd.sunk | while | flops 153551952 | bytes 14751081 | solution.py:43
  193.1 4.1 fusion.52
  200.7 4.1 fusion.52
  208.3 4.1 fusion.52
  215.9 4.1 fusion.52
  223.4 4.1 fusion.52
  231.0 4.1 fusion.52
  246.2 4.1 fusion.52
  253.7 4.1 fusion.52
  261.3 4.1 fusion.52
  268.9 4.1 fusion.52
  276.5 4.1 fusion.52
  284.1 4.1 fusion.52
  291.7 4.1 fusion.52
  299.3 4.1 fusion.52
  306.8 4.1 fusion.52
  310.9 5.8 %all-to-all-start.1 = ((bf16[128,32,384]{2,1,0:T(8,128)(2,1)}), bf16[128,32,384]{2,1,0:T(8,128)(2,1)S(1)}, u32[]{:S(2)}, u32[]{:S(2)}) async-start(bf16[128,32,384]{2,1,0:T(8,128)(2,1)} %bitcast.73), calls=%async_computation.1 | async-start | bytes 6291456 | tf_op jit(solution)/shard_map/all_to_all | solution.py:79
  316.8 73.4 %all-to-all-done.1 = bf16[128,32,384]{2,1,0:T(8,128)(2,1)S(1)} async-done(((bf16[128,32,384]{2,1,0:T(8,128)(2,1)}), bf16[128,32,384]{2,1,0:T(8,128)(2,1)S(1)}, u32[]{:S(2)}, u32[]{:S(2)}) %all-to-all-start.1) | async-done | bytes 3145760 | tf_op jit(solution)/shard_map/all_to_all | solution.py:79
  393.8 6.1 %copy.7 = bf16[64,32,384]{0,1,2:T(8,128)(2,1)} copy(bf16[64,32,384]{2,1,0:T(8,128)(2,1)S(1)} %broadcast_select_fusion) | data formatting | bytes 3145728 | tf_op jit(solution)/shard_map/jit(_take)/select_n | solution.py:80
  400.0 43.3 %reduce-scatter.2.cloned.1.call-done = bf16[64,32,48]{0,1,2:T(8,128)(2,1)} async-done(((bf16[64,32,384]{0,1,2:T(8,128)(2,1)}), bf16[64,32,48]{0,1,2:T(8,128)(2,1)}) %reduce-scatter.2.cloned.1.call-update) | async-done | bytes 196624 | tf_op jit(solution)/shard_map/reduce_scatter | solution.py:81
  (121 shorter events, 83.0 us)
Async XLA Ops:
  33.7 15.1 %copy-start.1 = (s32[128]{0:T(128)S(1)}, s32[128]{0:T(128)}, u32[]{:S(2)}) copy-start(s32[128]{0:T(128)} %param.13) | copy-start | bytes 1540
  33.7 155.9 %copy-start = (bf16[2,2,384,384]{3,2,1,0:T(8,128)(2,1)S(1)}, bf16[2,2,384,384]{3,2,1,0:T(8,128)(2,1)}, u32[]{:S(2)}) copy-start(bf16[2,2,384,384]{3,2,1,0:T(8,128)(2,1)} %param.11) | copy-start | bytes 3538948
  33.7 155.9 %all-to-all-start = ((bf16[128,2,32,384]{3,2,1,0:T(8,128)(2,1)}), bf16[128,2,32,384]{3,2,1,0:T(8,128)(2,1)}, u32[]{:S(2)}, u32[]{:S(2)}) async-start(bf16[128,2,32,384]{3,2,1,0:T(8,128)(2,1)} %scatter_fusion), calls=%async_computation | async-start | bytes 12582912 | tf_op jit(solution)/shard_map/all_to_all | solution.py:74
  310.9 79.3 %all-to-all-start.1 = ((bf16[128,32,384]{2,1,0:T(8,128)(2,1)}), bf16[128,32,384]{2,1,0:T(8,128)(2,1)S(1)}, u32[]{:S(2)}, u32[]{:S(2)}) async-start(bf16[128,32,384]{2,1,0:T(8,128)(2,1)} %bitcast.73), calls=%async_computation.1 | async-start | bytes 6291456 | tf_op jit(solution)/shard_map/all_to_all | solution.py:79
  316.7 126.6 %reduce-scatter.2.cloned.1.call-start = ((), (), s32[]{:S(2)}) async-start(), calls=%async_computation.3 | async-start | bytes 3538944 | tf_op jit(solution)/shard_map/reduce_scatter | solution.py:81
Sparse Core Ops, SparseCore 0:
  400.1 43.1 reduce-scatter.1
where the time goes:
time: 455 us; the launch traced here: 452 us
  waiting for transfers between devices  257 us (56%)
  local copies, waits for them, and re-layouts  85.7 us (19%)
  matrix products  71.2 us (16%)
  starting transfers between devices  20.9 us (5%)
  between operations  13.5 us (3%)
    all_to_all x1, waiting for transfers between devices, per_device(): lax.all_to_all(send_buffer, 'sec', split_axis=0, concat_axis=0, tiled=True)  141 us
    all_to_all x1, waiting for transfers between devices, per_device(): lax.all_to_all(partial_value, 'sec', split_axis=0, concat_axis=0, tiled=T...  73.4 us
    dot_general x16, matrix products, one_group(): jnp.einsum('jkab,jkbc->jac', block_data, chosen, preferred_element_type=j...  65.4 us
    gather x16, local copies, waits for them, and re-layouts, one_group(): chosen = jnp.take(right_environment, group_ids, axis=0)  55.1 us
    reduce_scatter x1, waiting for transfers between devices, per_device(): lax.psum_scatter(own_blocks.astype(jnp.float32).astype(jnp.bfloat16), 'op...  43.3 us
    all_to_all x1, starting transfers between devices, per_device(): lax.all_to_all(send_buffer, 'sec', split_axis=0, concat_axis=0, tiled=True)  15.1 us
    scatter x1, local copies, waits for them, and re-layouts, per_device(): send_buffer = jnp.zeros((slot_count, terms_here, row_count, col_count), j...  9.55 us
  transfers between devices with their start and end apart: 3, of which 3 were waited for; matrix products, arithmetic and copies ran while one was open for 0% of the time, Pallas kernels for 0%

commit v1 on v0

v1 whole, which is shorter than its diff:
```python
import functools

import jax
import jax.numpy as jnp
from jax import lax
from jax.experimental import pallas as pl
from jax.experimental.pallas import tpu as pltpu
from jax.sharding import PartitionSpec as P

BF16 = jnp.bfloat16
F32 = jnp.float32


def iota(shape, dim):
    return lax.broadcasted_iota(jnp.int32, shape, dim)


def contract_kernel(sector_ref, psi_ref, left_ref, *rest):
    right_refs, (out_ref, right_scr, x_scr, part_scr, piece_scr, sem) = rest[:7], rest[7:]
    copies = []
    for term in range(8):
        for sector in range(2):
            source = right_refs[0].at[sector, term] if term < 2 else right_refs[term - 1].at[sector]
            copies.append(
                pltpu.make_async_copy(
                    source,
                    right_scr.at[pl.ds(term * 384, 384), pl.ds(sector * 384, 384)],
                    sem.at[term * 2 + sector],
                )
            )
    for copy in copies:
        copy.start()

    lane, column = iota((128, 256), 0), iota((128, 256), 1)
    spread = [
        jnp.where(((lane >> 5) == kk) & ((lane & 31) == (column & 31)), 1.0, 0.0).astype(BF16)
        for kk in range(4)
    ]
    same_block = (iota((256, 256), 0) >> 5) == (iota((256, 256), 1) >> 5)

    def left_group(index, carry):
        left = left_ref[pl.ds(index * 8, 8)].reshape(256, 128)
        psi = psi_ref[pl.ds(index * 8, 8)].reshape(256, 384)
        row = pl.multiple_of(index * 128, 128)
        for kk in range(4):
            wide = jnp.dot(left, spread[kk], preferred_element_type=F32)
            wide = jnp.where(same_block, wide, 0.0).astype(BF16)
            product = jnp.dot(wide, psi, preferred_element_type=F32).astype(BF16)
            product = product.reshape(8, 2, 16, 384)
            for half in range(2):
                term = half * 4 + kk
                x_scr[pl.ds(row, 128), term * 384 : term * 384 + 384] = product[:, half].reshape(128, 384)
        return carry

    lax.fori_loop(0, 8, left_group, 0)
    for copy in copies:
        copy.wait()

    place = iota((384, 384), 1)
    wanted = 48 * ((place >> 4) & 7) + 16 * (place >> 7) + (place & 15)
    reorder = jnp.where(iota((384, 384), 0) == wanted, 1.0, 0.0).astype(BF16)

    def right_group(index, carry):
        row = pl.multiple_of(index * 256, 256)
        total = jnp.dot(x_scr[pl.ds(row, 256), :], right_scr[...], preferred_element_type=F32)
        chosen = []
        for j in range(16):
            entry = sector_ref[index * 16 + j]
            rows = total[j * 16 : j * 16 + 16]
            rows = jnp.where(entry == 1, rows[:, 384:], rows[:, :384])
            chosen.append(jnp.where(entry >= 0, rows, 0.0))
        chosen = jnp.concatenate(chosen, axis=0).astype(BF16)
        ordered = jnp.dot(chosen, reorder, preferred_element_type=F32)
        for tile in range(3):
            part_scr[pl.ds(tile * 1024 + row, 256), :] = ordered[:, tile * 128 : tile * 128 + 128]
        return carry

    lax.fori_loop(0, 4, right_group, 0)

    lane_group = iota((64, 128), 1) >> 4
    for upper in range(2):
        for tile in range(3):
            rows = [
                part_scr[pl.ds(tile * 1024 + upper * 8 + a, 64, stride=16), :]
                for a in range(8)
            ]
            for bit in range(3):
                low_lane = ((lane_group >> bit) & 1) == 0
                shift = 16 << bit
                for a in range(8):
                    if a & (1 << bit):
                        continue
                    first, second = rows[a], rows[a | (1 << bit)]
                    rows[a] = jnp.where(low_lane, first, pltpu.roll(second, shift, 1))
                    rows[a | (1 << bit)] = jnp.where(low_lane, pltpu.roll(first, 128 - shift, 1), second)
            for target in range(8):
                piece_scr[pl.ds(target * 6 + upper * 3 + tile, 64, stride=48), :] = rows[target]
    out_ref[...] = piece_scr[...].astype(BF16)


def contract(slot_sector, psi, left, rights):
    vmem = pl.BlockSpec(memory_space=pltpu.VMEM)
    return pl.pallas_call(
        contract_kernel,
        out_shape=jax.ShapeDtypeStruct((3072, 128), BF16),
        in_specs=[pl.BlockSpec(memory_space=pltpu.SMEM), vmem, vmem]
        + [pl.BlockSpec(memory_space=pl.ANY)] * 7,
        out_specs=vmem,
        scratch_shapes=[
            pltpu.VMEM((3072, 768), BF16),
            pltpu.VMEM((1024, 3072), BF16),
            pltpu.VMEM((3072, 128), F32),
            pltpu.VMEM((3072, 128), F32),
            pltpu.SemaphoreType.DMA((16,)),
        ],
        compiler_params=pltpu.CompilerParams(vmem_limit_bytes=40 << 20),
        cost_estimate=pl.CostEstimate(flops=7_000_000_000, bytes_accessed=8_000_000, transcendentals=0),
        name="contract",
    )(slot_sector, psi, left, *rights)


def collect_kernel(table_ref, piece_ref, out_ref, wide_scr):
    wide_scr[...] = piece_ref[...].astype(F32)
    slot = iota((64, 256), 1)
    owner = table_ref[:, 1:2]
    place = table_ref[:, 2:3]
    pick = jnp.where(((slot >> 2) == owner) & ((slot & 1) == place), 1.0, 0.0).astype(BF16)
    for half in range(2):
        for upper in range(2):
            for tile in range(3):
                rows = wide_scr[pl.ds(half * 6 + upper * 3 + tile, 256, stride=12), :].astype(BF16)
                total = jnp.dot(pick, rows, preferred_element_type=F32)
                first = half * 16 + upper * 8
                out_ref[first : first + 8, tile * 16 : tile * 16 + 16, :] = (
                    total.T.reshape(8, 16, 64).astype(BF16)
                )


def collect(left_table, pieces):
    vmem = pl.BlockSpec(memory_space=pltpu.VMEM)
    return pl.pallas_call(
        collect_kernel,
        out_shape=jax.ShapeDtypeStruct((32, 48, 64), BF16),
        in_specs=[vmem, vmem],
        out_specs=vmem,
        scratch_shapes=[pltpu.VMEM((3072, 128), F32)],
        name="collect",
    )(left_table, pieces)


def per_device(psi, left, right, left_table, right_table):
    me = lax.axis_index("op")
    slot, half = (me >> 1) & 1, me & 1
    hop = lambda value, step: lax.ppermute(value, "op", [(i, (i + step) % 8) for i in range(8)])

    match = (left_table[:, 1:2] == jnp.arange(64)[None, :]) & (left_table[:, 2:3] == slot)
    source = jnp.sum(jnp.where(match, jnp.arange(64)[:, None], 0), axis=0)
    left_of = jnp.sum(jnp.where(match, left_table[:, :1], 0), axis=0)
    psi_there = lax.all_to_all(
        psi.at[source].get(mode="promise_in_bounds"), "sec", split_axis=0, concat_axis=0, tiled=True
    )

    dense = left.reshape(16, 2, 2, 16, 32).transpose(0, 3, 2, 1, 4).reshape(16, 16, 128)
    before, after = hop(dense, 1), hop(dense, -1)
    two_before, two_after = hop(dense, 2), hop(dense, -2)
    part = lambda value: jnp.where(half == 0, value[:, :, :64], value[:, :, 64:])
    table = jnp.concatenate(
        [
            jnp.concatenate([part(dense), part(before)], axis=2),
            jnp.concatenate([part(after), part(two_before)[:, :, 32:], part(two_after)[:, :, :32]], axis=2),
        ],
        axis=1,
    )
    first, second = right[:, 0], right[:, 1]
    left_here, psi_there, before_second, after_first, before_first, after_second = lax.optimization_barrier(
        (
            table.at[left_of].get(mode="promise_in_bounds"),
            psi_there,
            hop(second, 1),
            hop(first, -1),
            hop(first, 1),
            hop(second, -1),
        )
    )
    left_there = lax.all_to_all(left_here, "sec", split_axis=0, concat_axis=0, tiled=True)
    two_before_second, two_after_first = hop(before_second, 1), hop(after_first, -1)

    slot_sector = jnp.where(slot == 0, right_table.reshape(64, 2)[:, 0], right_table.reshape(64, 2)[:, 1])
    pieces = contract(
        slot_sector,
        psi_there,
        left_there,
        [right, before_first, before_second, after_first, after_second, two_before_second, two_after_first],
    )
    pieces = lax.all_to_all(
        pieces.reshape(512, 3, 2, 128), ("sec", "op"), split_axis=0, concat_axis=0, tiled=True
    )
    return collect(left_table, pieces.reshape(3072, 128)).transpose(2, 0, 1)


def solution(mesh):
    in_specs = (
        P("sec", None, None),
        P("sec", "op", None, None),
        P("sec", "op", None, None),
        P("sec", None),
        P("sec"),
    )
    out_specs = P("sec", None, "op")
    return jax.shard_map(
        per_device, mesh=mesh, in_specs=in_specs, out_specs=out_specs, check_vma=False
    )
```

time: 455 us -> 171 us (0.38)
  waiting for transfers between devices: 257 us -> 56.4 us
  local copies, waits for them, and re-layouts: 85.7 us -> 12 us
  matrix products: 71.2 us -> 0 us
  starting transfers between devices: 20.9 us -> 78.5 us
  Pallas kernels: 0 us -> 21.1 us
  between operations: 13.5 us -> 0.32 us
    all_to_all x2 -> x3, waiting for transfers between devices: 214 us -> 26.2 us  [the longest x1 26.2 us: per_device(): lax.all_to_all(pieces.reshape(512, 3, 2, 128), ('sec', 'op'), split_axis=...]
    dot_general x20 -> x0, matrix products: 71.2 us -> none  [the longest x16 65.4 us: one_group(): jnp.einsum('jkab,jkbc->jac', block_data, chosen, preferred_element_type=j...]
    gather x21 -> x2, local copies, waits for them, and re-layouts: 63.3 us -> 3.39 us  [the longest x1 1.94 us: per_device(): psi.at[source].get(mode='promise_in_bounds')]
    reduce_scatter x1 -> x0, waiting for transfers between devices: 43.3 us -> none  [per_device(): lax.psum_scatter(own_blocks.astype(jnp.float32).astype(jnp.bfloat16), 'op...]
    ppermute x0 -> x10, starting transfers between devices: none -> 32.7 us  [per_device(): lax.ppermute(value, 'op', [(i, (i + step) % 8) for i in range(8)])]
    ppermute x0 -> x10, waiting for transfers between devices: none -> 30.3 us  [per_device(): lax.ppermute(value, 'op', [(i, (i + step) % 8) for i in range(8)])]
    all_to_all x2 -> x3, starting transfers between devices: 20.8 us -> 45.8 us  [the longest x1 18 us: per_device(): lax.all_to_all(pieces.reshape(512, 3, 2, 128), ('sec', 'op'), split_axis=...]
    pallas_call x0 -> x2, Pallas kernels: none -> 21.1 us  [the longest x1 18.7 us: contract(): pl.pallas_call(contract_kernel, out_shape=jax.ShapeDtypeStruct((3072, 128...]
  transfers between devices with their start and end apart: 3 -> 13, of which waited for: 3 -> 4; matrix products, arithmetic and copies ran while one was open for 0% -> 4% of each run, Pallas kernels for 0% -> 0%
where the time goes in v1:
time: 171 us; the launch traced here: 170 us
  starting transfers between devices  78.5 us (46%)
  waiting for transfers between devices  56.4 us (33%)
  Pallas kernels  21.1 us (12%)
  local copies, waits for them, and re-layouts  12 us (7%)
    ppermute x10, starting transfers between devices, per_device(): lax.ppermute(value, 'op', [(i, (i + step) % 8) for i in range(8)])  32.7 us
    ppermute x10, waiting for transfers between devices, per_device(): lax.ppermute(value, 'op', [(i, (i + step) % 8) for i in range(8)])  30.3 us
    all_to_all x1, waiting for transfers between devices, per_device(): lax.all_to_all(pieces.reshape(512, 3, 2, 128), ('sec', 'op'), split_axis=...  26.2 us
    pallas_call x1, Pallas kernels, contract(): pl.pallas_call(contract_kernel, out_shape=jax.ShapeDtypeStruct((3072, 128...  18.7 us
    all_to_all x1, starting transfers between devices, per_device(): lax.all_to_all(pieces.reshape(512, 3, 2, 128), ('sec', 'op'), split_axis=...  18 us
    all_to_all x1, starting transfers between devices, per_device(): lax.all_to_all(psi.at[source].get(mode='promise_in_bounds'), 'sec', split...  14.8 us
    all_to_all x1, starting transfers between devices, per_device(): lax.all_to_all(left_here, 'sec', split_axis=0, concat_axis=0, tiled=True)  12.9 us
    unnamed x13, local copies, waits for them, and re-layouts  3.76 us
  transfers between devices with their start and end apart: 13, of which 4 were waited for; matrix products, arithmetic and copies ran while one was open for 4% of the time, Pallas kernels for 0%

profile of v1, /device:TPU:1, one launch (start us, length us, event | category | flops | bytes accessed | tf_op | source)
XLA Modules:
  0.0 169.9 jit_solution(4141234151439065899)
XLA Ops:
  1.7 1.9 %gather_fusion.1 = bf16[64,32,384]{2,1,0:T(8,128)(2,1)} fusion(bf16[64,32,384]{2,1,0:T(8,128)(2,1)S(1)} %copy-done, s32[1024]{0:T(1024)S(1)} %pad_clamp_fusion), kind=kCustom, calls=%fused_computation.1 | custom fusion | bytes 3145984 | tf_op jit(solution)/shard_map/gather | solution.py:160
  3.6 14.8 %all-to-all-start = ((bf16[64,32,384]{2,1,0:T(8,128)(2,1)}), bf16[64,32,384]{2,1,0:T(8,128)(2,1)S(1)}, u32[]{:S(2)}, u32[]{:S(2)}) async-start(bf16[64,32,384]{2,1,0:T(8,128)(2,1)} %gather_fusion.1), calls=%async_computation | async-start | bytes 3145728 | tf_op jit(solution)/shard_map/all_to_all | solution.py:159
  18.4 1.2 copy.20
  19.8 4.2 %collective-permute-start.2 = (bf16[16,16,128]{2,1,0:T(8,128)(2,1)S(1)}, bf16[16,16,128]{2,1,0:T(8,128)(2,1)S(1)}, u32[]{:S(2)}, u32[]{:S(2)}) collective-permute-start(bf16[16,16,128]{2,1,0:T(8,128)(2,1)S(1)} %reshape.46), channel_id=1, source_target_pairs={{0,2},{1,3},{2,4},{3,5},{4,6},{5,7},{6,0},{7,1},{8,10},{9,11},{10,... | collective-permute-start | bytes 196616 | tf_op jit(solution)/shard_map/ppermute | solution.py:154
  24.0 3.6 %collective-permute-start.3 = (bf16[16,16,128]{2,1,0:T(8,128)(2,1)S(1)}, bf16[16,16,128]{2,1,0:T(8,128)(2,1)S(1)}, u32[]{:S(2)}, u32[]{:S(2)}) collective-permute-start(bf16[16,16,128]{2,1,0:T(8,128)(2,1)S(1)} %reshape.46), channel_id=1, source_target_pairs={{0,6},{1,7},{2,0},{3,1},{4,2},{5,3},{6,4},{7,5},{8,14},{9,15},{10,... | collective-permute-start | bytes 196616 | tf_op jit(solution)/shard_map/ppermute | solution.py:154
  27.6 3.5 %collective-permute-start.1 = (bf16[16,16,128]{2,1,0:T(8,128)(2,1)S(1)}, bf16[16,16,128]{2,1,0:T(8,128)(2,1)S(1)}, u32[]{:S(2)}, u32[]{:S(2)}) collective-permute-start(bf16[16,16,128]{2,1,0:T(8,128)(2,1)S(1)} %reshape.46), channel_id=1, source_target_pairs={{0,7},{1,0},{2,1},{3,2},{4,3},{5,4},{6,5},{7,6},{8,15},{9,8},{10,9... | collective-permute-start | bytes 196616 | tf_op jit(solution)/shard_map/ppermute | solution.py:154
  31.1 1.9 %collective-permute-start = (bf16[16,16,128]{2,1,0:T(8,128)(2,1)S(1)}, bf16[16,16,128]{2,1,0:T(8,128)(2,1)S(1)}, u32[]{:S(2)}, u32[]{:S(2)}) collective-permute-start(bf16[16,16,128]{2,1,0:T(8,128)(2,1)S(1)} %reshape.46), channel_id=1, source_target_pairs={{0,1},{1,2},{2,3},{3,4},{4,5},{5,6},{6,7},{7,0},{8,9},{9,10},{10,1... | collective-permute-start | bytes 196616 | tf_op jit(solution)/shard_map/ppermute | solution.py:154
  33.1 2.4 %slice_bitcast_fusion = (bf16[2,384,384]{2,1,0:T(8,128)(2,1)}, bf16[2,384,384]{2,1,0:T(8,128)(2,1)}) fusion(bf16[2,2,384,384]{3,2,1,0:T(8,128)(2,1)} %rest_0_.1), kind=kLoop, calls=%fused_computation.2 | loop fusion | bytes 2359296 | tf_op jit(solution)/shard_map/squeeze | solution.py:174
  35.4 4.6 %collective-permute-start.5 = (bf16[2,384,384]{2,1,0:T(8,128)(2,1)}, bf16[2,384,384]{2,1,0:T(8,128)(2,1)}, u32[]{:S(2)}, u32[]{:S(2)}) collective-permute-start(bf16[2,384,384]{2,1,0:T(8,128)(2,1)} %get-tuple-element.19), channel_id=1, source_target_pairs={{0,7},{1,0},{2,1},{3,2},{4,3},{5,4},{6,5},{7,6},{8,15},{9,8},{10,9... | collective-permute-start | bytes 1769480 | tf_op jit(solution)/shard_map/ppermute | solution.py:154
  40.1 1.9 %collective-permute-start.6 = (bf16[2,384,384]{2,1,0:T(8,128)(2,1)}, bf16[2,384,384]{2,1,0:T(8,128)(2,1)}, u32[]{:S(2)}, u32[]{:S(2)}) collective-permute-start(bf16[2,384,384]{2,1,0:T(8,128)(2,1)} %get-tuple-element.19), channel_id=1, source_target_pairs={{0,1},{1,2},{2,3},{3,4},{4,5},{5,6},{6,7},{7,0},{8,9},{9,10},{10,1... | collective-permute-start | bytes 1769480 | tf_op jit(solution)/shard_map/ppermute | solution.py:154
  42.2 1.9 %collective-permute-start.4 = (bf16[2,384,384]{2,1,0:T(8,128)(2,1)}, bf16[2,384,384]{2,1,0:T(8,128)(2,1)}, u32[]{:S(2)}, u32[]{:S(2)}) collective-permute-start(bf16[2,384,384]{2,1,0:T(8,128)(2,1)} %get-tuple-element.20), channel_id=1, source_target_pairs={{0,1},{1,2},{2,3},{3,4},{4,5},{5,6},{6,7},{7,0},{8,9},{9,10},{10,1... | collective-permute-start | bytes 1769480 | tf_op jit(solution)/shard_map/ppermute | solution.py:154
  44.2 4.6 %collective-permute-start.7 = (bf16[2,384,384]{2,1,0:T(8,128)(2,1)}, bf16[2,384,384]{2,1,0:T(8,128)(2,1)}, u32[]{:S(2)}, u32[]{:S(2)}) collective-permute-start(bf16[2,384,384]{2,1,0:T(8,128)(2,1)} %get-tuple-element.20), channel_id=1, source_target_pairs={{0,7},{1,0},{2,1},{3,2},{4,3},{5,4},{6,5},{7,6},{8,15},{9,8},{10,9... | collective-permute-start | bytes 1769480 | tf_op jit(solution)/shard_map/ppermute | solution.py:154
  49.2 1.5 gather_fusion
  50.7 18.5 %collective-permute-done.4.rest_2_ = bf16[2,384,384]{2,1,0:T(8,128)(2,1)} collective-permute-done((bf16[2,384,384]{2,1,0:T(8,128)(2,1)}, bf16[2,384,384]{2,1,0:T(8,128)(2,1)}, u32[]{:S(2)}, u32[]{:S(2)}) %collective-permute-start.4) | collective-permute-done | bytes 589856 | tf_op jit(solution)/shard_map/ppermute | solution.py:154
  69.2 12.9 %all-to-all-start.1 = ((bf16[64,32,128]{2,1,0:T(8,128)(2,1)}), bf16[64,32,128]{2,1,0:T(8,128)(2,1)}, u32[]{:S(2)}, u32[]{:S(2)}) async-start(bf16[64,32,128]{2,1,0:T(8,128)(2,1)} %gather_fusion), calls=%async_computation.1 | async-start | bytes 1048576 | tf_op jit(solution)/shard_map/all_to_all | solution.py:185
  82.1 1.9 %collective-permute-start.8 = (bf16[2,384,384]{2,1,0:T(8,128)(2,1)}, bf16[2,384,384]{2,1,0:T(8,128)(2,1)}, u32[]{:S(2)}, u32[]{:S(2)}) collective-permute-start(bf16[2,384,384]{2,1,0:T(8,128)(2,1)} %collective-permute-done.4.rest_2_), channel_id=1, source_target_pairs={{0,1},{1,2},{2,3},{3,4},{4,5},{5,6},{6,7},{7,0},{8,9},{9,10},{10,1... | collective-permute-start | bytes 1769480 | tf_op jit(solution)/shard_map/ppermute | solution.py:154
  84.1 4.6 %collective-permute-start.9 = (bf16[2,384,384]{2,1,0:T(8,128)(2,1)}, bf16[2,384,384]{2,1,0:T(8,128)(2,1)}, u32[]{:S(2)}, u32[]{:S(2)}) collective-permute-start(bf16[2,384,384]{2,1,0:T(8,128)(2,1)} %collective-permute-done.5.rest_3_), channel_id=1, source_target_pairs={{0,7},{1,0},{2,1},{3,2},{4,3},{5,4},{6,5},{7,6},{8,15},{9,8},{10,9... | collective-permute-start | bytes 1769480 | tf_op jit(solution)/shard_map/ppermute | solution.py:154
  89.0 10.9 %collective-permute-done.8.rest_5_ = bf16[2,384,384]{2,1,0:T(8,128)(2,1)} collective-permute-done((bf16[2,384,384]{2,1,0:T(8,128)(2,1)}, bf16[2,384,384]{2,1,0:T(8,128)(2,1)}, u32[]{:S(2)}, u32[]{:S(2)}) %collective-permute-start.8) | collective-permute-done | bytes 589856 | tf_op jit(solution)/shard_map/ppermute | solution.py:154
  100.8 1.3 copy-done.1
  102.1 18.7 %contract.1 = bf16[3072,128]{1,0:T(8,128)(2,1)S(1)} custom-call(s32[64]{0:T(128)S(1)} %fusion.sector_ref, bf16[64,32,384]{2,1,0:T(8,128)(2,1)S(1)} %all-to-all-done.psi_ref, bf16[64,32,128]{2,1,0:T(8,128)(2,1)} %all-to-all-done.1.left_ref, bf16[2,2,384,384]{3,2,1,0:T(8,128)(2,1)S(1)} %copy-done.1, bf16[2,384,384]{2,1,0:T(8,128)(2,1)} %collective-permute-done.6.rest_1_, ...), custom_call_target="tpu_custom_call" | custom-call | flops 7000000000 | bytes 8000000 | tf_op jit(solution)/shard_map/contract/pallas_call | solution.py:103
  121.7 18.0 %all-to-all-start.2 = ((bf16[512,3,2,128]{3,2,1,0:T(2,128)(2,1)}), bf16[512,3,2,128]{3,2,1,0:T(2,128)(2,1)S(1)}, u32[]{:S(2)}, u32[]{:S(2)}) async-start(bf16[512,3,2,128]{3,2,1,0:T(2,128)(2,1)} %bitcast.29), calls=%async_computation.2 | async-start | bytes 1572864 | tf_op jit(solution)/shard_map/all_to_all | solution.py:195
  140.5 26.2 %all-to-all-done.2 = bf16[512,3,2,128]{3,2,1,0:T(2,128)(2,1)S(1)} async-done(((bf16[512,3,2,128]{3,2,1,0:T(2,128)(2,1)}), bf16[512,3,2,128]{3,2,1,0:T(2,128)(2,1)S(1)}, u32[]{:S(2)}, u32[]{:S(2)}) %all-to-all-start.2) | async-done | bytes 786464 | tf_op jit(solution)/shard_map/all_to_all | solution.py:195
  166.6 0.9 copy-done.3
  167.5 2.4 %collect.1 = bf16[32,48,64]{2,1,0:T(8,128)(2,1)} custom-call(s32[64,3]{1,0:T(8,128)} %copy.16.table_ref, bf16[3072,128]{1,0:T(8,128)(2,1)} %bitcast.30), custom_call_target="tpu_custom_call" | custom-call | tf_op jit(solution)/shard_map/collect/pallas_call | solution.py:141
  (38 shorter events, 5.3 us)
Async XLA Ops:
  0.0 1.6 copy-start
  3.6 65.6 %all-to-all-start = ((bf16[64,32,384]{2,1,0:T(8,128)(2,1)}), bf16[64,32,384]{2,1,0:T(8,128)(2,1)S(1)}, u32[]{:S(2)}, u32[]{:S(2)}) async-start(bf16[64,32,384]{2,1,0:T(8,128)(2,1)} %gather_fusion.1), calls=%async_computation | async-start | bytes 3145728 | tf_op jit(solution)/shard_map/all_to_all | solution.py:159
  19.8 20.3 %collective-permute-start.2 = (bf16[16,16,128]{2,1,0:T(8,128)(2,1)S(1)}, bf16[16,16,128]{2,1,0:T(8,128)(2,1)S(1)}, u32[]{:S(2)}, u32[]{:S(2)}) collective-permute-start(bf16[16,16,128]{2,1,0:T(8,128)(2,1)S(1)} %reshape.46), channel_id=1, source_target_pairs={{0,2},{1,3},{2,4},{3,5},{4,6},{5,7},{6,0},{7,1},{8,10},{9,11},{10,... | collective-permute-start | bytes 196616 | tf_op jit(solution)/shard_map/ppermute | solution.py:154
  24.0 24.9 %collective-permute-start.3 = (bf16[16,16,128]{2,1,0:T(8,128)(2,1)S(1)}, bf16[16,16,128]{2,1,0:T(8,128)(2,1)S(1)}, u32[]{:S(2)}, u32[]{:S(2)}) collective-permute-start(bf16[16,16,128]{2,1,0:T(8,128)(2,1)S(1)} %reshape.46), channel_id=1, source_target_pairs={{0,6},{1,7},{2,0},{3,1},{4,2},{5,3},{6,4},{7,5},{8,14},{9,15},{10,... | collective-permute-start | bytes 196616 | tf_op jit(solution)/shard_map/ppermute | solution.py:154
  27.6 14.5 %collective-permute-start.1 = (bf16[16,16,128]{2,1,0:T(8,128)(2,1)S(1)}, bf16[16,16,128]{2,1,0:T(8,128)(2,1)S(1)}, u32[]{:S(2)}, u32[]{:S(2)}) collective-permute-start(bf16[16,16,128]{2,1,0:T(8,128)(2,1)S(1)} %reshape.46), channel_id=1, source_target_pairs={{0,7},{1,0},{2,1},{3,2},{4,3},{5,4},{6,5},{7,6},{8,15},{9,8},{10,9... | collective-permute-start | bytes 196616 | tf_op jit(solution)/shard_map/ppermute | solution.py:154
  31.1 13.1 %collective-permute-start = (bf16[16,16,128]{2,1,0:T(8,128)(2,1)S(1)}, bf16[16,16,128]{2,1,0:T(8,128)(2,1)S(1)}, u32[]{:S(2)}, u32[]{:S(2)}) collective-permute-start(bf16[16,16,128]{2,1,0:T(8,128)(2,1)S(1)} %reshape.46), channel_id=1, source_target_pairs={{0,1},{1,2},{2,3},{3,4},{4,5},{5,6},{6,7},{7,0},{8,9},{9,10},{10,1... | collective-permute-start | bytes 196616 | tf_op jit(solution)/shard_map/ppermute | solution.py:154
  35.4 33.7 %collective-permute-start.5 = (bf16[2,384,384]{2,1,0:T(8,128)(2,1)}, bf16[2,384,384]{2,1,0:T(8,128)(2,1)}, u32[]{:S(2)}, u32[]{:S(2)}) collective-permute-start(bf16[2,384,384]{2,1,0:T(8,128)(2,1)} %get-tuple-element.19), channel_id=1, source_target_pairs={{0,7},{1,0},{2,1},{3,2},{4,3},{5,4},{6,5},{7,6},{8,15},{9,8},{10,9... | collective-permute-start | bytes 1769480 | tf_op jit(solution)/shard_map/ppermute | solution.py:154
  40.1 29.0 %collective-permute-start.6 = (bf16[2,384,384]{2,1,0:T(8,128)(2,1)}, bf16[2,384,384]{2,1,0:T(8,128)(2,1)}, u32[]{:S(2)}, u32[]{:S(2)}) collective-permute-start(bf16[2,384,384]{2,1,0:T(8,128)(2,1)} %get-tuple-element.19), channel_id=1, source_target_pairs={{0,1},{1,2},{2,3},{3,4},{4,5},{5,6},{6,7},{7,0},{8,9},{9,10},{10,1... | collective-permute-start | bytes 1769480 | tf_op jit(solution)/shard_map/ppermute | solution.py:154
  42.2 27.0 %collective-permute-start.4 = (bf16[2,384,384]{2,1,0:T(8,128)(2,1)}, bf16[2,384,384]{2,1,0:T(8,128)(2,1)}, u32[]{:S(2)}, u32[]{:S(2)}) collective-permute-start(bf16[2,384,384]{2,1,0:T(8,128)(2,1)} %get-tuple-element.20), channel_id=1, source_target_pairs={{0,1},{1,2},{2,3},{3,4},{4,5},{5,6},{6,7},{7,0},{8,9},{9,10},{10,1... | collective-permute-start | bytes 1769480 | tf_op jit(solution)/shard_map/ppermute | solution.py:154
  44.2 25.0 %collective-permute-start.7 = (bf16[2,384,384]{2,1,0:T(8,128)(2,1)}, bf16[2,384,384]{2,1,0:T(8,128)(2,1)}, u32[]{:S(2)}, u32[]{:S(2)}) collective-permute-start(bf16[2,384,384]{2,1,0:T(8,128)(2,1)} %get-tuple-element.20), channel_id=1, source_target_pairs={{0,7},{1,0},{2,1},{3,2},{4,3},{5,4},{6,5},{7,6},{8,15},{9,8},{10,9... | collective-permute-start | bytes 1769480 | tf_op jit(solution)/shard_map/ppermute | solution.py:154
  48.9 39.8 %copy-start.5 = (s32[128]{0:T(128)S(1)}, s32[128]{0:T(128)}, u32[]{:S(2)}) copy-start(s32[128]{0:T(128)} %param.9) | copy-start | bytes 1540
  69.2 31.6 %all-to-all-start.1 = ((bf16[64,32,128]{2,1,0:T(8,128)(2,1)}), bf16[64,32,128]{2,1,0:T(8,128)(2,1)}, u32[]{:S(2)}, u32[]{:S(2)}) async-start(bf16[64,32,128]{2,1,0:T(8,128)(2,1)} %gather_fusion), calls=%async_computation.1 | async-start | bytes 1048576 | tf_op jit(solution)/shard_map/all_to_all | solution.py:185
  82.1 17.8 %collective-permute-start.8 = (bf16[2,384,384]{2,1,0:T(8,128)(2,1)}, bf16[2,384,384]{2,1,0:T(8,128)(2,1)}, u32[]{:S(2)}, u32[]{:S(2)}) collective-permute-start(bf16[2,384,384]{2,1,0:T(8,128)(2,1)} %collective-permute-done.4.rest_2_), channel_id=1, source_target_pairs={{0,1},{1,2},{2,3},{3,4},{4,5},{5,6},{6,7},{7,0},{8,9},{9,10},{10,1... | collective-permute-start | bytes 1769480 | tf_op jit(solution)/shard_map/ppermute | solution.py:154
  84.1 16.7 %collective-permute-start.9 = (bf16[2,384,384]{2,1,0:T(8,128)(2,1)}, bf16[2,384,384]{2,1,0:T(8,128)(2,1)}, u32[]{:S(2)}, u32[]{:S(2)}) collective-permute-start(bf16[2,384,384]{2,1,0:T(8,128)(2,1)} %collective-permute-done.5.rest_3_), channel_id=1, source_target_pairs={{0,7},{1,0},{2,1},{3,2},{4,3},{5,4},{6,5},{7,6},{8,15},{9,8},{10,9... | collective-permute-start | bytes 1769480 | tf_op jit(solution)/shard_map/ppermute | solution.py:154
  100.8 1.3 copy-start.1
  120.8 0.9 copy-start.2
  121.7 18.1 %copy-start.4 = (s32[64,3]{0,1:T(4,128)S(1)}, s32[64,3]{0,1:T(4,128)}, u32[]{:S(2)}) copy-start(s32[64,3]{0,1:T(4,128)} %param.8) | copy-start | bytes 2308
  121.7 44.9 %all-to-all-start.2 = ((bf16[512,3,2,128]{3,2,1,0:T(2,128)(2,1)}), bf16[512,3,2,128]{3,2,1,0:T(2,128)(2,1)S(1)}, u32[]{:S(2)}, u32[]{:S(2)}) async-start(bf16[512,3,2,128]{3,2,1,0:T(2,128)(2,1)} %bitcast.29), calls=%async_computation.2 | async-start | bytes 1572864 | tf_op jit(solution)/shard_map/all_to_all | solution.py:195
  166.6 0.9 copy-start.3

commit v2 on v1

--- a/solution.py
+++ b/solution.py
@@ -16,11 +16,16 @@
 
 
 def contract_kernel(sector_ref, psi_ref, left_ref, *rest):
-    right_refs, (out_ref, right_scr, x_scr, part_scr, piece_scr, sem) = rest[:7], rest[7:]
+    right_refs, (out_ref, right_scr, x_scr, part_scr, piece_scr, sem) = rest[:5], rest[5:]
     copies = []
     for term in range(8):
         for sector in range(2):
-            source = right_refs[0].at[sector, term] if term < 2 else right_refs[term - 1].at[sector]
+            if term < 2:
+                source = right_refs[0].at[sector, term]
+            elif term < 6:
+                source = right_refs[term // 2].at[term % 2, sector]
+            else:
+                source = right_refs[term - 3].at[sector]
             copies.append(
                 pltpu.make_async_copy(
                     source,
@@ -31,28 +36,29 @@
     for copy in copies:
         copy.start()
 
-    lane, column = iota((128, 256), 0), iota((128, 256), 1)
-    spread = [
-        jnp.where(((lane >> 5) == kk) & ((lane & 31) == (column & 31)), 1.0, 0.0).astype(BF16)
-        for kk in range(4)
-    ]
+    lane, column = iota((128, 1024), 0), iota((128, 1024), 1)
+    spread = jnp.where(
+        ((lane >> 5) == (column >> 8)) & ((lane & 31) == (column & 31)), 1.0, 0.0
+    ).astype(BF16)
     same_block = (iota((256, 256), 0) >> 5) == (iota((256, 256), 1) >> 5)
 
     def left_group(index, carry):
         left = left_ref[pl.ds(index * 8, 8)].reshape(256, 128)
         psi = psi_ref[pl.ds(index * 8, 8)].reshape(256, 384)
         row = pl.multiple_of(index * 128, 128)
+        wide = jnp.dot(left, spread, preferred_element_type=F32)
+        wide = jnp.concatenate(
+            [jnp.where(same_block, wide[:, kk * 256 : kk * 256 + 256], 0.0).astype(BF16) for kk in range(4)],
+            axis=0,
+        )
+        product = jnp.dot(wide, psi, preferred_element_type=F32).astype(BF16).reshape(4, 8, 2, 16, 384)
         for kk in range(4):
-            wide = jnp.dot(left, spread[kk], preferred_element_type=F32)
-            wide = jnp.where(same_block, wide, 0.0).astype(BF16)
-            product = jnp.dot(wide, psi, preferred_element_type=F32).astype(BF16)
-            product = product.reshape(8, 2, 16, 384)
             for half in range(2):
                 term = half * 4 + kk
-                x_scr[pl.ds(row, 128), term * 384 : term * 384 + 384] = product[:, half].reshape(128, 384)
+                x_scr[pl.ds(row, 128), term * 384 : term * 384 + 384] = product[kk, :, half].reshape(128, 384)
         return carry
 
-    lax.fori_loop(0, 8, left_group, 0)
+    lax.fori_loop(0, 8, left_group, 0, unroll=2)
     for copy in copies:
         copy.wait()
 
@@ -61,21 +67,21 @@
     reorder = jnp.where(iota((384, 384), 0) == wanted, 1.0, 0.0).astype(BF16)
 
     def right_group(index, carry):
-        row = pl.multiple_of(index * 256, 256)
-        total = jnp.dot(x_scr[pl.ds(row, 256), :], right_scr[...], preferred_element_type=F32)
+        row = pl.multiple_of(index * 1024, 1024)
+        total = jnp.dot(x_scr[pl.ds(row, 1024), :], right_scr[...], preferred_element_type=F32)
         chosen = []
-        for j in range(16):
-            entry = sector_ref[index * 16 + j]
+        for j in range(64):
+            entry = sector_ref[index * 64 + j]
             rows = total[j * 16 : j * 16 + 16]
             rows = jnp.where(entry == 1, rows[:, 384:], rows[:, :384])
             chosen.append(jnp.where(entry >= 0, rows, 0.0))
         chosen = jnp.concatenate(chosen, axis=0).astype(BF16)
         ordered = jnp.dot(chosen, reorder, preferred_element_type=F32)
         for tile in range(3):
-            part_scr[pl.ds(tile * 1024 + row, 256), :] = ordered[:, tile * 128 : tile * 128 + 128]
+            part_scr[pl.ds(tile * 1024 + row, 1024), :] = ordered[:, tile * 128 : tile * 128 + 128]
         return carry
 
-    lax.fori_loop(0, 4, right_group, 0)
+    lax.fori_loop(0, 1, right_group, 0)
 
     lane_group = iota((64, 128), 1) >> 4
     for upper in range(2):
@@ -104,7 +110,7 @@
         contract_kernel,
         out_shape=jax.ShapeDtypeStruct((3072, 128), BF16),
         in_specs=[pl.BlockSpec(memory_space=pltpu.SMEM), vmem, vmem]
-        + [pl.BlockSpec(memory_space=pl.ANY)] * 7,
+        + [pl.BlockSpec(memory_space=pltpu.HBM)] * 5,
         out_specs=vmem,
         scratch_shapes=[
             pltpu.VMEM((3072, 768), BF16),
@@ -113,7 +119,7 @@
             pltpu.VMEM((3072, 128), F32),
             pltpu.SemaphoreType.DMA((16,)),
         ],
-        compiler_params=pltpu.CompilerParams(vmem_limit_bytes=40 << 20),
+        compiler_params=pltpu.CompilerParams(vmem_limit_bytes=60 << 20),
         cost_estimate=pl.CostEstimate(flops=7_000_000_000, bytes_accessed=8_000_000, transcendentals=0),
         name="contract",
     )(slot_sector, psi, left, *rights)
@@ -144,6 +150,7 @@
         in_specs=[vmem, vmem],
         out_specs=vmem,
         scratch_shapes=[pltpu.VMEM((3072, 128), F32)],
+        compiler_params=pltpu.CompilerParams(vmem_limit_bytes=60 << 20),
         name="collect",
     )(left_table, pieces)
 
@@ -161,8 +168,10 @@
     )
 
     dense = left.reshape(16, 2, 2, 16, 32).transpose(0, 3, 2, 1, 4).reshape(16, 16, 128)
-    before, after = hop(dense, 1), hop(dense, -1)
-    two_before, two_after = hop(dense, 2), hop(dense, -2)
+    by_term = right.transpose(1, 0, 2, 3)
+    before, after, two_before, two_after, right_before, right_after = lax.optimization_barrier(
+        (hop(dense, 1), hop(dense, -1), hop(dense, 2), hop(dense, -2), hop(by_term, 1), hop(by_term, -1))
+    )
     part = lambda value: jnp.where(half == 0, value[:, :, :64], value[:, :, 64:])
     table = jnp.concatenate(
         [
@@ -171,26 +180,18 @@
         ],
         axis=1,
     )
-    first, second = right[:, 0], right[:, 1]
-    left_here, psi_there, before_second, after_first, before_first, after_second = lax.optimization_barrier(
-        (
-            table.at[left_of].get(mode="promise_in_bounds"),
-            psi_there,
-            hop(second, 1),
-            hop(first, -1),
-            hop(first, 1),
-            hop(second, -1),
-        )
+    left_here, psi_there = lax.optimization_barrier(
+        (table.at[left_of].get(mode="promise_in_bounds"), psi_there)
     )
     left_there = lax.all_to_all(left_here, "sec", split_axis=0, concat_axis=0, tiled=True)
-    two_before_second, two_after_first = hop(before_second, 1), hop(after_first, -1)
+    right_two_before, right_two_after = hop(right_before[1], 1), hop(right_after[0], -1)
 
     slot_sector = jnp.where(slot == 0, right_table.reshape(64, 2)[:, 0], right_table.reshape(64, 2)[:, 1])
     pieces = contract(
         slot_sector,
         psi_there,
         left_there,
-        [right, before_first, before_second, after_first, after_second, two_before_second, two_after_first],
+        [right, right_before, right_after, right_two_before, right_two_after],
     )
     pieces = lax.all_to_all(
         pieces.reshape(512, 3, 2, 128), ("sec", "op"), split_axis=0, concat_axis=0, tiled=True

time: 171 us -> 163 us (0.953)
  starting transfers between devices: 78.5 us -> 71.6 us
  Pallas kernels: 21.1 us -> 16.3 us
  waiting for transfers between devices: 56.4 us -> 59.1 us
    ppermute x10 -> x8, starting transfers between devices: 32.7 us -> 26.1 us  [per_device(): lax.ppermute(value, 'op', [(i, (i + step) % 8) for i in range(8)])]
    pallas_call x1, Pallas kernels: 18.7 us -> 13.9 us  [contract(): pl.pallas_call(contract_kernel, out_shape=jax.ShapeDtypeStruct((3072, 128...]
    ppermute x10 -> x8, waiting for transfers between devices: 30.3 us -> 33 us  [per_device(): lax.ppermute(value, 'op', [(i, (i + step) % 8) for i in range(8)])]
    squeeze x1 -> x2, local copies, waits for them, and re-layouts: 2.38 us -> 3.88 us  [the longest x1 1.95 us: per_device(): right_before[1]]
    unnamed x13 -> x14, local copies, waits for them, and re-layouts: 3.76 us -> 4.05 us
  transfers between devices with their start and end apart: 13 -> 11, of which waited for: 4 -> 5; matrix products, arithmetic and copies ran while one was open for 4% -> 6% of each run, Pallas kernels for 0% -> 0%
where the time goes in v2:
time: 163 us; the launch traced here: 162 us
  starting transfers between devices  71.6 us (44%)
  waiting for transfers between devices  59.1 us (36%)
  Pallas kernels  16.3 us (10%)
  local copies, waits for them, and re-layouts  12.7 us (8%)
  other arithmetic  1.95 us (1%)
    ppermute x8, waiting for transfers between devices, per_device(): lax.ppermute(value, 'op', [(i, (i + step) % 8) for i in range(8)])  33 us
    all_to_all x1, waiting for transfers between devices, per_device(): lax.all_to_all(pieces.reshape(512, 3, 2, 128), ('sec', 'op'), split_axis=...  26.2 us
    ppermute x8, starting transfers between devices, per_device(): lax.ppermute(value, 'op', [(i, (i + step) % 8) for i in range(8)])  26.1 us
    all_to_all x1, starting transfers between devices, per_device(): lax.all_to_all(pieces.reshape(512, 3, 2, 128), ('sec', 'op'), split_axis=...  17.4 us
    all_to_all x1, starting transfers between devices, per_device(): lax.all_to_all(psi.at[source].get(mode='promise_in_bounds'), 'sec', split...  14.8 us
    pallas_call x1, Pallas kernels, contract(): pl.pallas_call(contract_kernel, out_shape=jax.ShapeDtypeStruct((3072, 128...  13.9 us
    all_to_all x1, starting transfers between devices, per_device(): lax.all_to_all(left_here, 'sec', split_axis=0, concat_axis=0, tiled=True)  13.2 us
    unnamed x14, local copies, waits for them, and re-layouts  4.05 us
  transfers between devices with their start and end apart: 11, of which 5 were waited for; matrix products, arithmetic and copies ran while one was open for 6% of the time, Pallas kernels for 0%

profile of v2, /device:TPU:1, one launch (start us, length us, event | category | flops | bytes accessed | tf_op | source)
XLA Modules:
  0.0 161.9 jit_solution(888736769197738608)
XLA Ops:
  1.7 1.9 %gather_fusion.1 = bf16[64,32,384]{2,1,0:T(8,128)(2,1)} fusion(bf16[64,32,384]{2,1,0:T(8,128)(2,1)S(1)} %copy-done, s32[1024]{0:T(1024)S(1)} %pad_clamp_fusion), kind=kCustom, calls=%fused_computation.1 | custom fusion | bytes 3145984 | tf_op jit(solution)/shard_map/gather | solution.py:167
  3.6 14.8 %all-to-all-start = ((bf16[64,32,384]{2,1,0:T(8,128)(2,1)}), bf16[64,32,384]{2,1,0:T(8,128)(2,1)S(1)}, u32[]{:S(2)}, u32[]{:S(2)}) async-start(bf16[64,32,384]{2,1,0:T(8,128)(2,1)} %gather_fusion.1), calls=%async_computation | async-start | bytes 3145728 | tf_op jit(solution)/shard_map/all_to_all | solution.py:166
  18.4 2.4 %copy.16 = bf16[2,2,384,384]{3,2,0,1:T(8,128)(2,1)} copy(bf16[2,2,384,384]{3,2,1,0:T(8,128)(2,1)} %rest_0_.1) | data formatting | bytes 2359296 | tf_op args[2]
  20.9 3.2 %collective-permute-start.4 = (bf16[2,2,384,384]{3,2,1,0:T(8,128)(2,1)}, bf16[2,2,384,384]{3,2,1,0:T(8,128)(2,1)}, u32[]{:S(2)}, u32[]{:S(2)}) collective-permute-start(bf16[2,2,384,384]{3,2,1,0:T(8,128)(2,1)} %bitcast.26), channel_id=1, source_target_pairs={{0,1},{1,2},{2,3},{3,4},{4,5},{5,6},{6,7},{7,0},{8,9},{9,10},{10,1... | collective-permute-start | bytes 3538952 | tf_op jit(solution)/shard_map/ppermute | solution.py:161
  24.1 3.8 %collective-permute-start.5 = (bf16[2,2,384,384]{3,2,1,0:T(8,128)(2,1)}, bf16[2,2,384,384]{3,2,1,0:T(8,128)(2,1)}, u32[]{:S(2)}, u32[]{:S(2)}) collective-permute-start(bf16[2,2,384,384]{3,2,1,0:T(8,128)(2,1)} %bitcast.26), channel_id=1, source_target_pairs={{0,7},{1,0},{2,1},{3,2},{4,3},{5,4},{6,5},{7,6},{8,15},{9,8},{10,9... | collective-permute-start | bytes 3538952 | tf_op jit(solution)/shard_map/ppermute | solution.py:161
  28.3 1.9 %collective-permute-start = (bf16[16,16,128]{2,1,0:T(8,128)(2,1)S(1)}, bf16[16,16,128]{2,1,0:T(8,128)(2,1)S(1)}, u32[]{:S(2)}, u32[]{:S(2)}) collective-permute-start(bf16[16,16,128]{2,1,0:T(8,128)(2,1)S(1)} %reshape.46), channel_id=1, source_target_pairs={{0,1},{1,2},{2,3},{3,4},{4,5},{5,6},{6,7},{7,0},{8,9},{9,10},{10,1... | collective-permute-start | bytes 196616 | tf_op jit(solution)/shard_map/ppermute | solution.py:161
  30.2 4.6 %collective-permute-start.1 = (bf16[16,16,128]{2,1,0:T(8,128)(2,1)S(1)}, bf16[16,16,128]{2,1,0:T(8,128)(2,1)S(1)}, u32[]{:S(2)}, u32[]{:S(2)}) collective-permute-start(bf16[16,16,128]{2,1,0:T(8,128)(2,1)S(1)} %reshape.46), channel_id=1, source_target_pairs={{0,7},{1,0},{2,1},{3,2},{4,3},{5,4},{6,5},{7,6},{8,15},{9,8},{10,9... | collective-permute-start | bytes 196616 | tf_op jit(solution)/shard_map/ppermute | solution.py:161
  34.8 2.2 %collective-permute-start.2 = (bf16[16,16,128]{2,1,0:T(8,128)(2,1)S(1)}, bf16[16,16,128]{2,1,0:T(8,128)(2,1)S(1)}, u32[]{:S(2)}, u32[]{:S(2)}) collective-permute-start(bf16[16,16,128]{2,1,0:T(8,128)(2,1)S(1)} %reshape.46), channel_id=1, source_target_pairs={{0,2},{1,3},{2,4},{3,5},{4,6},{5,7},{6,0},{7,1},{8,10},{9,11},{10,... | collective-permute-start | bytes 196616 | tf_op jit(solution)/shard_map/ppermute | solution.py:161
  37.1 16.4 %collective-permute-done = bf16[16,16,128]{2,1,0:T(8,128)(2,1)S(1)} collective-permute-done((bf16[16,16,128]{2,1,0:T(8,128)(2,1)S(1)}, bf16[16,16,128]{2,1,0:T(8,128)(2,1)S(1)}, u32[]{:S(2)}, u32[]{:S(2)}) %collective-permute-start) | collective-permute-done | bytes 65568 | tf_op jit(solution)/shard_map/ppermute | solution.py:161
  53.5 3.9 %collective-permute-start.3 = (bf16[16,16,128]{2,1,0:T(8,128)(2,1)S(1)}, bf16[16,16,128]{2,1,0:T(8,128)(2,1)S(1)}, u32[]{:S(2)}, u32[]{:S(2)}) collective-permute-start(bf16[16,16,128]{2,1,0:T(8,128)(2,1)S(1)} %reshape.46), channel_id=1, source_target_pairs={{0,6},{1,7},{2,0},{3,1},{4,2},{5,3},{6,4},{7,5},{8,14},{9,15},{10,... | collective-permute-start | bytes 196616 | tf_op jit(solution)/shard_map/ppermute | solution.py:161
  57.5 2.4 %collective-permute-done.3 = bf16[16,16,128]{2,1,0:T(8,128)(2,1)S(1)} collective-permute-done((bf16[16,16,128]{2,1,0:T(8,128)(2,1)S(1)}, bf16[16,16,128]{2,1,0:T(8,128)(2,1)S(1)}, u32[]{:S(2)}, u32[]{:S(2)}) %collective-permute-start.3) | collective-permute-done | bytes 65568 | tf_op jit(solution)/shard_map/ppermute | solution.py:161
  60.3 1.4 gather_fusion
  61.8 13.2 %all-to-all-start.1 = ((bf16[64,32,128]{2,1,0:T(8,128)(2,1)}), bf16[64,32,128]{2,1,0:T(8,128)(2,1)}, u32[]{:S(2)}, u32[]{:S(2)}) async-start(bf16[64,32,128]{2,1,0:T(8,128)(2,1)} %gather_fusion), calls=%async_computation.1 | async-start | bytes 1048576 | tf_op jit(solution)/shard_map/all_to_all | solution.py:186
  74.9 2.0 %slice_bitcast_fusion.1 = bf16[2,384,384]{2,1,0:T(8,128)(2,1)} fusion(bf16[2,2,384,384]{3,2,1,0:T(8,128)(2,1)} %collective-permute-done.4.rest_1_), kind=kLoop, calls=%fused_computation.4 | loop fusion | bytes 1179648 | tf_op jit(solution)/shard_map/squeeze | solution.py:187
  76.9 2.3 %collective-permute-start.6 = (bf16[2,384,384]{2,1,0:T(8,128)(2,1)}, bf16[2,384,384]{2,1,0:T(8,128)(2,1)}, u32[]{:S(2)}, u32[]{:S(2)}) collective-permute-start(bf16[2,384,384]{2,1,0:T(8,128)(2,1)} %slice_bitcast_fusion.1), channel_id=1, source_target_pairs={{0,1},{1,2},{2,3},{3,4},{4,5},{5,6},{6,7},{7,0},{8,9},{9,10},{10,1... | collective-permute-start | bytes 1769480 | tf_op jit(solution)/shard_map/ppermute | solution.py:161
  79.2 1.9 %slice_bitcast_fusion = bf16[2,384,384]{2,1,0:T(8,128)(2,1)} fusion(bf16[2,2,384,384]{3,2,1,0:T(8,128)(2,1)} %collective-permute-done.5.rest_2_), kind=kLoop, calls=%fused_computation.3 | loop fusion | bytes 1179648 | tf_op jit(solution)/shard_map/squeeze | solution.py:187
  81.1 4.2 %collective-permute-start.7 = (bf16[2,384,384]{2,1,0:T(8,128)(2,1)}, bf16[2,384,384]{2,1,0:T(8,128)(2,1)}, u32[]{:S(2)}, u32[]{:S(2)}) collective-permute-start(bf16[2,384,384]{2,1,0:T(8,128)(2,1)} %slice_bitcast_fusion), channel_id=1, source_target_pairs={{0,7},{1,0},{2,1},{3,2},{4,3},{5,4},{6,5},{7,6},{8,15},{9,8},{10,9... | collective-permute-start | bytes 1769480 | tf_op jit(solution)/shard_map/ppermute | solution.py:161
  86.2 8.6 %collective-permute-done.6.rest_3_ = bf16[2,384,384]{2,1,0:T(8,128)(2,1)} collective-permute-done((bf16[2,384,384]{2,1,0:T(8,128)(2,1)}, bf16[2,384,384]{2,1,0:T(8,128)(2,1)}, u32[]{:S(2)}, u32[]{:S(2)}) %collective-permute-start.6) | collective-permute-done | bytes 589856 | tf_op jit(solution)/shard_map/ppermute | solution.py:161
  94.8 5.6 %collective-permute-done.7.rest_4_ = bf16[2,384,384]{2,1,0:T(8,128)(2,1)} collective-permute-done((bf16[2,384,384]{2,1,0:T(8,128)(2,1)}, bf16[2,384,384]{2,1,0:T(8,128)(2,1)}, u32[]{:S(2)}, u32[]{:S(2)}) %collective-permute-start.7) | collective-permute-done | bytes 589856 | tf_op jit(solution)/shard_map/ppermute | solution.py:161
  100.4 13.9 %contract.1 = bf16[3072,128]{1,0:T(8,128)(2,1)} custom-call(s32[64]{0:T(128)} %fusion.sector_ref, bf16[64,32,384]{2,1,0:T(8,128)(2,1)} %copy-done.2, bf16[64,32,128]{2,1,0:T(8,128)(2,1)} %all-to-all-done.1.left_ref, bf16[2,2,384,384]{3,2,1,0:T(8,128)(2,1)} %rest_0_.1, bf16[2,2,384,384]{3,2,1,0:T(8,128)(2,1)} %collective-permute-done.4.rest_1_, ...), custom_call_target="tpu_custom_call" | custom-call | flops 7000000000 | bytes 8000000 | tf_op jit(solution)/shard_map/contract/pallas_call | solution.py:109
  114.3 17.4 %all-to-all-start.2 = ((bf16[512,3,2,128]{3,2,1,0:T(2,128)(2,1)}), bf16[512,3,2,128]{3,2,1,0:T(2,128)(2,1)S(1)}, u32[]{:S(2)}, u32[]{:S(2)}) async-start(bf16[512,3,2,128]{3,2,1,0:T(2,128)(2,1)} %bitcast.30), calls=%async_computation.2 | async-start | bytes 1572864 | tf_op jit(solution)/shard_map/all_to_all | solution.py:196
  132.5 26.2 %all-to-all-done.2 = bf16[512,3,2,128]{3,2,1,0:T(2,128)(2,1)S(1)} async-done(((bf16[512,3,2,128]{3,2,1,0:T(2,128)(2,1)}), bf16[512,3,2,128]{3,2,1,0:T(2,128)(2,1)S(1)}, u32[]{:S(2)}, u32[]{:S(2)}) %all-to-all-start.2) | async-done | bytes 786464 | tf_op jit(solution)/shard_map/all_to_all | solution.py:196
  158.7 0.9 copy-done.1
  159.6 2.4 %collect.1 = bf16[32,48,64]{2,1,0:T(8,128)(2,1)} custom-call(s32[64,3]{1,0:T(8,128)} %copy.13.table_ref, bf16[3072,128]{1,0:T(8,128)(2,1)} %bitcast.28), custom_call_target="tpu_custom_call" | custom-call | tf_op jit(solution)/shard_map/collect/pallas_call | solution.py:147
  (34 shorter events, 4.1 us)
Async XLA Ops:
  0.0 1.7 %copy-start = (bf16[64,32,384]{2,1,0:T(8,128)(2,1)S(1)}, bf16[64,32,384]{2,1,0:T(8,128)(2,1)}, u32[]{:S(2)}) copy-start(bf16[64,32,384]{2,1,0:T(8,128)(2,1)} %param.5) | copy-start | bytes 4718596
  3.6 58.2 %all-to-all-start = ((bf16[64,32,384]{2,1,0:T(8,128)(2,1)}), bf16[64,32,384]{2,1,0:T(8,128)(2,1)S(1)}, u32[]{:S(2)}, u32[]{:S(2)}) async-start(bf16[64,32,384]{2,1,0:T(8,128)(2,1)} %gather_fusion.1), calls=%async_computation | async-start | bytes 3145728 | tf_op jit(solution)/shard_map/all_to_all | solution.py:166
  18.4 9.5 %copy-start.3 = (bf16[16,2,32,32]{3,2,1,0:T(8,128)(2,1)S(1)}, bf16[16,2,32,32]{3,2,1,0:T(8,128)(2,1)}, u32[]{:S(2)}) copy-start(bf16[16,2,32,32]{3,2,1,0:T(8,128)(2,1)} %param.6) | copy-start | bytes 196612
  20.9 39.0 %collective-permute-start.4 = (bf16[2,2,384,384]{3,2,1,0:T(8,128)(2,1)}, bf16[2,2,384,384]{3,2,1,0:T(8,128)(2,1)}, u32[]{:S(2)}, u32[]{:S(2)}) collective-permute-start(bf16[2,2,384,384]{3,2,1,0:T(8,128)(2,1)} %bitcast.26), channel_id=1, source_target_pairs={{0,1},{1,2},{2,3},{3,4},{4,5},{5,6},{6,7},{7,0},{8,9},{9,10},{10,1... | collective-permute-start | bytes 3538952 | tf_op jit(solution)/shard_map/ppermute | solution.py:161
  24.1 35.8 %collective-permute-start.5 = (bf16[2,2,384,384]{3,2,1,0:T(8,128)(2,1)}, bf16[2,2,384,384]{3,2,1,0:T(8,128)(2,1)}, u32[]{:S(2)}, u32[]{:S(2)}) collective-permute-start(bf16[2,2,384,384]{3,2,1,0:T(8,128)(2,1)} %bitcast.26), channel_id=1, source_target_pairs={{0,7},{1,0},{2,1},{3,2},{4,3},{5,4},{6,5},{7,6},{8,15},{9,8},{10,9... | collective-permute-start | bytes 3538952 | tf_op jit(solution)/shard_map/ppermute | solution.py:161
  28.3 25.2 %collective-permute-start = (bf16[16,16,128]{2,1,0:T(8,128)(2,1)S(1)}, bf16[16,16,128]{2,1,0:T(8,128)(2,1)S(1)}, u32[]{:S(2)}, u32[]{:S(2)}) collective-permute-start(bf16[16,16,128]{2,1,0:T(8,128)(2,1)S(1)} %reshape.46), channel_id=1, source_target_pairs={{0,1},{1,2},{2,3},{3,4},{4,5},{5,6},{6,7},{7,0},{8,9},{9,10},{10,1... | collective-permute-start | bytes 196616 | tf_op jit(solution)/shard_map/ppermute | solution.py:161
  30.2 27.2 %collective-permute-start.1 = (bf16[16,16,128]{2,1,0:T(8,128)(2,1)S(1)}, bf16[16,16,128]{2,1,0:T(8,128)(2,1)S(1)}, u32[]{:S(2)}, u32[]{:S(2)}) collective-permute-start(bf16[16,16,128]{2,1,0:T(8,128)(2,1)S(1)} %reshape.46), channel_id=1, source_target_pairs={{0,7},{1,0},{2,1},{3,2},{4,3},{5,4},{6,5},{7,6},{8,15},{9,8},{10,9... | collective-permute-start | bytes 196616 | tf_op jit(solution)/shard_map/ppermute | solution.py:161
  34.8 22.6 %collective-permute-start.2 = (bf16[16,16,128]{2,1,0:T(8,128)(2,1)S(1)}, bf16[16,16,128]{2,1,0:T(8,128)(2,1)S(1)}, u32[]{:S(2)}, u32[]{:S(2)}) collective-permute-start(bf16[16,16,128]{2,1,0:T(8,128)(2,1)S(1)} %reshape.46), channel_id=1, source_target_pairs={{0,2},{1,3},{2,4},{3,5},{4,6},{5,7},{6,0},{7,1},{8,10},{9,11},{10,... | collective-permute-start | bytes 196616 | tf_op jit(solution)/shard_map/ppermute | solution.py:161
  53.5 6.4 %collective-permute-start.3 = (bf16[16,16,128]{2,1,0:T(8,128)(2,1)S(1)}, bf16[16,16,128]{2,1,0:T(8,128)(2,1)S(1)}, u32[]{:S(2)}, u32[]{:S(2)}) collective-permute-start(bf16[16,16,128]{2,1,0:T(8,128)(2,1)S(1)} %reshape.46), channel_id=1, source_target_pairs={{0,6},{1,7},{2,0},{3,1},{4,2},{5,3},{6,4},{7,5},{8,14},{9,15},{10,... | collective-permute-start | bytes 196616 | tf_op jit(solution)/shard_map/ppermute | solution.py:161
  61.7 23.6 %copy-start.5 = (s32[128]{0:T(128)S(1)}, s32[128]{0:T(128)}, u32[]{:S(2)}) copy-start(s32[128]{0:T(128)} %param.9) | copy-start | bytes 1540
  61.7 19.4 %copy-start.2 = (bf16[64,32,384]{2,1,0:T(8,128)(2,1)}, bf16[64,32,384]{2,1,0:T(8,128)(2,1)S(1)}, u32[]{:S(2)}) copy-start(bf16[64,32,384]{2,1,0:T(8,128)(2,1)S(1)} %all-to-all-done.psi_ref) | copy-start | bytes 4718596
  61.8 38.6 %all-to-all-start.1 = ((bf16[64,32,128]{2,1,0:T(8,128)(2,1)}), bf16[64,32,128]{2,1,0:T(8,128)(2,1)}, u32[]{:S(2)}, u32[]{:S(2)}) async-start(bf16[64,32,128]{2,1,0:T(8,128)(2,1)} %gather_fusion), calls=%async_computation.1 | async-start | bytes 1048576 | tf_op jit(solution)/shard_map/all_to_all | solution.py:186
  76.9 17.9 %collective-permute-start.6 = (bf16[2,384,384]{2,1,0:T(8,128)(2,1)}, bf16[2,384,384]{2,1,0:T(8,128)(2,1)}, u32[]{:S(2)}, u32[]{:S(2)}) collective-permute-start(bf16[2,384,384]{2,1,0:T(8,128)(2,1)} %slice_bitcast_fusion.1), channel_id=1, source_target_pairs={{0,1},{1,2},{2,3},{3,4},{4,5},{5,6},{6,7},{7,0},{8,9},{9,10},{10,1... | collective-permute-start | bytes 1769480 | tf_op jit(solution)/shard_map/ppermute | solution.py:161
  81.1 19.3 %collective-permute-start.7 = (bf16[2,384,384]{2,1,0:T(8,128)(2,1)}, bf16[2,384,384]{2,1,0:T(8,128)(2,1)}, u32[]{:S(2)}, u32[]{:S(2)}) collective-permute-start(bf16[2,384,384]{2,1,0:T(8,128)(2,1)} %slice_bitcast_fusion), channel_id=1, source_target_pairs={{0,7},{1,0},{2,1},{3,2},{4,3},{5,4},{6,5},{7,6},{8,15},{9,8},{10,9... | collective-permute-start | bytes 1769480 | tf_op jit(solution)/shard_map/ppermute | solution.py:161
  114.3 17.5 %copy-start.4 = (s32[64,3]{0,1:T(4,128)S(1)}, s32[64,3]{0,1:T(4,128)}, u32[]{:S(2)}) copy-start(s32[64,3]{0,1:T(4,128)} %param.8) | copy-start | bytes 2308
  114.3 44.3 %all-to-all-start.2 = ((bf16[512,3,2,128]{3,2,1,0:T(2,128)(2,1)}), bf16[512,3,2,128]{3,2,1,0:T(2,128)(2,1)S(1)}, u32[]{:S(2)}, u32[]{:S(2)}) async-start(bf16[512,3,2,128]{3,2,1,0:T(2,128)(2,1)} %bitcast.30), calls=%async_computation.2 | async-start | bytes 1572864 | tf_op jit(solution)/shard_map/all_to_all | solution.py:196
  158.7 0.9 copy-start.1

commit v3 on v2

--- a/solution.py
+++ b/solution.py
@@ -20,10 +20,8 @@
     copies = []
     for term in range(8):
         for sector in range(2):
-            if term < 2:
-                source = right_refs[0].at[sector, term]
-            elif term < 6:
-                source = right_refs[term // 2].at[term % 2, sector]
+            if term < 6:
+                source = right_refs[term // 2].at[sector, term % 2]
             else:
                 source = right_refs[term - 3].at[sector]
             copies.append(
@@ -127,15 +125,14 @@
 
 def collect_kernel(table_ref, piece_ref, out_ref, wide_scr):
     wide_scr[...] = piece_ref[...].astype(F32)
-    slot = iota((64, 256), 1)
-    owner = table_ref[:, 1:2]
-    place = table_ref[:, 2:3]
-    pick = jnp.where(((slot >> 2) == owner) & ((slot & 1) == place), 1.0, 0.0).astype(BF16)
+    slot = iota((256, 64), 0)
+    chosen = ((slot >> 2) == table_ref[1:2]) & ((slot & 1) == table_ref[2:3])
+    wanted = jnp.where(chosen, 1.0, 0.0).T.astype(BF16)
     for half in range(2):
         for upper in range(2):
             for tile in range(3):
                 rows = wide_scr[pl.ds(half * 6 + upper * 3 + tile, 256, stride=12), :].astype(BF16)
-                total = jnp.dot(pick, rows, preferred_element_type=F32)
+                total = jnp.dot(wanted, rows, preferred_element_type=F32)
                 first = half * 16 + upper * 8
                 out_ref[first : first + 8, tile * 16 : tile * 16 + 16, :] = (
                     total.T.reshape(8, 16, 64).astype(BF16)
@@ -150,9 +147,31 @@
         in_specs=[vmem, vmem],
         out_specs=vmem,
         scratch_shapes=[pltpu.VMEM((3072, 128), F32)],
-        compiler_params=pltpu.CompilerParams(vmem_limit_bytes=60 << 20),
+        compiler_params=pltpu.CompilerParams(vmem_limit_bytes=16 << 20),
         name="collect",
     )(left_table, pieces)
+
+
+def pick_kernel(term, right_ref, out_ref, sem):
+    copies = [
+        pltpu.make_async_copy(right_ref.at[sector, term], out_ref.at[sector], sem.at[sector]) for sector in range(2)
+    ]
+    for copy in copies:
+        copy.start()
+    for copy in copies:
+        copy.wait()
+
+
+def pick(right, term):
+    return pl.pallas_call(
+        functools.partial(pick_kernel, term),
+        out_shape=jax.ShapeDtypeStruct((2, 384, 384), BF16),
+        in_specs=[pl.BlockSpec(memory_space=pltpu.HBM)],
+        out_specs=pl.BlockSpec(memory_space=pltpu.HBM),
+        scratch_shapes=[pltpu.SemaphoreType.DMA((2,))],
+        compiler_params=pltpu.CompilerParams(vmem_limit_bytes=60 << 20),
+        name="pick",
+    )(right)
 
 
 def per_device(psi, left, right, left_table, right_table):
@@ -168,10 +187,8 @@
     )
 
     dense = left.reshape(16, 2, 2, 16, 32).transpose(0, 3, 2, 1, 4).reshape(16, 16, 128)
-    by_term = right.transpose(1, 0, 2, 3)
-    before, after, two_before, two_after, right_before, right_after = lax.optimization_barrier(
-        (hop(dense, 1), hop(dense, -1), hop(dense, 2), hop(dense, -2), hop(by_term, 1), hop(by_term, -1))
-    )
+    before, after, two_before, two_after = hop(dense, 1), hop(dense, -1), hop(dense, 2), hop(dense, -2)
+    right_before, right_after = hop(right, 1), hop(right, -1)
     part = lambda value: jnp.where(half == 0, value[:, :, :64], value[:, :, 64:])
     table = jnp.concatenate(
         [
@@ -184,7 +201,7 @@
         (table.at[left_of].get(mode="promise_in_bounds"), psi_there)
     )
     left_there = lax.all_to_all(left_here, "sec", split_axis=0, concat_axis=0, tiled=True)
-    right_two_before, right_two_after = hop(right_before[1], 1), hop(right_after[0], -1)
+    right_two_before, right_two_after = hop(pick(right_before, 1), 1), hop(pick(right_after, 0), -1)
 
     slot_sector = jnp.where(slot == 0, right_table.reshape(64, 2)[:, 0], right_table.reshape(64, 2)[:, 1])
     pieces = contract(
@@ -196,7 +213,7 @@
     pieces = lax.all_to_all(
         pieces.reshape(512, 3, 2, 128), ("sec", "op"), split_axis=0, concat_axis=0, tiled=True
     )
-    return collect(left_table, pieces.reshape(3072, 128)).transpose(2, 0, 1)
+    return collect(left_table.T, pieces.reshape(3072, 128)).transpose(2, 0, 1)
 
 
 def solution(mesh):

time: 163 us -> 184 us (1.13)
  blocking collectives: 0 us -> 46 us
  Pallas kernels: 16.3 us -> 53.1 us
  waiting for transfers between devices: 59.1 us -> 28.1 us
  starting transfers between devices: 71.6 us -> 47.9 us
  local copies, waits for them, and re-layouts: 12.7 us -> 5.83 us
    all_to_all x0 -> x1, blocking collectives: none -> 46 us  [per_device(): lax.all_to_all(pieces.reshape(512, 3, 2, 128), ('sec', 'op'), split_axis=...]
    pallas_call x0 -> x2, Pallas kernels: none -> 38 us  [pick(): pl.pallas_call(functools.partial(pick_kernel, term), out_shape=jax.ShapeD...]
    all_to_all x1 -> x0, waiting for transfers between devices: 26.2 us -> none  [per_device(): lax.all_to_all(pieces.reshape(512, 3, 2, 128), ('sec', 'op'), split_axis=...]
    ppermute x8, waiting for transfers between devices: 33 us -> 11.6 us  [per_device(): lax.ppermute(value, 'op', [(i, (i + step) % 8) for i in range(8)])]
    all_to_all x1 -> x0, starting transfers between devices: 17.4 us -> none  [per_device(): lax.all_to_all(pieces.reshape(512, 3, 2, 128), ('sec', 'op'), split_axis=...]
    all_to_all x1, waiting for transfers between devices: 0.01 us -> 16.5 us  [per_device(): lax.all_to_all(psi.at[source].get(mode='promise_in_bounds'), 'sec', split...]
    all_to_all x1, starting transfers between devices: 13.2 us -> 6.31 us  [per_device(): lax.all_to_all(left_here, 'sec', split_axis=0, concat_axis=0, tiled=True)]
    unnamed x14 -> x8, local copies, waits for them, and re-layouts: 4.05 us -> 0.02 us
  transfers between devices with their start and end apart: 11 -> 10, of which waited for: 5 -> 2; matrix products, arithmetic and copies ran while one was open for 6% -> 2% of each run, Pallas kernels for 0% -> 21%
where the time goes in v3:
time: 184 us; the launch traced here: 183 us
  Pallas kernels  53.1 us (29%)
  starting transfers between devices  47.9 us (26%)
  blocking collectives  46 us (25%)
  waiting for transfers between devices  28.1 us (15%)
  local copies, waits for them, and re-layouts  5.83 us (3%)
  other arithmetic  2.02 us (1%)
    all_to_all x1, blocking collectives, per_device(): lax.all_to_all(pieces.reshape(512, 3, 2, 128), ('sec', 'op'), split_axis=...  46 us
    pallas_call x2, Pallas kernels, pick(): pl.pallas_call(functools.partial(pick_kernel, term), out_shape=jax.ShapeD...  38 us
    ppermute x8, starting transfers between devices, per_device(): lax.ppermute(value, 'op', [(i, (i + step) % 8) for i in range(8)])  26.7 us
    all_to_all x1, waiting for transfers between devices, per_device(): lax.all_to_all(psi.at[source].get(mode='promise_in_bounds'), 'sec', split...  16.5 us
    all_to_all x1, starting transfers between devices, per_device(): lax.all_to_all(psi.at[source].get(mode='promise_in_bounds'), 'sec', split...  14.8 us
    pallas_call x1, Pallas kernels, contract(): pl.pallas_call(contract_kernel, out_shape=jax.ShapeDtypeStruct((3072, 128...  13.9 us
    ppermute x8, waiting for transfers between devices, per_device(): lax.ppermute(value, 'op', [(i, (i + step) % 8) for i in range(8)])  11.6 us
    all_to_all x1, starting transfers between devices, per_device(): lax.all_to_all(left_here, 'sec', split_axis=0, concat_axis=0, tiled=True)  6.31 us
  transfers between devices with their start and end apart: 10, of which 2 were waited for; matrix products, arithmetic and copies ran while one was open for 2% of the time, Pallas kernels for 21%

profile of v3, /device:TPU:1, one launch (start us, length us, event | category | flops | bytes accessed | tf_op | source)
XLA Modules:
  0.0 183.3 jit_solution(17871428457405871919)
XLA Ops:
  0.0 0.8 slice_bitcast_fusion
  0.8 0.7 compare_bitcast_fusion
  1.7 1.9 %gather_fusion.1 = bf16[64,32,384]{2,1,0:T(8,128)(2,1)} fusion(bf16[64,32,384]{2,1,0:T(8,128)(2,1)S(1)} %copy-done, s32[1024]{0:T(1024)S(1)} %pad_clamp_fusion), kind=kCustom, calls=%fused_computation.1 | custom fusion | bytes 3145984 | tf_op jit(solution)/shard_map/gather | solution.py:186
  3.6 14.8 %all-to-all-start = ((bf16[64,32,384]{2,1,0:T(8,128)(2,1)}), bf16[64,32,384]{2,1,0:T(8,128)(2,1)S(1)}, u32[]{:S(2)}, u32[]{:S(2)}) async-start(bf16[64,32,384]{2,1,0:T(8,128)(2,1)} %gather_fusion.1), calls=%async_computation | async-start | bytes 3145728 | tf_op jit(solution)/shard_map/all_to_all | solution.py:185
  18.4 1.2 copy.9
  19.6 0.2 reshape.46
  19.8 4.2 %collective-permute-start.2 = (bf16[16,16,128]{2,1,0:T(8,128)(2,1)S(1)}, bf16[16,16,128]{2,1,0:T(8,128)(2,1)S(1)}, u32[]{:S(2)}, u32[]{:S(2)}) collective-permute-start(bf16[16,16,128]{2,1,0:T(8,128)(2,1)S(1)} %reshape.46), channel_id=1, source_target_pairs={{0,2},{1,3},{2,4},{3,5},{4,6},{5,7},{6,0},{7,1},{8,10},{9,11},{10,... | collective-permute-start | bytes 196616 | tf_op jit(solution)/shard_map/ppermute | solution.py:180
  24.0 3.6 %collective-permute-start.3 = (bf16[16,16,128]{2,1,0:T(8,128)(2,1)S(1)}, bf16[16,16,128]{2,1,0:T(8,128)(2,1)S(1)}, u32[]{:S(2)}, u32[]{:S(2)}) collective-permute-start(bf16[16,16,128]{2,1,0:T(8,128)(2,1)S(1)} %reshape.46), channel_id=1, source_target_pairs={{0,6},{1,7},{2,0},{3,1},{4,2},{5,3},{6,4},{7,5},{8,14},{9,15},{10,... | collective-permute-start | bytes 196616 | tf_op jit(solution)/shard_map/ppermute | solution.py:180
  27.6 3.5 %collective-permute-start.1 = (bf16[16,16,128]{2,1,0:T(8,128)(2,1)S(1)}, bf16[16,16,128]{2,1,0:T(8,128)(2,1)S(1)}, u32[]{:S(2)}, u32[]{:S(2)}) collective-permute-start(bf16[16,16,128]{2,1,0:T(8,128)(2,1)S(1)} %reshape.46), channel_id=1, source_target_pairs={{0,7},{1,0},{2,1},{3,2},{4,3},{5,4},{6,5},{7,6},{8,15},{9,8},{10,9... | collective-permute-start | bytes 196616 | tf_op jit(solution)/shard_map/ppermute | solution.py:180
  31.1 1.9 %collective-permute-start = (bf16[16,16,128]{2,1,0:T(8,128)(2,1)S(1)}, bf16[16,16,128]{2,1,0:T(8,128)(2,1)S(1)}, u32[]{:S(2)}, u32[]{:S(2)}) collective-permute-start(bf16[16,16,128]{2,1,0:T(8,128)(2,1)S(1)} %reshape.46), channel_id=1, source_target_pairs={{0,1},{1,2},{2,3},{3,4},{4,5},{5,6},{6,7},{7,0},{8,9},{9,10},{10,1... | collective-permute-start | bytes 196616 | tf_op jit(solution)/shard_map/ppermute | solution.py:180
  33.0 2.7 %collective-permute-start.4 = (bf16[2,2,384,384]{3,2,1,0:T(8,128)(2,1)}, bf16[2,2,384,384]{3,2,1,0:T(8,128)(2,1)}, u32[]{:S(2)}, u32[]{:S(2)}) collective-permute-start(bf16[2,2,384,384]{3,2,1,0:T(8,128)(2,1)} %rest_0_.1), channel_id=1, source_target_pairs={{0,1},{1,2},{2,3},{3,4},{4,5},{5,6},{6,7},{7,0},{8,9},{9,10},{10,1... | collective-permute-start | bytes 3538952 | tf_op jit(solution)/shard_map/ppermute | solution.py:180
  35.8 3.8 %collective-permute-start.5 = (bf16[2,2,384,384]{3,2,1,0:T(8,128)(2,1)}, bf16[2,2,384,384]{3,2,1,0:T(8,128)(2,1)}, u32[]{:S(2)}, u32[]{:S(2)}) collective-permute-start(bf16[2,2,384,384]{3,2,1,0:T(8,128)(2,1)} %rest_0_.1), channel_id=1, source_target_pairs={{0,7},{1,0},{2,1},{3,2},{4,3},{5,4},{6,5},{7,6},{8,15},{9,8},{10,9... | collective-permute-start | bytes 3538952 | tf_op jit(solution)/shard_map/ppermute | solution.py:180
  40.3 1.4 gather_fusion
  41.7 16.5 %all-to-all-done.psi_ref = bf16[64,32,384]{2,1,0:T(8,128)(2,1)S(1)} async-done(((bf16[64,32,384]{2,1,0:T(8,128)(2,1)}), bf16[64,32,384]{2,1,0:T(8,128)(2,1)S(1)}, u32[]{:S(2)}, u32[]{:S(2)}) %all-to-all-start) | async-done | bytes 1572896 | tf_op jit(solution)/shard_map/all_to_all | solution.py:185
  58.2 6.3 %all-to-all-start.1 = ((bf16[64,32,128]{2,1,0:T(8,128)(2,1)}), bf16[64,32,128]{2,1,0:T(8,128)(2,1)}, u32[]{:S(2)}, u32[]{:S(2)}) async-start(bf16[64,32,128]{2,1,0:T(8,128)(2,1)} %gather_fusion), calls=%async_computation.1 | async-start | bytes 1048576 | tf_op jit(solution)/shard_map/all_to_all | solution.py:203
  64.5 19.0 %pick.2 = bf16[2,384,384]{2,1,0:T(8,128)(2,1)} custom-call(bf16[2,2,384,384]{3,2,1,0:T(8,128)(2,1)} %collective-permute-done.4.right_ref.rest_1_), custom_call_target="tpu_custom_call" | custom-call | tf_op jit(solution)/shard_map/pick/pallas_call | solution.py:166
  83.5 3.2 %collective-permute-start.6 = (bf16[2,384,384]{2,1,0:T(8,128)(2,1)}, bf16[2,384,384]{2,1,0:T(8,128)(2,1)}, u32[]{:S(2)}, u32[]{:S(2)}) collective-permute-start(bf16[2,384,384]{2,1,0:T(8,128)(2,1)} %pick.2), channel_id=1, source_target_pairs={{0,1},{1,2},{2,3},{3,4},{4,5},{5,6},{6,7},{7,0},{8,9},{9,10},{10,1... | collective-permute-start | bytes 1769480 | tf_op jit(solution)/shard_map/ppermute | solution.py:180
  86.7 19.0 %pick.3 = bf16[2,384,384]{2,1,0:T(8,128)(2,1)} custom-call(bf16[2,2,384,384]{3,2,1,0:T(8,128)(2,1)} %collective-permute-done.5.right_ref.rest_2_), custom_call_target="tpu_custom_call" | custom-call | tf_op jit(solution)/shard_map/pick/pallas_call | solution.py:166
  105.8 3.8 %collective-permute-start.7 = (bf16[2,384,384]{2,1,0:T(8,128)(2,1)}, bf16[2,384,384]{2,1,0:T(8,128)(2,1)}, u32[]{:S(2)}, u32[]{:S(2)}) collective-permute-start(bf16[2,384,384]{2,1,0:T(8,128)(2,1)} %pick.3), channel_id=1, source_target_pairs={{0,7},{1,0},{2,1},{3,2},{4,3},{5,4},{6,5},{7,6},{8,15},{9,8},{10,9... | collective-permute-start | bytes 1769480 | tf_op jit(solution)/shard_map/ppermute | solution.py:180
  109.7 0.7 fusion.sector_ref
  110.4 11.6 %collective-permute-done.7.rest_4_ = bf16[2,384,384]{2,1,0:T(8,128)(2,1)} collective-permute-done((bf16[2,384,384]{2,1,0:T(8,128)(2,1)}, bf16[2,384,384]{2,1,0:T(8,128)(2,1)}, u32[]{:S(2)}, u32[]{:S(2)}) %collective-permute-start.7) | collective-permute-done | bytes 589856 | tf_op jit(solution)/shard_map/ppermute | solution.py:180
  122.0 13.9 %contract.1 = bf16[3072,128]{1,0:T(8,128)(2,1)} custom-call(s32[64]{0:T(128)} %fusion.sector_ref, bf16[64,32,384]{2,1,0:T(8,128)(2,1)} %copy-done.2, bf16[64,32,128]{2,1,0:T(8,128)(2,1)} %all-to-all-done.1.left_ref, bf16[2,2,384,384]{3,2,1,0:T(8,128)(2,1)} %rest_0_.1, bf16[2,2,384,384]{3,2,1,0:T(8,128)(2,1)} %collective-permute-done.4.right_ref.rest_1_, ...), custom_call_target="tpu_custom_call" | custom-call | flops 7000000000 | bytes 8000000 | tf_op jit(solution)/shard_map/contract/pallas_call | solution.py:107
  136.0 46.0 %all_to_all.15 = bf16[512,3,2,128]{3,2,1,0:T(2,128)(2,1)S(1)} all-to-all(bf16[512,3,2,128]{3,2,1,0:T(2,128)(2,1)} %bitcast.25), channel_id=1, replica_groups=mesh['sec'=64,'op'=8] {'sec','op'}, dimensions={0} | all-to-all | bytes 1572864 | tf_op jit(solution)/shard_map/all_to_all | solution.py:213
  182.0 1.2 collect.1
  (29 shorter events, 1.0 us)
Async XLA Ops:
  0.0 1.6 copy-start
  3.6 54.6 %all-to-all-start = ((bf16[64,32,384]{2,1,0:T(8,128)(2,1)}), bf16[64,32,384]{2,1,0:T(8,128)(2,1)S(1)}, u32[]{:S(2)}, u32[]{:S(2)}) async-start(bf16[64,32,384]{2,1,0:T(8,128)(2,1)} %gather_fusion.1), calls=%async_computation | async-start | bytes 3145728 | tf_op jit(solution)/shard_map/all_to_all | solution.py:185
  19.8 16.1 %collective-permute-start.2 = (bf16[16,16,128]{2,1,0:T(8,128)(2,1)S(1)}, bf16[16,16,128]{2,1,0:T(8,128)(2,1)S(1)}, u32[]{:S(2)}, u32[]{:S(2)}) collective-permute-start(bf16[16,16,128]{2,1,0:T(8,128)(2,1)S(1)} %reshape.46), channel_id=1, source_target_pairs={{0,2},{1,3},{2,4},{3,5},{4,6},{5,7},{6,0},{7,1},{8,10},{9,11},{10,... | collective-permute-start | bytes 196616 | tf_op jit(solution)/shard_map/ppermute | solution.py:180
  24.0 16.0 %collective-permute-start.3 = (bf16[16,16,128]{2,1,0:T(8,128)(2,1)S(1)}, bf16[16,16,128]{2,1,0:T(8,128)(2,1)S(1)}, u32[]{:S(2)}, u32[]{:S(2)}) collective-permute-start(bf16[16,16,128]{2,1,0:T(8,128)(2,1)S(1)} %reshape.46), channel_id=1, source_target_pairs={{0,6},{1,7},{2,0},{3,1},{4,2},{5,3},{6,4},{7,5},{8,14},{9,15},{10,... | collective-permute-start | bytes 196616 | tf_op jit(solution)/shard_map/ppermute | solution.py:180
  27.6 12.2 %collective-permute-start.1 = (bf16[16,16,128]{2,1,0:T(8,128)(2,1)S(1)}, bf16[16,16,128]{2,1,0:T(8,128)(2,1)S(1)}, u32[]{:S(2)}, u32[]{:S(2)}) collective-permute-start(bf16[16,16,128]{2,1,0:T(8,128)(2,1)S(1)} %reshape.46), channel_id=1, source_target_pairs={{0,7},{1,0},{2,1},{3,2},{4,3},{5,4},{6,5},{7,6},{8,15},{9,8},{10,9... | collective-permute-start | bytes 196616 | tf_op jit(solution)/shard_map/ppermute | solution.py:180
  31.1 8.8 %collective-permute-start = (bf16[16,16,128]{2,1,0:T(8,128)(2,1)S(1)}, bf16[16,16,128]{2,1,0:T(8,128)(2,1)S(1)}, u32[]{:S(2)}, u32[]{:S(2)}) collective-permute-start(bf16[16,16,128]{2,1,0:T(8,128)(2,1)S(1)} %reshape.46), channel_id=1, source_target_pairs={{0,1},{1,2},{2,3},{3,4},{4,5},{5,6},{6,7},{7,0},{8,9},{9,10},{10,1... | collective-permute-start | bytes 196616 | tf_op jit(solution)/shard_map/ppermute | solution.py:180
  33.0 31.5 %collective-permute-start.4 = (bf16[2,2,384,384]{3,2,1,0:T(8,128)(2,1)}, bf16[2,2,384,384]{3,2,1,0:T(8,128)(2,1)}, u32[]{:S(2)}, u32[]{:S(2)}) collective-permute-start(bf16[2,2,384,384]{3,2,1,0:T(8,128)(2,1)} %rest_0_.1), channel_id=1, source_target_pairs={{0,1},{1,2},{2,3},{3,4},{4,5},{5,6},{6,7},{7,0},{8,9},{9,10},{10,1... | collective-permute-start | bytes 3538952 | tf_op jit(solution)/shard_map/ppermute | solution.py:180
  35.8 50.9 %collective-permute-start.5 = (bf16[2,2,384,384]{3,2,1,0:T(8,128)(2,1)}, bf16[2,2,384,384]{3,2,1,0:T(8,128)(2,1)}, u32[]{:S(2)}, u32[]{:S(2)}) collective-permute-start(bf16[2,2,384,384]{3,2,1,0:T(8,128)(2,1)} %rest_0_.1), channel_id=1, source_target_pairs={{0,7},{1,0},{2,1},{3,2},{4,3},{5,4},{6,5},{7,6},{8,15},{9,8},{10,9... | collective-permute-start | bytes 3538952 | tf_op jit(solution)/shard_map/ppermute | solution.py:180
  58.2 47.6 %copy-start.2 = (bf16[64,32,384]{2,1,0:T(8,128)(2,1)}, bf16[64,32,384]{2,1,0:T(8,128)(2,1)S(1)}, u32[]{:S(2)}) copy-start(bf16[64,32,384]{2,1,0:T(8,128)(2,1)S(1)} %all-to-all-done.psi_ref) | copy-start | bytes 4718596
  58.2 63.8 %all-to-all-start.1 = ((bf16[64,32,128]{2,1,0:T(8,128)(2,1)}), bf16[64,32,128]{2,1,0:T(8,128)(2,1)}, u32[]{:S(2)}, u32[]{:S(2)}) async-start(bf16[64,32,128]{2,1,0:T(8,128)(2,1)} %gather_fusion), calls=%async_computation.1 | async-start | bytes 1048576 | tf_op jit(solution)/shard_map/all_to_all | solution.py:203
  64.5 45.1 %copy-start.3 = (s32[128]{0:T(128)S(1)}, s32[128]{0:T(128)}, u32[]{:S(2)}) copy-start(s32[128]{0:T(128)} %param.9) | copy-start | bytes 1540
  83.5 26.9 %collective-permute-start.6 = (bf16[2,384,384]{2,1,0:T(8,128)(2,1)}, bf16[2,384,384]{2,1,0:T(8,128)(2,1)}, u32[]{:S(2)}, u32[]{:S(2)}) collective-permute-start(bf16[2,384,384]{2,1,0:T(8,128)(2,1)} %pick.2), channel_id=1, source_target_pairs={{0,1},{1,2},{2,3},{3,4},{4,5},{5,6},{6,7},{7,0},{8,9},{9,10},{10,1... | collective-permute-start | bytes 1769480 | tf_op jit(solution)/shard_map/ppermute | solution.py:180
  105.8 16.3 %collective-permute-start.7 = (bf16[2,384,384]{2,1,0:T(8,128)(2,1)}, bf16[2,384,384]{2,1,0:T(8,128)(2,1)}, u32[]{:S(2)}, u32[]{:S(2)}) collective-permute-start(bf16[2,384,384]{2,1,0:T(8,128)(2,1)} %pick.3), channel_id=1, source_target_pairs={{0,7},{1,0},{2,1},{3,2},{4,3},{5,4},{6,5},{7,6},{8,15},{9,8},{10,9... | collective-permute-start | bytes 1769480 | tf_op jit(solution)/shard_map/ppermute | solution.py:180
  136.0 46.1 %copy-start.1 = (s32[64,3]{0,1:T(4,128)S(1)}, s32[64,3]{0,1:T(4,128)}, u32[]{:S(2)}) copy-start(s32[64,3]{0,1:T(4,128)} %param.8) | copy-start | bytes 2308

commit v4 on v3

--- a/solution.py
+++ b/solution.py
@@ -1,5 +1,3 @@
-import functools
-
 import jax
 import jax.numpy as jnp
 from jax import lax
@@ -152,23 +150,17 @@
     )(left_table, pieces)
 
 
-def pick_kernel(term, right_ref, out_ref, sem):
-    copies = [
-        pltpu.make_async_copy(right_ref.at[sector, term], out_ref.at[sector], sem.at[sector]) for sector in range(2)
-    ]
-    for copy in copies:
-        copy.start()
-    for copy in copies:
-        copy.wait()
+def pick_kernel(right_ref, out_ref):
+    out_ref[...] = right_ref[:, 0]
 
 
 def pick(right, term):
     return pl.pallas_call(
-        functools.partial(pick_kernel, term),
+        pick_kernel,
+        grid=(2,),
         out_shape=jax.ShapeDtypeStruct((2, 384, 384), BF16),
-        in_specs=[pl.BlockSpec(memory_space=pltpu.HBM)],
-        out_specs=pl.BlockSpec(memory_space=pltpu.HBM),
-        scratch_shapes=[pltpu.SemaphoreType.DMA((2,))],
+        in_specs=[pl.BlockSpec((1, 1, 384, 384), lambda sector: (sector, term, 0, 0))],
+        out_specs=pl.BlockSpec((1, 384, 384), lambda sector: (sector, 0, 0)),
         compiler_params=pltpu.CompilerParams(vmem_limit_bytes=60 << 20),
         name="pick",
     )(right)

time: 184 us -> 150 us (0.82)
  Pallas kernels: 53.1 us -> 18.8 us
    pallas_call x2, Pallas kernels: 38 us -> 3.64 us  [pick(): pl.pallas_call(pick_kernel, grid=(2,), out_shape=jax.ShapeDtypeStruct((2,...]
  transfers between devices with their start and end apart: 10 -> 10, of which waited for: 2 -> 3; matrix products, arithmetic and copies ran while one was open for 2% -> 3% of each run, Pallas kernels for 21% -> 2%
where the time goes in v4:
time: 150 us; the launch traced here: 149 us
  starting transfers between devices  47.8 us (32%)
  blocking collectives  46 us (31%)
  waiting for transfers between devices  28.1 us (19%)
  Pallas kernels  18.8 us (13%)
  local copies, waits for them, and re-layouts  5.83 us (4%)
  other arithmetic  2.02 us (1%)
    all_to_all x1, blocking collectives, per_device(): lax.all_to_all(pieces.reshape(512, 3, 2, 128), ('sec', 'op'), split_axis=...  46 us
    ppermute x8, starting transfers between devices, per_device(): lax.ppermute(value, 'op', [(i, (i + step) % 8) for i in range(8)])  26.7 us
    all_to_all x1, waiting for transfers between devices, per_device(): lax.all_to_all(psi.at[source].get(mode='promise_in_bounds'), 'sec', split...  16.5 us
    all_to_all x1, starting transfers between devices, per_device(): lax.all_to_all(psi.at[source].get(mode='promise_in_bounds'), 'sec', split...  14.8 us
    pallas_call x1, Pallas kernels, contract(): pl.pallas_call(contract_kernel, out_shape=jax.ShapeDtypeStruct((3072, 128...  13.9 us
    ppermute x8, waiting for transfers between devices, per_device(): lax.ppermute(value, 'op', [(i, (i + step) % 8) for i in range(8)])  11.6 us
    all_to_all x1, starting transfers between devices, per_device(): lax.all_to_all(left_here, 'sec', split_axis=0, concat_axis=0, tiled=True)  6.31 us
    pallas_call x2, Pallas kernels, pick(): pl.pallas_call(pick_kernel, grid=(2,), out_shape=jax.ShapeDtypeStruct((2,...  3.64 us
  transfers between devices with their start and end apart: 10, of which 3 were waited for; matrix products, arithmetic and copies ran while one was open for 3% of the time, Pallas kernels for 2%

profile of v4, /device:TPU:1, one launch (start us, length us, event | category | flops | bytes accessed | tf_op | source)
XLA Modules:
  0.0 148.9 jit_solution(4015558055886599418)
XLA Ops:
  0.0 0.8 slice_bitcast_fusion
  0.8 0.7 compare_bitcast_fusion
  1.7 1.9 %gather_fusion.1 = bf16[64,32,384]{2,1,0:T(8,128)(2,1)} fusion(bf16[64,32,384]{2,1,0:T(8,128)(2,1)S(1)} %copy-done, s32[1024]{0:T(1024)S(1)} %pad_clamp_fusion), kind=kCustom, calls=%fused_computation.1 | custom fusion | bytes 3145984 | tf_op jit(solution)/shard_map/gather | solution.py:178
  3.6 14.8 %all-to-all-start = ((bf16[64,32,384]{2,1,0:T(8,128)(2,1)}), bf16[64,32,384]{2,1,0:T(8,128)(2,1)S(1)}, u32[]{:S(2)}, u32[]{:S(2)}) async-start(bf16[64,32,384]{2,1,0:T(8,128)(2,1)} %gather_fusion.1), calls=%async_computation | async-start | bytes 3145728 | tf_op jit(solution)/shard_map/all_to_all | solution.py:177
  18.4 1.2 copy.9
  19.8 4.2 %collective-permute-start.2 = (bf16[16,16,128]{2,1,0:T(8,128)(2,1)S(1)}, bf16[16,16,128]{2,1,0:T(8,128)(2,1)S(1)}, u32[]{:S(2)}, u32[]{:S(2)}) collective-permute-start(bf16[16,16,128]{2,1,0:T(8,128)(2,1)S(1)} %reshape.46), channel_id=1, source_target_pairs={{0,2},{1,3},{2,4},{3,5},{4,6},{5,7},{6,0},{7,1},{8,10},{9,11},{10,... | collective-permute-start | bytes 196616 | tf_op jit(solution)/shard_map/ppermute | solution.py:172
  24.0 3.6 %collective-permute-start.3 = (bf16[16,16,128]{2,1,0:T(8,128)(2,1)S(1)}, bf16[16,16,128]{2,1,0:T(8,128)(2,1)S(1)}, u32[]{:S(2)}, u32[]{:S(2)}) collective-permute-start(bf16[16,16,128]{2,1,0:T(8,128)(2,1)S(1)} %reshape.46), channel_id=1, source_target_pairs={{0,6},{1,7},{2,0},{3,1},{4,2},{5,3},{6,4},{7,5},{8,14},{9,15},{10,... | collective-permute-start | bytes 196616 | tf_op jit(solution)/shard_map/ppermute | solution.py:172
  27.6 3.5 %collective-permute-start.1 = (bf16[16,16,128]{2,1,0:T(8,128)(2,1)S(1)}, bf16[16,16,128]{2,1,0:T(8,128)(2,1)S(1)}, u32[]{:S(2)}, u32[]{:S(2)}) collective-permute-start(bf16[16,16,128]{2,1,0:T(8,128)(2,1)S(1)} %reshape.46), channel_id=1, source_target_pairs={{0,7},{1,0},{2,1},{3,2},{4,3},{5,4},{6,5},{7,6},{8,15},{9,8},{10,9... | collective-permute-start | bytes 196616 | tf_op jit(solution)/shard_map/ppermute | solution.py:172
  31.1 1.9 %collective-permute-start = (bf16[16,16,128]{2,1,0:T(8,128)(2,1)S(1)}, bf16[16,16,128]{2,1,0:T(8,128)(2,1)S(1)}, u32[]{:S(2)}, u32[]{:S(2)}) collective-permute-start(bf16[16,16,128]{2,1,0:T(8,128)(2,1)S(1)} %reshape.46), channel_id=1, source_target_pairs={{0,1},{1,2},{2,3},{3,4},{4,5},{5,6},{6,7},{7,0},{8,9},{9,10},{10,1... | collective-permute-start | bytes 196616 | tf_op jit(solution)/shard_map/ppermute | solution.py:172
  33.0 2.7 %collective-permute-start.4 = (bf16[2,2,384,384]{3,2,1,0:T(8,128)(2,1)}, bf16[2,2,384,384]{3,2,1,0:T(8,128)(2,1)}, u32[]{:S(2)}, u32[]{:S(2)}) collective-permute-start(bf16[2,2,384,384]{3,2,1,0:T(8,128)(2,1)} %rest_0_.1), channel_id=1, source_target_pairs={{0,1},{1,2},{2,3},{3,4},{4,5},{5,6},{6,7},{7,0},{8,9},{9,10},{10,1... | collective-permute-start | bytes 3538952 | tf_op jit(solution)/shard_map/ppermute | solution.py:172
  35.8 3.8 %collective-permute-start.5 = (bf16[2,2,384,384]{3,2,1,0:T(8,128)(2,1)}, bf16[2,2,384,384]{3,2,1,0:T(8,128)(2,1)}, u32[]{:S(2)}, u32[]{:S(2)}) collective-permute-start(bf16[2,2,384,384]{3,2,1,0:T(8,128)(2,1)} %rest_0_.1), channel_id=1, source_target_pairs={{0,7},{1,0},{2,1},{3,2},{4,3},{5,4},{6,5},{7,6},{8,15},{9,8},{10,9... | collective-permute-start | bytes 3538952 | tf_op jit(solution)/shard_map/ppermute | solution.py:172
  40.3 1.4 gather_fusion
  41.7 16.5 %all-to-all-done.psi_ref = bf16[64,32,384]{2,1,0:T(8,128)(2,1)S(1)} async-done(((bf16[64,32,384]{2,1,0:T(8,128)(2,1)}), bf16[64,32,384]{2,1,0:T(8,128)(2,1)S(1)}, u32[]{:S(2)}, u32[]{:S(2)}) %all-to-all-start) | async-done | bytes 1572896 | tf_op jit(solution)/shard_map/all_to_all | solution.py:177
  58.2 6.3 %all-to-all-start.1 = ((bf16[64,32,128]{2,1,0:T(8,128)(2,1)}), bf16[64,32,128]{2,1,0:T(8,128)(2,1)}, u32[]{:S(2)}, u32[]{:S(2)}) async-start(bf16[64,32,128]{2,1,0:T(8,128)(2,1)} %gather_fusion), calls=%async_computation.1 | async-start | bytes 1048576 | tf_op jit(solution)/shard_map/all_to_all | solution.py:195
  64.5 1.8 %pick.2 = bf16[2,384,384]{2,1,0:T(8,128)(2,1)} custom-call(bf16[2,2,384,384]{3,2,1,0:T(8,128)(2,1)} %collective-permute-done.4.right_ref.rest_1_), custom_call_target="tpu_custom_call" | custom-call | tf_op jit(solution)/shard_map/pick/pallas_call | solution.py:158
  66.4 3.2 %collective-permute-start.6 = (bf16[2,384,384]{2,1,0:T(8,128)(2,1)}, bf16[2,384,384]{2,1,0:T(8,128)(2,1)}, u32[]{:S(2)}, u32[]{:S(2)}) collective-permute-start(bf16[2,384,384]{2,1,0:T(8,128)(2,1)} %pick.2), channel_id=1, source_target_pairs={{0,1},{1,2},{2,3},{3,4},{4,5},{5,6},{6,7},{7,0},{8,9},{9,10},{10,1... | collective-permute-start | bytes 1769480 | tf_op jit(solution)/shard_map/ppermute | solution.py:172
  69.6 1.8 %pick.3 = bf16[2,384,384]{2,1,0:T(8,128)(2,1)} custom-call(bf16[2,2,384,384]{3,2,1,0:T(8,128)(2,1)} %collective-permute-done.5.right_ref.rest_2_), custom_call_target="tpu_custom_call" | custom-call | tf_op jit(solution)/shard_map/pick/pallas_call | solution.py:158
  71.4 3.8 %collective-permute-start.7 = (bf16[2,384,384]{2,1,0:T(8,128)(2,1)}, bf16[2,384,384]{2,1,0:T(8,128)(2,1)}, u32[]{:S(2)}, u32[]{:S(2)}) collective-permute-start(bf16[2,384,384]{2,1,0:T(8,128)(2,1)} %pick.3), channel_id=1, source_target_pairs={{0,7},{1,0},{2,1},{3,2},{4,3},{5,4},{6,5},{7,6},{8,15},{9,8},{10,9... | collective-permute-start | bytes 1769480 | tf_op jit(solution)/shard_map/ppermute | solution.py:172
  75.4 0.7 fusion.sector_ref
  76.1 8.9 %collective-permute-done.6.rest_3_ = bf16[2,384,384]{2,1,0:T(8,128)(2,1)} collective-permute-done((bf16[2,384,384]{2,1,0:T(8,128)(2,1)}, bf16[2,384,384]{2,1,0:T(8,128)(2,1)}, u32[]{:S(2)}, u32[]{:S(2)}) %collective-permute-start.6) | collective-permute-done | bytes 589856 | tf_op jit(solution)/shard_map/ppermute | solution.py:172
  85.0 2.7 %collective-permute-done.7.rest_4_ = bf16[2,384,384]{2,1,0:T(8,128)(2,1)} collective-permute-done((bf16[2,384,384]{2,1,0:T(8,128)(2,1)}, bf16[2,384,384]{2,1,0:T(8,128)(2,1)}, u32[]{:S(2)}, u32[]{:S(2)}) %collective-permute-start.7) | collective-permute-done | bytes 589856 | tf_op jit(solution)/shard_map/ppermute | solution.py:172
  87.7 13.9 %contract.1 = bf16[3072,128]{1,0:T(8,128)(2,1)} custom-call(s32[64]{0:T(128)} %fusion.sector_ref, bf16[64,32,384]{2,1,0:T(8,128)(2,1)} %copy-done.2, bf16[64,32,128]{2,1,0:T(8,128)(2,1)} %all-to-all-done.1.left_ref, bf16[2,2,384,384]{3,2,1,0:T(8,128)(2,1)} %rest_0_.1, bf16[2,2,384,384]{3,2,1,0:T(8,128)(2,1)} %collective-permute-done.4.right_ref.rest_1_, ...), custom_call_target="tpu_custom_call" | custom-call | flops 7000000000 | bytes 8000000 | tf_op jit(solution)/shard_map/contract/pallas_call | solution.py:105
  101.6 46.0 %all_to_all.15 = bf16[512,3,2,128]{3,2,1,0:T(2,128)(2,1)S(1)} all-to-all(bf16[512,3,2,128]{3,2,1,0:T(2,128)(2,1)} %bitcast.25), channel_id=1, replica_groups=mesh['sec'=64,'op'=8] {'sec','op'}, dimensions={0} | all-to-all | bytes 1572864 | tf_op jit(solution)/shard_map/all_to_all | solution.py:205
  147.6 1.2 collect.1
  (29 shorter events, 1.1 us)
Async XLA Ops:
  0.0 1.6 %copy-start = (bf16[64,32,384]{2,1,0:T(8,128)(2,1)S(1)}, bf16[64,32,384]{2,1,0:T(8,128)(2,1)}, u32[]{:S(2)}) copy-start(bf16[64,32,384]{2,1,0:T(8,128)(2,1)} %param.5) | copy-start | bytes 4718596
  3.6 54.6 %all-to-all-start = ((bf16[64,32,384]{2,1,0:T(8,128)(2,1)}), bf16[64,32,384]{2,1,0:T(8,128)(2,1)S(1)}, u32[]{:S(2)}, u32[]{:S(2)}) async-start(bf16[64,32,384]{2,1,0:T(8,128)(2,1)} %gather_fusion.1), calls=%async_computation | async-start | bytes 3145728 | tf_op jit(solution)/shard_map/all_to_all | solution.py:177
  19.8 16.1 %collective-permute-start.2 = (bf16[16,16,128]{2,1,0:T(8,128)(2,1)S(1)}, bf16[16,16,128]{2,1,0:T(8,128)(2,1)S(1)}, u32[]{:S(2)}, u32[]{:S(2)}) collective-permute-start(bf16[16,16,128]{2,1,0:T(8,128)(2,1)S(1)} %reshape.46), channel_id=1, source_target_pairs={{0,2},{1,3},{2,4},{3,5},{4,6},{5,7},{6,0},{7,1},{8,10},{9,11},{10,... | collective-permute-start | bytes 196616 | tf_op jit(solution)/shard_map/ppermute | solution.py:172
  24.0 16.0 %collective-permute-start.3 = (bf16[16,16,128]{2,1,0:T(8,128)(2,1)S(1)}, bf16[16,16,128]{2,1,0:T(8,128)(2,1)S(1)}, u32[]{:S(2)}, u32[]{:S(2)}) collective-permute-start(bf16[16,16,128]{2,1,0:T(8,128)(2,1)S(1)} %reshape.46), channel_id=1, source_target_pairs={{0,6},{1,7},{2,0},{3,1},{4,2},{5,3},{6,4},{7,5},{8,14},{9,15},{10,... | collective-permute-start | bytes 196616 | tf_op jit(solution)/shard_map/ppermute | solution.py:172
  27.6 12.2 %collective-permute-start.1 = (bf16[16,16,128]{2,1,0:T(8,128)(2,1)S(1)}, bf16[16,16,128]{2,1,0:T(8,128)(2,1)S(1)}, u32[]{:S(2)}, u32[]{:S(2)}) collective-permute-start(bf16[16,16,128]{2,1,0:T(8,128)(2,1)S(1)} %reshape.46), channel_id=1, source_target_pairs={{0,7},{1,0},{2,1},{3,2},{4,3},{5,4},{6,5},{7,6},{8,15},{9,8},{10,9... | collective-permute-start | bytes 196616 | tf_op jit(solution)/shard_map/ppermute | solution.py:172
  31.1 8.8 %collective-permute-start = (bf16[16,16,128]{2,1,0:T(8,128)(2,1)S(1)}, bf16[16,16,128]{2,1,0:T(8,128)(2,1)S(1)}, u32[]{:S(2)}, u32[]{:S(2)}) collective-permute-start(bf16[16,16,128]{2,1,0:T(8,128)(2,1)S(1)} %reshape.46), channel_id=1, source_target_pairs={{0,1},{1,2},{2,3},{3,4},{4,5},{5,6},{6,7},{7,0},{8,9},{9,10},{10,1... | collective-permute-start | bytes 196616 | tf_op jit(solution)/shard_map/ppermute | solution.py:172
  33.0 31.5 %collective-permute-start.4 = (bf16[2,2,384,384]{3,2,1,0:T(8,128)(2,1)}, bf16[2,2,384,384]{3,2,1,0:T(8,128)(2,1)}, u32[]{:S(2)}, u32[]{:S(2)}) collective-permute-start(bf16[2,2,384,384]{3,2,1,0:T(8,128)(2,1)} %rest_0_.1), channel_id=1, source_target_pairs={{0,1},{1,2},{2,3},{3,4},{4,5},{5,6},{6,7},{7,0},{8,9},{9,10},{10,1... | collective-permute-start | bytes 3538952 | tf_op jit(solution)/shard_map/ppermute | solution.py:172
  35.8 33.7 %collective-permute-start.5 = (bf16[2,2,384,384]{3,2,1,0:T(8,128)(2,1)}, bf16[2,2,384,384]{3,2,1,0:T(8,128)(2,1)}, u32[]{:S(2)}, u32[]{:S(2)}) collective-permute-start(bf16[2,2,384,384]{3,2,1,0:T(8,128)(2,1)} %rest_0_.1), channel_id=1, source_target_pairs={{0,7},{1,0},{2,1},{3,2},{4,3},{5,4},{6,5},{7,6},{8,15},{9,8},{10,9... | collective-permute-start | bytes 3538952 | tf_op jit(solution)/shard_map/ppermute | solution.py:172
  58.2 13.2 %copy-start.2 = (bf16[64,32,384]{2,1,0:T(8,128)(2,1)}, bf16[64,32,384]{2,1,0:T(8,128)(2,1)S(1)}, u32[]{:S(2)}) copy-start(bf16[64,32,384]{2,1,0:T(8,128)(2,1)S(1)} %all-to-all-done.psi_ref) | copy-start | bytes 4718596
  58.2 29.5 %all-to-all-start.1 = ((bf16[64,32,128]{2,1,0:T(8,128)(2,1)}), bf16[64,32,128]{2,1,0:T(8,128)(2,1)}, u32[]{:S(2)}, u32[]{:S(2)}) async-start(bf16[64,32,128]{2,1,0:T(8,128)(2,1)} %gather_fusion), calls=%async_computation.1 | async-start | bytes 1048576 | tf_op jit(solution)/shard_map/all_to_all | solution.py:195
  64.5 10.7 %copy-start.3 = (s32[128]{0:T(128)S(1)}, s32[128]{0:T(128)}, u32[]{:S(2)}) copy-start(s32[128]{0:T(128)} %param.9) | copy-start | bytes 1540
  66.4 18.6 %collective-permute-start.6 = (bf16[2,384,384]{2,1,0:T(8,128)(2,1)}, bf16[2,384,384]{2,1,0:T(8,128)(2,1)}, u32[]{:S(2)}, u32[]{:S(2)}) collective-permute-start(bf16[2,384,384]{2,1,0:T(8,128)(2,1)} %pick.2), channel_id=1, source_target_pairs={{0,1},{1,2},{2,3},{3,4},{4,5},{5,6},{6,7},{7,0},{8,9},{9,10},{10,1... | collective-permute-start | bytes 1769480 | tf_op jit(solution)/shard_map/ppermute | solution.py:172
  71.4 16.3 %collective-permute-start.7 = (bf16[2,384,384]{2,1,0:T(8,128)(2,1)}, bf16[2,384,384]{2,1,0:T(8,128)(2,1)}, u32[]{:S(2)}, u32[]{:S(2)}) collective-permute-start(bf16[2,384,384]{2,1,0:T(8,128)(2,1)} %pick.3), channel_id=1, source_target_pairs={{0,7},{1,0},{2,1},{3,2},{4,3},{5,4},{6,5},{7,6},{8,15},{9,8},{10,9... | collective-permute-start | bytes 1769480 | tf_op jit(solution)/shard_map/ppermute | solution.py:172
  101.6 46.1 %copy-start.1 = (s32[64,3]{0,1:T(4,128)S(1)}, s32[64,3]{0,1:T(4,128)}, u32[]{:S(2)}) copy-start(s32[64,3]{0,1:T(4,128)} %param.8) | copy-start | bytes 2308

commit v5 on v4

--- a/solution.py
+++ b/solution.py
@@ -179,7 +179,8 @@
     )
 
     dense = left.reshape(16, 2, 2, 16, 32).transpose(0, 3, 2, 1, 4).reshape(16, 16, 128)
-    before, after, two_before, two_after = hop(dense, 1), hop(dense, -1), hop(dense, 2), hop(dense, -2)
+    two_before, two_after, again = lax.optimization_barrier((hop(dense, 2), hop(dense, -2), dense))
+    before, after = hop(again, 1), hop(again, -1)
     right_before, right_after = hop(right, 1), hop(right, -1)
     part = lambda value: jnp.where(half == 0, value[:, :, :64], value[:, :, 64:])
     table = jnp.concatenate(

time: 150 us -> 159 us (1.060)
  starting transfers between devices: 47.8 us -> 53.5 us
  waiting for transfers between devices: 28.1 us -> 33.4 us
    ppermute x8, waiting for transfers between devices: 11.6 us -> 33.4 us  [per_device(): lax.ppermute(value, 'op', [(i, (i + step) % 8) for i in range(8)])]
    all_to_all x1, waiting for transfers between devices: 16.5 us -> 0.01 us  [per_device(): lax.all_to_all(psi.at[source].get(mode='promise_in_bounds'), 'sec', split...]
    all_to_all x1, starting transfers between devices: 6.31 us -> 12.3 us  [per_device(): lax.all_to_all(left_here, 'sec', split_axis=0, concat_axis=0, tiled=True)]
where the time goes in v5:
time: 159 us
  starting transfers between devices  53.5 us (34%)
  blocking collectives  44.8 us (28%)
  waiting for transfers between devices  33.4 us (21%)
  Pallas kernels  18.8 us (12%)
  local copies, waits for them, and re-layouts  5.76 us (4%)
  other arithmetic  2.02 us (1%)
    all_to_all x1, blocking collectives, per_device(): lax.all_to_all(pieces.reshape(512, 3, 2, 128), ('sec', 'op'), split_axis=...  44.8 us
    ppermute x8, waiting for transfers between devices, per_device(): lax.ppermute(value, 'op', [(i, (i + step) % 8) for i in range(8)])  33.4 us
    ppermute x8, starting transfers between devices, per_device(): lax.ppermute(value, 'op', [(i, (i + step) % 8) for i in range(8)])  26.4 us
    all_to_all x1, starting transfers between devices, per_device(): lax.all_to_all(psi.at[source].get(mode='promise_in_bounds'), 'sec', split...  14.8 us
    pallas_call x1, Pallas kernels, contract(): pl.pallas_call(contract_kernel, out_shape=jax.ShapeDtypeStruct((3072, 128...  13.9 us
    all_to_all x1, starting transfers between devices, per_device(): lax.all_to_all(left_here, 'sec', split_axis=0, concat_axis=0, tiled=True)  12.3 us
    pallas_call x2, Pallas kernels, pick(): pl.pallas_call(pick_kernel, grid=(2,), out_shape=jax.ShapeDtypeStruct((2,...  3.66 us
  transfers between devices with their start and end apart: 10, of which 3 were waited for; matrix products, arithmetic and copies ran while one was open for 3% of the time, Pallas kernels for 2%

profile of v5, /device:TPU:1, one launch (start us, length us, event | category | flops | bytes accessed | tf_op | source)
XLA Modules:
  0.0 158.6 jit_solution(4052836133292418601)
XLA Ops:
  0.0 0.8 slice_bitcast_fusion
  0.8 0.7 compare_bitcast_fusion
  1.7 1.9 %gather_fusion.1 = bf16[64,32,384]{2,1,0:T(8,128)(2,1)} fusion(bf16[64,32,384]{2,1,0:T(8,128)(2,1)S(1)} %copy-done, s32[1024]{0:T(1024)S(1)} %pad_clamp_fusion), kind=kCustom, calls=%fused_computation.1 | custom fusion | bytes 3145984 | tf_op jit(solution)/shard_map/gather | solution.py:178
  3.6 14.8 %all-to-all-start = ((bf16[64,32,384]{2,1,0:T(8,128)(2,1)}), bf16[64,32,384]{2,1,0:T(8,128)(2,1)S(1)}, u32[]{:S(2)}, u32[]{:S(2)}) async-start(bf16[64,32,384]{2,1,0:T(8,128)(2,1)} %gather_fusion.1), calls=%async_computation | async-start | bytes 3145728 | tf_op jit(solution)/shard_map/all_to_all | solution.py:177
  18.4 1.2 copy.9
  19.8 4.2 %collective-permute-start = (bf16[16,16,128]{2,1,0:T(8,128)(2,1)S(1)}, bf16[16,16,128]{2,1,0:T(8,128)(2,1)S(1)}, u32[]{:S(2)}, u32[]{:S(2)}) collective-permute-start(bf16[16,16,128]{2,1,0:T(8,128)(2,1)S(1)} %reshape.46), channel_id=1, source_target_pairs={{0,2},{1,3},{2,4},{3,5},{4,6},{5,7},{6,0},{7,1},{8,10},{9,11},{10,... | collective-permute-start | bytes 196616 | tf_op jit(solution)/shard_map/ppermute | solution.py:172
  24.0 3.6 %collective-permute-start.1 = (bf16[16,16,128]{2,1,0:T(8,128)(2,1)S(1)}, bf16[16,16,128]{2,1,0:T(8,128)(2,1)S(1)}, u32[]{:S(2)}, u32[]{:S(2)}) collective-permute-start(bf16[16,16,128]{2,1,0:T(8,128)(2,1)S(1)} %reshape.46), channel_id=1, source_target_pairs={{0,6},{1,7},{2,0},{3,1},{4,2},{5,3},{6,4},{7,5},{8,14},{9,15},{10,... | collective-permute-start | bytes 196616 | tf_op jit(solution)/shard_map/ppermute | solution.py:172
  27.6 2.8 %collective-permute-start.4 = (bf16[2,2,384,384]{3,2,1,0:T(8,128)(2,1)}, bf16[2,2,384,384]{3,2,1,0:T(8,128)(2,1)}, u32[]{:S(2)}, u32[]{:S(2)}) collective-permute-start(bf16[2,2,384,384]{3,2,1,0:T(8,128)(2,1)} %rest_0_.1), channel_id=1, source_target_pairs={{0,1},{1,2},{2,3},{3,4},{4,5},{5,6},{6,7},{7,0},{8,9},{9,10},{10,1... | collective-permute-start | bytes 3538952 | tf_op jit(solution)/shard_map/ppermute | solution.py:172
  30.4 3.7 %collective-permute-start.5 = (bf16[2,2,384,384]{3,2,1,0:T(8,128)(2,1)}, bf16[2,2,384,384]{3,2,1,0:T(8,128)(2,1)}, u32[]{:S(2)}, u32[]{:S(2)}) collective-permute-start(bf16[2,2,384,384]{3,2,1,0:T(8,128)(2,1)} %rest_0_.1), channel_id=1, source_target_pairs={{0,7},{1,0},{2,1},{3,2},{4,3},{5,4},{6,5},{7,6},{8,15},{9,8},{10,9... | collective-permute-start | bytes 3538952 | tf_op jit(solution)/shard_map/ppermute | solution.py:172
  34.3 2.3 %collective-permute-start.3 = (bf16[16,16,128]{2,1,0:T(8,128)(2,1)S(1)}, bf16[16,16,128]{2,1,0:T(8,128)(2,1)S(1)}, u32[]{:S(2)}, u32[]{:S(2)}) collective-permute-start(bf16[16,16,128]{2,1,0:T(8,128)(2,1)S(1)} %reshape.46), channel_id=1, source_target_pairs={{0,7},{1,0},{2,1},{3,2},{4,3},{5,4},{6,5},{7,6},{8,15},{9,8},{10,9... | collective-permute-start | bytes 196616 | tf_op jit(solution)/shard_map/ppermute | solution.py:172
  36.5 3.0 %collective-permute-start.2 = (bf16[16,16,128]{2,1,0:T(8,128)(2,1)S(1)}, bf16[16,16,128]{2,1,0:T(8,128)(2,1)S(1)}, u32[]{:S(2)}, u32[]{:S(2)}) collective-permute-start(bf16[16,16,128]{2,1,0:T(8,128)(2,1)S(1)} %reshape.46), channel_id=1, source_target_pairs={{0,1},{1,2},{2,3},{3,4},{4,5},{5,6},{6,7},{7,0},{8,9},{9,10},{10,1... | collective-permute-start | bytes 196616 | tf_op jit(solution)/shard_map/ppermute | solution.py:172
  39.8 20.4 %collective-permute-done.3 = bf16[16,16,128]{2,1,0:T(8,128)(2,1)S(1)} collective-permute-done((bf16[16,16,128]{2,1,0:T(8,128)(2,1)S(1)}, bf16[16,16,128]{2,1,0:T(8,128)(2,1)S(1)}, u32[]{:S(2)}, u32[]{:S(2)}) %collective-permute-start.3) | collective-permute-done | bytes 65568 | tf_op jit(solution)/shard_map/ppermute | solution.py:172
  60.5 1.4 gather_fusion
  61.9 12.3 %all-to-all-start.1 = ((bf16[64,32,128]{2,1,0:T(8,128)(2,1)}), bf16[64,32,128]{2,1,0:T(8,128)(2,1)}, u32[]{:S(2)}, u32[]{:S(2)}) async-start(bf16[64,32,128]{2,1,0:T(8,128)(2,1)} %gather_fusion), calls=%async_computation.1 | async-start | bytes 1048576 | tf_op jit(solution)/shard_map/all_to_all | solution.py:196
  74.2 1.8 %pick.2 = bf16[2,384,384]{2,1,0:T(8,128)(2,1)} custom-call(bf16[2,2,384,384]{3,2,1,0:T(8,128)(2,1)} %collective-permute-done.4.right_ref.rest_1_), custom_call_target="tpu_custom_call" | custom-call | tf_op jit(solution)/shard_map/pick/pallas_call | solution.py:158
  76.1 3.1 %collective-permute-start.6 = (bf16[2,384,384]{2,1,0:T(8,128)(2,1)}, bf16[2,384,384]{2,1,0:T(8,128)(2,1)}, u32[]{:S(2)}, u32[]{:S(2)}) collective-permute-start(bf16[2,384,384]{2,1,0:T(8,128)(2,1)} %pick.2), channel_id=1, source_target_pairs={{0,1},{1,2},{2,3},{3,4},{4,5},{5,6},{6,7},{7,0},{8,9},{9,10},{10,1... | collective-permute-start | bytes 1769480 | tf_op jit(solution)/shard_map/ppermute | solution.py:172
  79.2 1.8 %pick.3 = bf16[2,384,384]{2,1,0:T(8,128)(2,1)} custom-call(bf16[2,2,384,384]{3,2,1,0:T(8,128)(2,1)} %collective-permute-done.5.right_ref.rest_2_), custom_call_target="tpu_custom_call" | custom-call | tf_op jit(solution)/shard_map/pick/pallas_call | solution.py:158
  81.1 3.7 %collective-permute-start.7 = (bf16[2,384,384]{2,1,0:T(8,128)(2,1)}, bf16[2,384,384]{2,1,0:T(8,128)(2,1)}, u32[]{:S(2)}, u32[]{:S(2)}) collective-permute-start(bf16[2,384,384]{2,1,0:T(8,128)(2,1)} %pick.3), channel_id=1, source_target_pairs={{0,7},{1,0},{2,1},{3,2},{4,3},{5,4},{6,5},{7,6},{8,15},{9,8},{10,9... | collective-permute-start | bytes 1769480 | tf_op jit(solution)/shard_map/ppermute | solution.py:172
  84.9 0.7 fusion.sector_ref
  85.6 8.9 %collective-permute-done.6.rest_3_ = bf16[2,384,384]{2,1,0:T(8,128)(2,1)} collective-permute-done((bf16[2,384,384]{2,1,0:T(8,128)(2,1)}, bf16[2,384,384]{2,1,0:T(8,128)(2,1)}, u32[]{:S(2)}, u32[]{:S(2)}) %collective-permute-start.6) | collective-permute-done | bytes 589856 | tf_op jit(solution)/shard_map/ppermute | solution.py:172
  94.5 4.1 %collective-permute-done.7.rest_4_ = bf16[2,384,384]{2,1,0:T(8,128)(2,1)} collective-permute-done((bf16[2,384,384]{2,1,0:T(8,128)(2,1)}, bf16[2,384,384]{2,1,0:T(8,128)(2,1)}, u32[]{:S(2)}, u32[]{:S(2)}) %collective-permute-start.7) | collective-permute-done | bytes 589856 | tf_op jit(solution)/shard_map/ppermute | solution.py:172
  98.6 13.9 %contract.1 = bf16[3072,128]{1,0:T(8,128)(2,1)} custom-call(s32[64]{0:T(128)} %fusion.sector_ref, bf16[64,32,384]{2,1,0:T(8,128)(2,1)} %copy-done.2, bf16[64,32,128]{2,1,0:T(8,128)(2,1)} %all-to-all-done.1.left_ref, bf16[2,2,384,384]{3,2,1,0:T(8,128)(2,1)} %rest_0_.1, bf16[2,2,384,384]{3,2,1,0:T(8,128)(2,1)} %collective-permute-done.4.right_ref.rest_1_, ...), custom_call_target="tpu_custom_call" | custom-call | flops 7000000000 | bytes 8000000 | tf_op jit(solution)/shard_map/contract/pallas_call | solution.py:105
  112.5 44.8 %all_to_all.15 = bf16[512,3,2,128]{3,2,1,0:T(2,128)(2,1)S(1)} all-to-all(bf16[512,3,2,128]{3,2,1,0:T(2,128)(2,1)} %bitcast.25), channel_id=1, replica_groups=mesh['sec'=64,'op'=8] {'sec','op'}, dimensions={0} | all-to-all | bytes 1572864 | tf_op jit(solution)/shard_map/all_to_all | solution.py:206
  157.3 1.3 collect.1
  (29 shorter events, 1.1 us)
Async XLA Ops:
  0.0 1.6 %copy-start = (bf16[64,32,384]{2,1,0:T(8,128)(2,1)S(1)}, bf16[64,32,384]{2,1,0:T(8,128)(2,1)}, u32[]{:S(2)}) copy-start(bf16[64,32,384]{2,1,0:T(8,128)(2,1)} %param.5) | copy-start | bytes 4718596
  3.6 58.4 %all-to-all-start = ((bf16[64,32,384]{2,1,0:T(8,128)(2,1)}), bf16[64,32,384]{2,1,0:T(8,128)(2,1)S(1)}, u32[]{:S(2)}, u32[]{:S(2)}) async-start(bf16[64,32,384]{2,1,0:T(8,128)(2,1)} %gather_fusion.1), calls=%async_computation | async-start | bytes 3145728 | tf_op jit(solution)/shard_map/all_to_all | solution.py:177
  19.8 14.5 %collective-permute-start = (bf16[16,16,128]{2,1,0:T(8,128)(2,1)S(1)}, bf16[16,16,128]{2,1,0:T(8,128)(2,1)S(1)}, u32[]{:S(2)}, u32[]{:S(2)}) collective-permute-start(bf16[16,16,128]{2,1,0:T(8,128)(2,1)S(1)} %reshape.46), channel_id=1, source_target_pairs={{0,2},{1,3},{2,4},{3,5},{4,6},{5,7},{6,0},{7,1},{8,10},{9,11},{10,... | collective-permute-start | bytes 196616 | tf_op jit(solution)/shard_map/ppermute | solution.py:172
  24.0 10.2 %collective-permute-start.1 = (bf16[16,16,128]{2,1,0:T(8,128)(2,1)S(1)}, bf16[16,16,128]{2,1,0:T(8,128)(2,1)S(1)}, u32[]{:S(2)}, u32[]{:S(2)}) collective-permute-start(bf16[16,16,128]{2,1,0:T(8,128)(2,1)S(1)} %reshape.46), channel_id=1, source_target_pairs={{0,6},{1,7},{2,0},{3,1},{4,2},{5,3},{6,4},{7,5},{8,14},{9,15},{10,... | collective-permute-start | bytes 196616 | tf_op jit(solution)/shard_map/ppermute | solution.py:172
  27.6 46.6 %collective-permute-start.4 = (bf16[2,2,384,384]{3,2,1,0:T(8,128)(2,1)}, bf16[2,2,384,384]{3,2,1,0:T(8,128)(2,1)}, u32[]{:S(2)}, u32[]{:S(2)}) collective-permute-start(bf16[2,2,384,384]{3,2,1,0:T(8,128)(2,1)} %rest_0_.1), channel_id=1, source_target_pairs={{0,1},{1,2},{2,3},{3,4},{4,5},{5,6},{6,7},{7,0},{8,9},{9,10},{10,1... | collective-permute-start | bytes 3538952 | tf_op jit(solution)/shard_map/ppermute | solution.py:172
  30.4 48.8 %collective-permute-start.5 = (bf16[2,2,384,384]{3,2,1,0:T(8,128)(2,1)}, bf16[2,2,384,384]{3,2,1,0:T(8,128)(2,1)}, u32[]{:S(2)}, u32[]{:S(2)}) collective-permute-start(bf16[2,2,384,384]{3,2,1,0:T(8,128)(2,1)} %rest_0_.1), channel_id=1, source_target_pairs={{0,7},{1,0},{2,1},{3,2},{4,3},{5,4},{6,5},{7,6},{8,15},{9,8},{10,9... | collective-permute-start | bytes 3538952 | tf_op jit(solution)/shard_map/ppermute | solution.py:172
  34.3 25.9 %collective-permute-start.3 = (bf16[16,16,128]{2,1,0:T(8,128)(2,1)S(1)}, bf16[16,16,128]{2,1,0:T(8,128)(2,1)S(1)}, u32[]{:S(2)}, u32[]{:S(2)}) collective-permute-start(bf16[16,16,128]{2,1,0:T(8,128)(2,1)S(1)} %reshape.46), channel_id=1, source_target_pairs={{0,7},{1,0},{2,1},{3,2},{4,3},{5,4},{6,5},{7,6},{8,15},{9,8},{10,9... | collective-permute-start | bytes 196616 | tf_op jit(solution)/shard_map/ppermute | solution.py:172
  36.5 23.7 %collective-permute-start.2 = (bf16[16,16,128]{2,1,0:T(8,128)(2,1)S(1)}, bf16[16,16,128]{2,1,0:T(8,128)(2,1)S(1)}, u32[]{:S(2)}, u32[]{:S(2)}) collective-permute-start(bf16[16,16,128]{2,1,0:T(8,128)(2,1)S(1)} %reshape.46), channel_id=1, source_target_pairs={{0,1},{1,2},{2,3},{3,4},{4,5},{5,6},{6,7},{7,0},{8,9},{9,10},{10,1... | collective-permute-start | bytes 196616 | tf_op jit(solution)/shard_map/ppermute | solution.py:172
  61.9 19.1 %copy-start.2 = (bf16[64,32,384]{2,1,0:T(8,128)(2,1)}, bf16[64,32,384]{2,1,0:T(8,128)(2,1)S(1)}, u32[]{:S(2)}) copy-start(bf16[64,32,384]{2,1,0:T(8,128)(2,1)S(1)} %all-to-all-done.psi_ref) | copy-start | bytes 4718596
  61.9 36.6 %all-to-all-start.1 = ((bf16[64,32,128]{2,1,0:T(8,128)(2,1)}), bf16[64,32,128]{2,1,0:T(8,128)(2,1)}, u32[]{:S(2)}, u32[]{:S(2)}) async-start(bf16[64,32,128]{2,1,0:T(8,128)(2,1)} %gather_fusion), calls=%async_computation.1 | async-start | bytes 1048576 | tf_op jit(solution)/shard_map/all_to_all | solution.py:196
  74.2 10.5 %copy-start.3 = (s32[128]{0:T(128)S(1)}, s32[128]{0:T(128)}, u32[]{:S(2)}) copy-start(s32[128]{0:T(128)} %param.9) | copy-start | bytes 1540
  76.1 18.4 %collective-permute-start.6 = (bf16[2,384,384]{2,1,0:T(8,128)(2,1)}, bf16[2,384,384]{2,1,0:T(8,128)(2,1)}, u32[]{:S(2)}, u32[]{:S(2)}) collective-permute-start(bf16[2,384,384]{2,1,0:T(8,128)(2,1)} %pick.2), channel_id=1, source_target_pairs={{0,1},{1,2},{2,3},{3,4},{4,5},{5,6},{6,7},{7,0},{8,9},{9,10},{10,1... | collective-permute-start | bytes 1769480 | tf_op jit(solution)/shard_map/ppermute | solution.py:172
  81.1 17.5 %collective-permute-start.7 = (bf16[2,384,384]{2,1,0:T(8,128)(2,1)}, bf16[2,384,384]{2,1,0:T(8,128)(2,1)}, u32[]{:S(2)}, u32[]{:S(2)}) collective-permute-start(bf16[2,384,384]{2,1,0:T(8,128)(2,1)} %pick.3), channel_id=1, source_target_pairs={{0,7},{1,0},{2,1},{3,2},{4,3},{5,4},{6,5},{7,6},{8,15},{9,8},{10,9... | collective-permute-start | bytes 1769480 | tf_op jit(solution)/shard_map/ppermute | solution.py:172
  112.5 44.8 %copy-start.1 = (s32[64,3]{0,1:T(4,128)S(1)}, s32[64,3]{0,1:T(4,128)}, u32[]{:S(2)}) copy-start(s32[64,3]{0,1:T(4,128)} %param.8) | copy-start | bytes 2308

commit v6 on v4

--- a/solution.py
+++ b/solution.py
@@ -13,22 +13,38 @@
     return lax.broadcasted_iota(jnp.int32, shape, dim)
 
 
-def contract_kernel(sector_ref, psi_ref, left_ref, *rest):
-    right_refs, (out_ref, right_scr, x_scr, part_scr, piece_scr, sem) = rest[:5], rest[5:]
+def right_copies(right_refs, right_scr, sem):
     copies = []
-    for term in range(8):
+    for term, source in enumerate(right_refs):
         for sector in range(2):
-            if term < 6:
-                source = right_refs[term // 2].at[sector, term % 2]
-            else:
-                source = right_refs[term - 3].at[sector]
             copies.append(
                 pltpu.make_async_copy(
-                    source,
+                    source(sector),
                     right_scr.at[pl.ds(term * 384, 384), pl.ds(sector * 384, 384)],
                     sem.at[term * 2 + sector],
                 )
             )
+    return copies
+
+
+def by_sector(sector_ref, total):
+    rows = []
+    for j in range(64):
+        here = total[j * 16 : j * 16 + 16]
+        rows.append(jnp.where(sector_ref[j] == 1, here[:, 384:], here[:, :384]))
+    return rows
+
+
+def first_kernel(sector_ref, psi_ref, left_ref, own_ref, before_ref, after_ref, sum_ref, last_ref, right_scr, x_scr, sem):
+    copies = right_copies(
+        [
+            lambda sector, ref=ref, term=term: ref.at[sector, term]
+            for ref in (own_ref, before_ref, after_ref)
+            for term in range(2)
+        ],
+        right_scr,
+        sem,
+    )
     for copy in copies:
         copy.start()
 
@@ -51,33 +67,45 @@
         for kk in range(4):
             for half in range(2):
                 term = half * 4 + kk
-                x_scr[pl.ds(row, 128), term * 384 : term * 384 + 384] = product[kk, :, half].reshape(128, 384)
+                target, term = (x_scr, term) if term < 6 else (last_ref, term - 6)
+                target[pl.ds(row, 128), term * 384 : term * 384 + 384] = product[kk, :, half].reshape(128, 384)
         return carry
 
     lax.fori_loop(0, 8, left_group, 0, unroll=2)
     for copy in copies:
         copy.wait()
 
+    def right_all(index, carry):
+        total = jnp.dot(x_scr[...], right_scr[...], preferred_element_type=F32)
+        for j, rows in enumerate(by_sector(sector_ref, total)):
+            sum_ref[j * 16 : j * 16 + 16, :] = rows
+        return carry
+
+    lax.fori_loop(0, 1, right_all, 0)
+
+
+def last_kernel(sector_ref, sum_ref, last_ref, before_ref, after_ref, out_ref, right_scr, part_scr, piece_scr, sem):
+    copies = right_copies([lambda sector, ref=ref: ref.at[sector] for ref in (before_ref, after_ref)], right_scr, sem)
+    for copy in copies:
+        copy.start()
     place = iota((384, 384), 1)
     wanted = 48 * ((place >> 4) & 7) + 16 * (place >> 7) + (place & 15)
     reorder = jnp.where(iota((384, 384), 0) == wanted, 1.0, 0.0).astype(BF16)
-
-    def right_group(index, carry):
-        row = pl.multiple_of(index * 1024, 1024)
-        total = jnp.dot(x_scr[pl.ds(row, 1024), :], right_scr[...], preferred_element_type=F32)
+    for copy in copies:
+        copy.wait()
+
+    def right_all(index, carry):
+        total = jnp.dot(last_ref[...], right_scr[...], preferred_element_type=F32)
         chosen = []
-        for j in range(64):
-            entry = sector_ref[index * 64 + j]
-            rows = total[j * 16 : j * 16 + 16]
-            rows = jnp.where(entry == 1, rows[:, 384:], rows[:, :384])
-            chosen.append(jnp.where(entry >= 0, rows, 0.0))
+        for j, rows in enumerate(by_sector(sector_ref, total)):
+            chosen.append(jnp.where(sector_ref[j] >= 0, rows + sum_ref[j * 16 : j * 16 + 16, :], 0.0))
         chosen = jnp.concatenate(chosen, axis=0).astype(BF16)
         ordered = jnp.dot(chosen, reorder, preferred_element_type=F32)
         for tile in range(3):
-            part_scr[pl.ds(tile * 1024 + row, 1024), :] = ordered[:, tile * 128 : tile * 128 + 128]
+            part_scr[pl.ds(tile * 1024, 1024), :] = ordered[:, tile * 128 : tile * 128 + 128]
         return carry
 
-    lax.fori_loop(0, 1, right_group, 0)
+    lax.fori_loop(0, 1, right_all, 0)
 
     lane_group = iota((64, 128), 1) >> 4
     for upper in range(2):
@@ -102,23 +130,37 @@
 
 def contract(slot_sector, psi, left, rights):
     vmem = pl.BlockSpec(memory_space=pltpu.VMEM)
+    hbm = pl.BlockSpec(memory_space=pltpu.HBM)
+    smem = pl.BlockSpec(memory_space=pltpu.SMEM)
+    sums, last = pl.pallas_call(
+        first_kernel,
+        out_shape=[jax.ShapeDtypeStruct((1024, 384), F32), jax.ShapeDtypeStruct((1024, 768), BF16)],
+        in_specs=[smem, vmem, vmem, hbm, hbm, hbm],
+        out_specs=[vmem, vmem],
+        scratch_shapes=[
+            pltpu.VMEM((2304, 768), BF16),
+            pltpu.VMEM((1024, 2304), BF16),
+            pltpu.SemaphoreType.DMA((12,)),
+        ],
+        compiler_params=pltpu.CompilerParams(vmem_limit_bytes=60 << 20),
+        cost_estimate=pl.CostEstimate(flops=6_000_000_000, bytes_accessed=9_000_000, transcendentals=0),
+        name="contract_first",
+    )(slot_sector, psi, left, *rights[:3])
     return pl.pallas_call(
-        contract_kernel,
+        last_kernel,
         out_shape=jax.ShapeDtypeStruct((3072, 128), BF16),
-        in_specs=[pl.BlockSpec(memory_space=pltpu.SMEM), vmem, vmem]
-        + [pl.BlockSpec(memory_space=pltpu.HBM)] * 5,
+        in_specs=[smem, vmem, vmem, hbm, hbm],
         out_specs=vmem,
         scratch_shapes=[
-            pltpu.VMEM((3072, 768), BF16),
-            pltpu.VMEM((1024, 3072), BF16),
+            pltpu.VMEM((768, 768), BF16),
             pltpu.VMEM((3072, 128), F32),
             pltpu.VMEM((3072, 128), F32),
-            pltpu.SemaphoreType.DMA((16,)),
+            pltpu.SemaphoreType.DMA((4,)),
         ],
         compiler_params=pltpu.CompilerParams(vmem_limit_bytes=60 << 20),
-        cost_estimate=pl.CostEstimate(flops=7_000_000_000, bytes_accessed=8_000_000, transcendentals=0),
-        name="contract",
-    )(slot_sector, psi, left, *rights)
+        cost_estimate=pl.CostEstimate(flops=2_000_000_000, bytes_accessed=5_000_000, transcendentals=0),
+        name="contract_last",
+    )(slot_sector, sums, last, *rights[3:])
 
 
 def collect_kernel(table_ref, piece_ref, out_ref, wide_scr):

time: 150 us -> 143 us (0.953)
  waiting for transfers between devices: 28.1 us -> 22.1 us
  blocking collectives: 46 us -> 41.2 us
  Pallas kernels: 18.8 us -> 23.5 us
    ppermute x8, waiting for transfers between devices: 11.6 us -> 0.02 us  [per_device(): lax.ppermute(value, 'op', [(i, (i + step) % 8) for i in range(8)])]
    all_to_all x1, waiting for transfers between devices: 0.01 us -> 5.61 us  [per_device(): lax.all_to_all(left_here, 'sec', split_axis=0, concat_axis=0, tiled=True)]
    all_to_all x1, blocking collectives: 46 us -> 41.2 us  [per_device(): lax.all_to_all(pieces.reshape(512, 3, 2, 128), ('sec', 'op'), split_axis=...]
    pallas_call x1 -> x2, Pallas kernels: 13.9 us -> 18.5 us  [the longest x1 11 us: contract(): pl.pallas_call(first_kernel, out_shape=[jax.ShapeDtypeStruct((1024, 384),...]
  transfers between devices with their start and end apart: 10 -> 10, of which waited for: 3 -> 2; matrix products, arithmetic and copies ran while one was open for 3% -> 3% of each run, Pallas kernels for 2% -> 10%
where the time goes in v6:
time: 143 us
  starting transfers between devices  47.8 us (33%)
  blocking collectives  41.2 us (29%)
  Pallas kernels  23.5 us (16%)
  waiting for transfers between devices  22.1 us (15%)
  local copies, waits for them, and re-layouts  5.86 us (4%)
  other arithmetic  2.01 us (1%)
    all_to_all x1, blocking collectives, per_device(): lax.all_to_all(pieces.reshape(512, 3, 2, 128), ('sec', 'op'), split_axis=...  41.2 us
    ppermute x8, starting transfers between devices, per_device(): lax.ppermute(value, 'op', [(i, (i + step) % 8) for i in range(8)])  26.7 us
    all_to_all x1, waiting for transfers between devices, per_device(): lax.all_to_all(psi.at[source].get(mode='promise_in_bounds'), 'sec', split...  16.4 us
    all_to_all x1, starting transfers between devices, per_device(): lax.all_to_all(psi.at[source].get(mode='promise_in_bounds'), 'sec', split...  14.8 us
    pallas_call x1, Pallas kernels, contract(): pl.pallas_call(first_kernel, out_shape=[jax.ShapeDtypeStruct((1024, 384),...  11 us
    pallas_call x1, Pallas kernels, contract(): pl.pallas_call(last_kernel, out_shape=jax.ShapeDtypeStruct((3072, 128), B...  7.49 us
    all_to_all x1, starting transfers between devices, per_device(): lax.all_to_all(left_here, 'sec', split_axis=0, concat_axis=0, tiled=True)  6.31 us
    all_to_all x1, waiting for transfers between devices, per_device(): lax.all_to_all(left_here, 'sec', split_axis=0, concat_axis=0, tiled=True)  5.61 us
  transfers between devices with their start and end apart: 10, of which 2 were waited for; matrix products, arithmetic and copies ran while one was open for 3% of the time, Pallas kernels for 10%

profile of v6, /device:TPU:1, one launch (start us, length us, event | category | flops | bytes accessed | tf_op | source)
XLA Modules:
  0.0 142.7 jit_solution(13683505576022533073)
XLA Ops:
  0.0 0.8 slice_bitcast_fusion
  0.8 0.7 compare_bitcast_fusion
  1.7 1.9 %gather_fusion.1 = bf16[64,32,384]{2,1,0:T(8,128)(2,1)} fusion(bf16[64,32,384]{2,1,0:T(8,128)(2,1)S(1)} %copy-done, s32[1024]{0:T(1024)S(1)} %pad_clamp_fusion), kind=kCustom, calls=%fused_computation.1 | custom fusion | bytes 3145984 | tf_op jit(solution)/shard_map/gather | solution.py:220
  3.6 14.8 %all-to-all-start = ((bf16[64,32,384]{2,1,0:T(8,128)(2,1)}), bf16[64,32,384]{2,1,0:T(8,128)(2,1)S(1)}, u32[]{:S(2)}, u32[]{:S(2)}) async-start(bf16[64,32,384]{2,1,0:T(8,128)(2,1)} %gather_fusion.1), calls=%async_computation | async-start | bytes 3145728 | tf_op jit(solution)/shard_map/all_to_all | solution.py:219
  18.4 1.2 copy.9
  19.8 4.2 %collective-permute-start.2 = (bf16[16,16,128]{2,1,0:T(8,128)(2,1)S(1)}, bf16[16,16,128]{2,1,0:T(8,128)(2,1)S(1)}, u32[]{:S(2)}, u32[]{:S(2)}) collective-permute-start(bf16[16,16,128]{2,1,0:T(8,128)(2,1)S(1)} %reshape.46), channel_id=1, source_target_pairs={{0,2},{1,3},{2,4},{3,5},{4,6},{5,7},{6,0},{7,1},{8,10},{9,11},{10,... | collective-permute-start | bytes 196616 | tf_op jit(solution)/shard_map/ppermute | solution.py:214
  24.0 3.6 %collective-permute-start.3 = (bf16[16,16,128]{2,1,0:T(8,128)(2,1)S(1)}, bf16[16,16,128]{2,1,0:T(8,128)(2,1)S(1)}, u32[]{:S(2)}, u32[]{:S(2)}) collective-permute-start(bf16[16,16,128]{2,1,0:T(8,128)(2,1)S(1)} %reshape.46), channel_id=1, source_target_pairs={{0,6},{1,7},{2,0},{3,1},{4,2},{5,3},{6,4},{7,5},{8,14},{9,15},{10,... | collective-permute-start | bytes 196616 | tf_op jit(solution)/shard_map/ppermute | solution.py:214
  27.6 3.5 %collective-permute-start.1 = (bf16[16,16,128]{2,1,0:T(8,128)(2,1)S(1)}, bf16[16,16,128]{2,1,0:T(8,128)(2,1)S(1)}, u32[]{:S(2)}, u32[]{:S(2)}) collective-permute-start(bf16[16,16,128]{2,1,0:T(8,128)(2,1)S(1)} %reshape.46), channel_id=1, source_target_pairs={{0,7},{1,0},{2,1},{3,2},{4,3},{5,4},{6,5},{7,6},{8,15},{9,8},{10,9... | collective-permute-start | bytes 196616 | tf_op jit(solution)/shard_map/ppermute | solution.py:214
  31.1 1.9 %collective-permute-start = (bf16[16,16,128]{2,1,0:T(8,128)(2,1)S(1)}, bf16[16,16,128]{2,1,0:T(8,128)(2,1)S(1)}, u32[]{:S(2)}, u32[]{:S(2)}) collective-permute-start(bf16[16,16,128]{2,1,0:T(8,128)(2,1)S(1)} %reshape.46), channel_id=1, source_target_pairs={{0,1},{1,2},{2,3},{3,4},{4,5},{5,6},{6,7},{7,0},{8,9},{9,10},{10,1... | collective-permute-start | bytes 196616 | tf_op jit(solution)/shard_map/ppermute | solution.py:214
  33.0 2.7 %collective-permute-start.4 = (bf16[2,2,384,384]{3,2,1,0:T(8,128)(2,1)}, bf16[2,2,384,384]{3,2,1,0:T(8,128)(2,1)}, u32[]{:S(2)}, u32[]{:S(2)}) collective-permute-start(bf16[2,2,384,384]{3,2,1,0:T(8,128)(2,1)} %own_ref.1), channel_id=1, source_target_pairs={{0,1},{1,2},{2,3},{3,4},{4,5},{5,6},{6,7},{7,0},{8,9},{9,10},{10,1... | collective-permute-start | bytes 3538952 | tf_op jit(solution)/shard_map/ppermute | solution.py:214
  35.9 3.8 %collective-permute-start.5 = (bf16[2,2,384,384]{3,2,1,0:T(8,128)(2,1)}, bf16[2,2,384,384]{3,2,1,0:T(8,128)(2,1)}, u32[]{:S(2)}, u32[]{:S(2)}) collective-permute-start(bf16[2,2,384,384]{3,2,1,0:T(8,128)(2,1)} %own_ref.1), channel_id=1, source_target_pairs={{0,7},{1,0},{2,1},{3,2},{4,3},{5,4},{6,5},{7,6},{8,15},{9,8},{10,9... | collective-permute-start | bytes 3538952 | tf_op jit(solution)/shard_map/ppermute | solution.py:214
  40.4 1.4 gather_fusion
  41.8 16.4 %all-to-all-done.psi_ref = bf16[64,32,384]{2,1,0:T(8,128)(2,1)S(1)} async-done(((bf16[64,32,384]{2,1,0:T(8,128)(2,1)}), bf16[64,32,384]{2,1,0:T(8,128)(2,1)S(1)}, u32[]{:S(2)}, u32[]{:S(2)}) %all-to-all-start) | async-done | bytes 1572896 | tf_op jit(solution)/shard_map/all_to_all | solution.py:219
  58.2 6.3 %all-to-all-start.1 = ((bf16[64,32,128]{2,1,0:T(8,128)(2,1)}), bf16[64,32,128]{2,1,0:T(8,128)(2,1)}, u32[]{:S(2)}, u32[]{:S(2)}) async-start(bf16[64,32,128]{2,1,0:T(8,128)(2,1)} %gather_fusion), calls=%async_computation.1 | async-start | bytes 1048576 | tf_op jit(solution)/shard_map/all_to_all | solution.py:237
  64.7 1.9 %pick.2 = bf16[2,384,384]{2,1,0:T(8,128)(2,1)} custom-call(bf16[2,2,384,384]{3,2,1,0:T(8,128)(2,1)} %collective-permute-done.4.before_ref.right_ref), custom_call_target="tpu_custom_call" | custom-call | tf_op jit(solution)/shard_map/pick/pallas_call | solution.py:200
  66.6 3.2 %collective-permute-start.6 = (bf16[2,384,384]{2,1,0:T(8,128)(2,1)}, bf16[2,384,384]{2,1,0:T(8,128)(2,1)}, u32[]{:S(2)}, u32[]{:S(2)}) collective-permute-start(bf16[2,384,384]{2,1,0:T(8,128)(2,1)} %pick.2), channel_id=1, source_target_pairs={{0,1},{1,2},{2,3},{3,4},{4,5},{5,6},{6,7},{7,0},{8,9},{9,10},{10,1... | collective-permute-start | bytes 1769480 | tf_op jit(solution)/shard_map/ppermute | solution.py:214
  69.8 1.9 %pick.3 = bf16[2,384,384]{2,1,0:T(8,128)(2,1)} custom-call(bf16[2,2,384,384]{3,2,1,0:T(8,128)(2,1)} %collective-permute-done.5.after_ref.right_ref), custom_call_target="tpu_custom_call" | custom-call | tf_op jit(solution)/shard_map/pick/pallas_call | solution.py:200
  71.6 3.8 %collective-permute-start.7 = (bf16[2,384,384]{2,1,0:T(8,128)(2,1)}, bf16[2,384,384]{2,1,0:T(8,128)(2,1)}, u32[]{:S(2)}, u32[]{:S(2)}) collective-permute-start(bf16[2,384,384]{2,1,0:T(8,128)(2,1)} %pick.3), channel_id=1, source_target_pairs={{0,7},{1,0},{2,1},{3,2},{4,3},{5,4},{6,5},{7,6},{8,15},{9,8},{10,9... | collective-permute-start | bytes 1769480 | tf_op jit(solution)/shard_map/ppermute | solution.py:214
  75.5 0.7 fusion.sector_ref
  76.2 5.6 %all-to-all-done.1.left_ref = bf16[64,32,128]{2,1,0:T(8,128)(2,1)} async-done(((bf16[64,32,128]{2,1,0:T(8,128)(2,1)}), bf16[64,32,128]{2,1,0:T(8,128)(2,1)}, u32[]{:S(2)}, u32[]{:S(2)}) %all-to-all-start.1) | async-done | bytes 524320 | tf_op jit(solution)/shard_map/all_to_all | solution.py:237
  81.8 11.0 %contract_first.1 = (f32[1024,384]{1,0:T(8,128)}, bf16[1024,768]{1,0:T(8,128)(2,1)}) custom-call(s32[64]{0:T(128)} %fusion.sector_ref, bf16[64,32,384]{2,1,0:T(8,128)(2,1)} %copy-done.2, bf16[64,32,128]{2,1,0:T(8,128)(2,1)} %all-to-all-done.1.left_ref, bf16[2,2,384,384]{3,2,1,0:T(8,128)(2,1)} %own_ref.1, ...), custom_call_target="tpu_custom_call" | custom-call | flops 6000000000 | bytes 9000000 | tf_op jit(solution)/shard_map/contract_first/pallas_call | solution.py:135
  92.8 7.5 %contract_last.1 = bf16[3072,128]{1,0:T(8,128)(2,1)} custom-call(s32[64]{0:T(128)} %fusion.sector_ref, f32[1024,384]{1,0:T(8,128)} %get-tuple-element.11.sum_ref, bf16[1024,768]{1,0:T(8,128)(2,1)} %get-tuple-element.12.last_ref, bf16[2,384,384]{2,1,0:T(8,128)(2,1)} %collective-permute-done.6.before_ref, bf16[2,384,384]{2,1,0:T(8,128)(2,1)} %collective-permute-done.7.after_ref), custom_call_target="tpu_custom_call" | custom-call | flops 2000000000 | bytes 5000000 | tf_op jit(solution)/shard_map/contract_last/pallas_call | solution.py:149
  100.3 41.2 %all_to_all.15 = bf16[512,3,2,128]{3,2,1,0:T(2,128)(2,1)S(1)} all-to-all(bf16[512,3,2,128]{3,2,1,0:T(2,128)(2,1)} %bitcast.25), channel_id=1, replica_groups=mesh['sec'=64,'op'=8] {'sec','op'}, dimensions={0} | all-to-all | bytes 1572864 | tf_op jit(solution)/shard_map/all_to_all | solution.py:247
  141.5 1.2 collect.1
  (30 shorter events, 1.1 us)
Async XLA Ops:
  0.0 1.6 %copy-start = (bf16[64,32,384]{2,1,0:T(8,128)(2,1)S(1)}, bf16[64,32,384]{2,1,0:T(8,128)(2,1)}, u32[]{:S(2)}) copy-start(bf16[64,32,384]{2,1,0:T(8,128)(2,1)} %param.5) | copy-start | bytes 4718596
  3.6 54.6 %all-to-all-start = ((bf16[64,32,384]{2,1,0:T(8,128)(2,1)}), bf16[64,32,384]{2,1,0:T(8,128)(2,1)S(1)}, u32[]{:S(2)}, u32[]{:S(2)}) async-start(bf16[64,32,384]{2,1,0:T(8,128)(2,1)} %gather_fusion.1), calls=%async_computation | async-start | bytes 3145728 | tf_op jit(solution)/shard_map/all_to_all | solution.py:219
  19.8 16.1 %collective-permute-start.2 = (bf16[16,16,128]{2,1,0:T(8,128)(2,1)S(1)}, bf16[16,16,128]{2,1,0:T(8,128)(2,1)S(1)}, u32[]{:S(2)}, u32[]{:S(2)}) collective-permute-start(bf16[16,16,128]{2,1,0:T(8,128)(2,1)S(1)} %reshape.46), channel_id=1, source_target_pairs={{0,2},{1,3},{2,4},{3,5},{4,6},{5,7},{6,0},{7,1},{8,10},{9,11},{10,... | collective-permute-start | bytes 196616 | tf_op jit(solution)/shard_map/ppermute | solution.py:214
  24.0 15.8 %collective-permute-start.3 = (bf16[16,16,128]{2,1,0:T(8,128)(2,1)S(1)}, bf16[16,16,128]{2,1,0:T(8,128)(2,1)S(1)}, u32[]{:S(2)}, u32[]{:S(2)}) collective-permute-start(bf16[16,16,128]{2,1,0:T(8,128)(2,1)S(1)} %reshape.46), channel_id=1, source_target_pairs={{0,6},{1,7},{2,0},{3,1},{4,2},{5,3},{6,4},{7,5},{8,14},{9,15},{10,... | collective-permute-start | bytes 196616 | tf_op jit(solution)/shard_map/ppermute | solution.py:214
  27.6 12.4 %collective-permute-start.1 = (bf16[16,16,128]{2,1,0:T(8,128)(2,1)S(1)}, bf16[16,16,128]{2,1,0:T(8,128)(2,1)S(1)}, u32[]{:S(2)}, u32[]{:S(2)}) collective-permute-start(bf16[16,16,128]{2,1,0:T(8,128)(2,1)S(1)} %reshape.46), channel_id=1, source_target_pairs={{0,7},{1,0},{2,1},{3,2},{4,3},{5,4},{6,5},{7,6},{8,15},{9,8},{10,9... | collective-permute-start | bytes 196616 | tf_op jit(solution)/shard_map/ppermute | solution.py:214
  31.1 9.0 %collective-permute-start = (bf16[16,16,128]{2,1,0:T(8,128)(2,1)S(1)}, bf16[16,16,128]{2,1,0:T(8,128)(2,1)S(1)}, u32[]{:S(2)}, u32[]{:S(2)}) collective-permute-start(bf16[16,16,128]{2,1,0:T(8,128)(2,1)S(1)} %reshape.46), channel_id=1, source_target_pairs={{0,1},{1,2},{2,3},{3,4},{4,5},{5,6},{6,7},{7,0},{8,9},{9,10},{10,1... | collective-permute-start | bytes 196616 | tf_op jit(solution)/shard_map/ppermute | solution.py:214
  33.0 31.7 %collective-permute-start.4 = (bf16[2,2,384,384]{3,2,1,0:T(8,128)(2,1)}, bf16[2,2,384,384]{3,2,1,0:T(8,128)(2,1)}, u32[]{:S(2)}, u32[]{:S(2)}) collective-permute-start(bf16[2,2,384,384]{3,2,1,0:T(8,128)(2,1)} %own_ref.1), channel_id=1, source_target_pairs={{0,1},{1,2},{2,3},{3,4},{4,5},{5,6},{6,7},{7,0},{8,9},{9,10},{10,1... | collective-permute-start | bytes 3538952 | tf_op jit(solution)/shard_map/ppermute | solution.py:214
  35.9 33.9 %collective-permute-start.5 = (bf16[2,2,384,384]{3,2,1,0:T(8,128)(2,1)}, bf16[2,2,384,384]{3,2,1,0:T(8,128)(2,1)}, u32[]{:S(2)}, u32[]{:S(2)}) collective-permute-start(bf16[2,2,384,384]{3,2,1,0:T(8,128)(2,1)} %own_ref.1), channel_id=1, source_target_pairs={{0,7},{1,0},{2,1},{3,2},{4,3},{5,4},{6,5},{7,6},{8,15},{9,8},{10,9... | collective-permute-start | bytes 3538952 | tf_op jit(solution)/shard_map/ppermute | solution.py:214
  40.0 24.5 %copy-start.3 = (s32[128]{0:T(128)S(1)}, s32[128]{0:T(128)}, u32[]{:S(2)}) copy-start(s32[128]{0:T(128)} %param.9) | copy-start | bytes 1540
  58.2 13.4 %copy-start.2 = (bf16[64,32,384]{2,1,0:T(8,128)(2,1)}, bf16[64,32,384]{2,1,0:T(8,128)(2,1)S(1)}, u32[]{:S(2)}) copy-start(bf16[64,32,384]{2,1,0:T(8,128)(2,1)S(1)} %all-to-all-done.psi_ref) | copy-start | bytes 4718596
  58.2 23.6 %all-to-all-start.1 = ((bf16[64,32,128]{2,1,0:T(8,128)(2,1)}), bf16[64,32,128]{2,1,0:T(8,128)(2,1)}, u32[]{:S(2)}, u32[]{:S(2)}) async-start(bf16[64,32,128]{2,1,0:T(8,128)(2,1)} %gather_fusion), calls=%async_computation.1 | async-start | bytes 1048576 | tf_op jit(solution)/shard_map/all_to_all | solution.py:237
  66.6 26.2 %collective-permute-start.6 = (bf16[2,384,384]{2,1,0:T(8,128)(2,1)}, bf16[2,384,384]{2,1,0:T(8,128)(2,1)}, u32[]{:S(2)}, u32[]{:S(2)}) collective-permute-start(bf16[2,384,384]{2,1,0:T(8,128)(2,1)} %pick.2), channel_id=1, source_target_pairs={{0,1},{1,2},{2,3},{3,4},{4,5},{5,6},{6,7},{7,0},{8,9},{9,10},{10,1... | collective-permute-start | bytes 1769480 | tf_op jit(solution)/shard_map/ppermute | solution.py:214
  71.6 21.1 %collective-permute-start.7 = (bf16[2,384,384]{2,1,0:T(8,128)(2,1)}, bf16[2,384,384]{2,1,0:T(8,128)(2,1)}, u32[]{:S(2)}, u32[]{:S(2)}) collective-permute-start(bf16[2,384,384]{2,1,0:T(8,128)(2,1)} %pick.3), channel_id=1, source_target_pairs={{0,7},{1,0},{2,1},{3,2},{4,3},{5,4},{6,5},{7,6},{8,15},{9,8},{10,9... | collective-permute-start | bytes 1769480 | tf_op jit(solution)/shard_map/ppermute | solution.py:214
  100.3 41.2 %copy-start.1 = (s32[64,3]{0,1:T(4,128)S(1)}, s32[64,3]{0,1:T(4,128)}, u32[]{:S(2)}) copy-start(s32[64,3]{0,1:T(4,128)} %param.8) | copy-start | bytes 2308

commit v7 on v6

--- a/solution.py
+++ b/solution.py
@@ -129,6 +129,7 @@
 
 
 def contract(slot_sector, psi, left, rights):
+    rights = [pltpu.with_memory_space_constraint(value, pltpu.HBM) for value in rights]
     vmem = pl.BlockSpec(memory_space=pltpu.VMEM)
     hbm = pl.BlockSpec(memory_space=pltpu.HBM)
     smem = pl.BlockSpec(memory_space=pltpu.SMEM)
@@ -142,7 +143,7 @@
             pltpu.VMEM((1024, 2304), BF16),
             pltpu.SemaphoreType.DMA((12,)),
         ],
-        compiler_params=pltpu.CompilerParams(vmem_limit_bytes=60 << 20),
+        compiler_params=pltpu.CompilerParams(vmem_limit_bytes=28 << 20),
         cost_estimate=pl.CostEstimate(flops=6_000_000_000, bytes_accessed=9_000_000, transcendentals=0),
         name="contract_first",
     )(slot_sector, psi, left, *rights[:3])
@@ -157,7 +158,7 @@
             pltpu.VMEM((3072, 128), F32),
             pltpu.SemaphoreType.DMA((4,)),
         ],
-        compiler_params=pltpu.CompilerParams(vmem_limit_bytes=60 << 20),
+        compiler_params=pltpu.CompilerParams(vmem_limit_bytes=20 << 20),
         cost_estimate=pl.CostEstimate(flops=2_000_000_000, bytes_accessed=5_000_000, transcendentals=0),
         name="contract_last",
     )(slot_sector, sums, last, *rights[3:])

time: 143 us -> 141 us (0.986)
  Pallas kernels: 23.5 us -> 19.2 us
  blocking collectives: 41.2 us -> 42.8 us
    pallas_call x1, Pallas kernels: 7.49 us -> 5.24 us  [contract(): pl.pallas_call(last_kernel, out_shape=jax.ShapeDtypeStruct((3072, 128), B...]
    pallas_call x1, Pallas kernels: 11 us -> 9.03 us  [contract(): pl.pallas_call(first_kernel, out_shape=[jax.ShapeDtypeStruct((1024, 384),...]
    all_to_all x1, blocking collectives: 41.2 us -> 42.8 us  [per_device(): lax.all_to_all(pieces.reshape(512, 3, 2, 128), ('sec', 'op'), split_axis=...]
  transfers between devices with their start and end apart: 10 -> 10, of which waited for: 2 -> 2; matrix products, arithmetic and copies ran while one was open for 3% -> 3% of each run, Pallas kernels for 10% -> 9%
where the time goes in v7:
time: 141 us; the launch traced here: 140 us
  starting transfers between devices  47.8 us (34%)
  blocking collectives  42.8 us (30%)
  waiting for transfers between devices  22.7 us (16%)
  Pallas kernels  19.2 us (14%)
  local copies, waits for them, and re-layouts  5.87 us (4%)
  other arithmetic  1.49 us (1%)
    all_to_all x1, blocking collectives, per_device(): lax.all_to_all(pieces.reshape(512, 3, 2, 128), ('sec', 'op'), split_axis=...  42.8 us
    ppermute x8, starting transfers between devices, per_device(): lax.ppermute(value, 'op', [(i, (i + step) % 8) for i in range(8)])  26.7 us
    all_to_all x1, waiting for transfers between devices, per_device(): lax.all_to_all(psi.at[source].get(mode='promise_in_bounds'), 'sec', split...  16.4 us
    all_to_all x1, starting transfers between devices, per_device(): lax.all_to_all(psi.at[source].get(mode='promise_in_bounds'), 'sec', split...  14.8 us
    pallas_call x1, Pallas kernels, contract(): pl.pallas_call(first_kernel, out_shape=[jax.ShapeDtypeStruct((1024, 384),...  9.03 us
    all_to_all x1, starting transfers between devices, per_device(): lax.all_to_all(left_here, 'sec', split_axis=0, concat_axis=0, tiled=True)  6.31 us
    all_to_all x1, waiting for transfers between devices, per_device(): lax.all_to_all(left_here, 'sec', split_axis=0, concat_axis=0, tiled=True)  6.24 us
    pallas_call x1, Pallas kernels, contract(): pl.pallas_call(last_kernel, out_shape=jax.ShapeDtypeStruct((3072, 128), B...  5.24 us
  transfers between devices with their start and end apart: 10, of which 2 were waited for; matrix products, arithmetic and copies ran while one was open for 3% of the time, Pallas kernels for 9%

profile of v7, /device:TPU:1, one launch (start us, length us, event | category | flops | bytes accessed | tf_op | source)
XLA Modules:
  0.0 140.1 jit_solution(4433554854229732755)
XLA Ops:
  0.0 0.8 slice_bitcast_fusion
  0.8 0.7 compare_bitcast_fusion
  1.7 1.9 %gather_fusion.1 = bf16[64,32,384]{2,1,0:T(8,128)(2,1)} fusion(bf16[64,32,384]{2,1,0:T(8,128)(2,1)S(1)} %copy-done, s32[1024]{0:T(1024)S(1)} %pad_clamp_fusion), kind=kCustom, calls=%fused_computation.1 | custom fusion | bytes 3145984 | tf_op jit(solution)/shard_map/gather | solution.py:221
  3.6 14.8 %all-to-all-start = ((bf16[64,32,384]{2,1,0:T(8,128)(2,1)}), bf16[64,32,384]{2,1,0:T(8,128)(2,1)S(1)}, u32[]{:S(2)}, u32[]{:S(2)}) async-start(bf16[64,32,384]{2,1,0:T(8,128)(2,1)} %gather_fusion.1), calls=%async_computation | async-start | bytes 3145728 | tf_op jit(solution)/shard_map/all_to_all | solution.py:220
  18.4 1.2 copy.9
  19.8 4.2 %collective-permute-start.2 = (bf16[16,16,128]{2,1,0:T(8,128)(2,1)S(1)}, bf16[16,16,128]{2,1,0:T(8,128)(2,1)S(1)}, u32[]{:S(2)}, u32[]{:S(2)}) collective-permute-start(bf16[16,16,128]{2,1,0:T(8,128)(2,1)S(1)} %reshape.46), channel_id=1, source_target_pairs={{0,2},{1,3},{2,4},{3,5},{4,6},{5,7},{6,0},{7,1},{8,10},{9,11},{10,... | collective-permute-start | bytes 196616 | tf_op jit(solution)/shard_map/ppermute | solution.py:215
  24.0 3.6 %collective-permute-start.3 = (bf16[16,16,128]{2,1,0:T(8,128)(2,1)S(1)}, bf16[16,16,128]{2,1,0:T(8,128)(2,1)S(1)}, u32[]{:S(2)}, u32[]{:S(2)}) collective-permute-start(bf16[16,16,128]{2,1,0:T(8,128)(2,1)S(1)} %reshape.46), channel_id=1, source_target_pairs={{0,6},{1,7},{2,0},{3,1},{4,2},{5,3},{6,4},{7,5},{8,14},{9,15},{10,... | collective-permute-start | bytes 196616 | tf_op jit(solution)/shard_map/ppermute | solution.py:215
  27.6 3.5 %collective-permute-start.1 = (bf16[16,16,128]{2,1,0:T(8,128)(2,1)S(1)}, bf16[16,16,128]{2,1,0:T(8,128)(2,1)S(1)}, u32[]{:S(2)}, u32[]{:S(2)}) collective-permute-start(bf16[16,16,128]{2,1,0:T(8,128)(2,1)S(1)} %reshape.46), channel_id=1, source_target_pairs={{0,7},{1,0},{2,1},{3,2},{4,3},{5,4},{6,5},{7,6},{8,15},{9,8},{10,9... | collective-permute-start | bytes 196616 | tf_op jit(solution)/shard_map/ppermute | solution.py:215
  31.1 1.9 %collective-permute-start = (bf16[16,16,128]{2,1,0:T(8,128)(2,1)S(1)}, bf16[16,16,128]{2,1,0:T(8,128)(2,1)S(1)}, u32[]{:S(2)}, u32[]{:S(2)}) collective-permute-start(bf16[16,16,128]{2,1,0:T(8,128)(2,1)S(1)} %reshape.46), channel_id=1, source_target_pairs={{0,1},{1,2},{2,3},{3,4},{4,5},{5,6},{6,7},{7,0},{8,9},{9,10},{10,1... | collective-permute-start | bytes 196616 | tf_op jit(solution)/shard_map/ppermute | solution.py:215
  33.0 2.7 %collective-permute-start.4 = (bf16[2,2,384,384]{3,2,1,0:T(8,128)(2,1)}, bf16[2,2,384,384]{3,2,1,0:T(8,128)(2,1)}, u32[]{:S(2)}, u32[]{:S(2)}) collective-permute-start(bf16[2,2,384,384]{3,2,1,0:T(8,128)(2,1)} %own_ref.1), channel_id=1, source_target_pairs={{0,1},{1,2},{2,3},{3,4},{4,5},{5,6},{6,7},{7,0},{8,9},{9,10},{10,1... | collective-permute-start | bytes 3538952 | tf_op jit(solution)/shard_map/ppermute | solution.py:215
  35.8 3.8 %collective-permute-start.5 = (bf16[2,2,384,384]{3,2,1,0:T(8,128)(2,1)}, bf16[2,2,384,384]{3,2,1,0:T(8,128)(2,1)}, u32[]{:S(2)}, u32[]{:S(2)}) collective-permute-start(bf16[2,2,384,384]{3,2,1,0:T(8,128)(2,1)} %own_ref.1), channel_id=1, source_target_pairs={{0,7},{1,0},{2,1},{3,2},{4,3},{5,4},{6,5},{7,6},{8,15},{9,8},{10,9... | collective-permute-start | bytes 3538952 | tf_op jit(solution)/shard_map/ppermute | solution.py:215
  40.3 1.5 %gather_fusion = bf16[64,32,128]{2,1,0:T(8,128)(2,1)} fusion(bf16[16,32,128]{2,1,0:T(8,128)(2,1)S(1)} %maximum_maximum_fusion, s32[1024]{0:T(1024)S(1)} %pad_clamp_fusion.1), kind=kCustom, calls=%fused_computation | custom fusion | bytes 1048832 | tf_op jit(solution)/shard_map/gather | solution.py:236
  41.8 16.4 %all-to-all-done.psi_ref = bf16[64,32,384]{2,1,0:T(8,128)(2,1)S(1)} async-done(((bf16[64,32,384]{2,1,0:T(8,128)(2,1)}), bf16[64,32,384]{2,1,0:T(8,128)(2,1)S(1)}, u32[]{:S(2)}, u32[]{:S(2)}) %all-to-all-start) | async-done | bytes 1572896 | tf_op jit(solution)/shard_map/all_to_all | solution.py:220
  58.2 6.3 %all-to-all-start.1 = ((bf16[64,32,128]{2,1,0:T(8,128)(2,1)}), bf16[64,32,128]{2,1,0:T(8,128)(2,1)}, u32[]{:S(2)}, u32[]{:S(2)}) async-start(bf16[64,32,128]{2,1,0:T(8,128)(2,1)} %gather_fusion), calls=%async_computation.1 | async-start | bytes 1048576 | tf_op jit(solution)/shard_map/all_to_all | solution.py:238
  64.7 1.8 %pick.2 = bf16[2,384,384]{2,1,0:T(8,128)(2,1)} custom-call(bf16[2,2,384,384]{3,2,1,0:T(8,128)(2,1)} %collective-permute-done.4.before_ref.right_ref), custom_call_target="tpu_custom_call" | custom-call | tf_op jit(solution)/shard_map/pick/pallas_call | solution.py:201
  66.5 3.2 %collective-permute-start.6 = (bf16[2,384,384]{2,1,0:T(8,128)(2,1)}, bf16[2,384,384]{2,1,0:T(8,128)(2,1)}, u32[]{:S(2)}, u32[]{:S(2)}) collective-permute-start(bf16[2,384,384]{2,1,0:T(8,128)(2,1)} %pick.2), channel_id=1, source_target_pairs={{0,1},{1,2},{2,3},{3,4},{4,5},{5,6},{6,7},{7,0},{8,9},{9,10},{10,1... | collective-permute-start | bytes 1769480 | tf_op jit(solution)/shard_map/ppermute | solution.py:215
  69.7 1.8 %pick.3 = bf16[2,384,384]{2,1,0:T(8,128)(2,1)} custom-call(bf16[2,2,384,384]{3,2,1,0:T(8,128)(2,1)} %collective-permute-done.5.after_ref.right_ref), custom_call_target="tpu_custom_call" | custom-call | tf_op jit(solution)/shard_map/pick/pallas_call | solution.py:201
  71.5 3.8 %collective-permute-start.7 = (bf16[2,384,384]{2,1,0:T(8,128)(2,1)}, bf16[2,384,384]{2,1,0:T(8,128)(2,1)}, u32[]{:S(2)}, u32[]{:S(2)}) collective-permute-start(bf16[2,384,384]{2,1,0:T(8,128)(2,1)} %pick.3), channel_id=1, source_target_pairs={{0,7},{1,0},{2,1},{3,2},{4,3},{5,4},{6,5},{7,6},{8,15},{9,8},{10,9... | collective-permute-start | bytes 1769480 | tf_op jit(solution)/shard_map/ppermute | solution.py:215
  75.3 0.2 fusion.sector_ref
  75.5 6.2 %all-to-all-done.1.left_ref = bf16[64,32,128]{2,1,0:T(8,128)(2,1)} async-done(((bf16[64,32,128]{2,1,0:T(8,128)(2,1)}), bf16[64,32,128]{2,1,0:T(8,128)(2,1)}, u32[]{:S(2)}, u32[]{:S(2)}) %all-to-all-start.1) | async-done | bytes 524320 | tf_op jit(solution)/shard_map/all_to_all | solution.py:238
  81.7 9.0 %contract_first.1 = (f32[1024,384]{1,0:T(8,128)S(1)}, bf16[1024,768]{1,0:T(8,128)(2,1)S(1)}) custom-call(s32[64]{0:T(128)S(1)} %fusion.sector_ref, bf16[64,32,384]{2,1,0:T(8,128)(2,1)S(1)} %all-to-all-done.psi_ref, bf16[64,32,128]{2,1,0:T(8,128)(2,1)} %all-to-all-done.1.left_ref, bf16[2,2,384,384]{3,2,1,0:T(8,128)(2,1)} %own_ref.1, ...), custom_call_target="tpu_custom_call" | custom-call | flops 6000000000 | bytes 9000000 | tf_op jit(solution)/shard_map/contract_first/pallas_call | solution.py:136
  90.8 5.2 %contract_last.1 = bf16[3072,128]{1,0:T(8,128)(2,1)S(1)} custom-call(s32[64]{0:T(128)S(1)} %fusion.sector_ref, f32[1024,384]{1,0:T(8,128)S(1)} %get-tuple-element.11.sum_ref, bf16[1024,768]{1,0:T(8,128)(2,1)S(1)} %get-tuple-element.12.last_ref, bf16[2,384,384]{2,1,0:T(8,128)(2,1)} %collective-permute-done.6.before_ref, ...), custom_call_target="tpu_custom_call" | custom-call | flops 2000000000 | bytes 5000000 | tf_op jit(solution)/shard_map/contract_last/pallas_call | solution.py:150
  96.1 42.8 %all_to_all.15 = bf16[512,3,2,128]{3,2,1,0:T(2,128)(2,1)S(1)} all-to-all(bf16[512,3,2,128]{3,2,1,0:T(2,128)(2,1)S(1)} %bitcast.23), channel_id=1, replica_groups=mesh['sec'=64,'op'=8] {'sec','op'}, dimensions={0} | all-to-all | bytes 1572864 | tf_op jit(solution)/shard_map/all_to_all | solution.py:248
  138.9 1.3 collect.1
  (28 shorter events, 1.1 us)
Async XLA Ops:
  0.0 1.6 %copy-start = (bf16[64,32,384]{2,1,0:T(8,128)(2,1)S(1)}, bf16[64,32,384]{2,1,0:T(8,128)(2,1)}, u32[]{:S(2)}) copy-start(bf16[64,32,384]{2,1,0:T(8,128)(2,1)} %param.5) | copy-start | bytes 4718596
  3.6 54.6 %all-to-all-start = ((bf16[64,32,384]{2,1,0:T(8,128)(2,1)}), bf16[64,32,384]{2,1,0:T(8,128)(2,1)S(1)}, u32[]{:S(2)}, u32[]{:S(2)}) async-start(bf16[64,32,384]{2,1,0:T(8,128)(2,1)} %gather_fusion.1), calls=%async_computation | async-start | bytes 3145728 | tf_op jit(solution)/shard_map/all_to_all | solution.py:220
  19.8 16.1 %collective-permute-start.2 = (bf16[16,16,128]{2,1,0:T(8,128)(2,1)S(1)}, bf16[16,16,128]{2,1,0:T(8,128)(2,1)S(1)}, u32[]{:S(2)}, u32[]{:S(2)}) collective-permute-start(bf16[16,16,128]{2,1,0:T(8,128)(2,1)S(1)} %reshape.46), channel_id=1, source_target_pairs={{0,2},{1,3},{2,4},{3,5},{4,6},{5,7},{6,0},{7,1},{8,10},{9,11},{10,... | collective-permute-start | bytes 196616 | tf_op jit(solution)/shard_map/ppermute | solution.py:215
  24.0 15.8 %collective-permute-start.3 = (bf16[16,16,128]{2,1,0:T(8,128)(2,1)S(1)}, bf16[16,16,128]{2,1,0:T(8,128)(2,1)S(1)}, u32[]{:S(2)}, u32[]{:S(2)}) collective-permute-start(bf16[16,16,128]{2,1,0:T(8,128)(2,1)S(1)} %reshape.46), channel_id=1, source_target_pairs={{0,6},{1,7},{2,0},{3,1},{4,2},{5,3},{6,4},{7,5},{8,14},{9,15},{10,... | collective-permute-start | bytes 196616 | tf_op jit(solution)/shard_map/ppermute | solution.py:215
  27.6 12.4 %collective-permute-start.1 = (bf16[16,16,128]{2,1,0:T(8,128)(2,1)S(1)}, bf16[16,16,128]{2,1,0:T(8,128)(2,1)S(1)}, u32[]{:S(2)}, u32[]{:S(2)}) collective-permute-start(bf16[16,16,128]{2,1,0:T(8,128)(2,1)S(1)} %reshape.46), channel_id=1, source_target_pairs={{0,7},{1,0},{2,1},{3,2},{4,3},{5,4},{6,5},{7,6},{8,15},{9,8},{10,9... | collective-permute-start | bytes 196616 | tf_op jit(solution)/shard_map/ppermute | solution.py:215
  31.1 9.0 %collective-permute-start = (bf16[16,16,128]{2,1,0:T(8,128)(2,1)S(1)}, bf16[16,16,128]{2,1,0:T(8,128)(2,1)S(1)}, u32[]{:S(2)}, u32[]{:S(2)}) collective-permute-start(bf16[16,16,128]{2,1,0:T(8,128)(2,1)S(1)} %reshape.46), channel_id=1, source_target_pairs={{0,1},{1,2},{2,3},{3,4},{4,5},{5,6},{6,7},{7,0},{8,9},{9,10},{10,1... | collective-permute-start | bytes 196616 | tf_op jit(solution)/shard_map/ppermute | solution.py:215
  33.0 31.7 %collective-permute-start.4 = (bf16[2,2,384,384]{3,2,1,0:T(8,128)(2,1)}, bf16[2,2,384,384]{3,2,1,0:T(8,128)(2,1)}, u32[]{:S(2)}, u32[]{:S(2)}) collective-permute-start(bf16[2,2,384,384]{3,2,1,0:T(8,128)(2,1)} %own_ref.1), channel_id=1, source_target_pairs={{0,1},{1,2},{2,3},{3,4},{4,5},{5,6},{6,7},{7,0},{8,9},{9,10},{10,1... | collective-permute-start | bytes 3538952 | tf_op jit(solution)/shard_map/ppermute | solution.py:215
  35.8 33.8 %collective-permute-start.5 = (bf16[2,2,384,384]{3,2,1,0:T(8,128)(2,1)}, bf16[2,2,384,384]{3,2,1,0:T(8,128)(2,1)}, u32[]{:S(2)}, u32[]{:S(2)}) collective-permute-start(bf16[2,2,384,384]{3,2,1,0:T(8,128)(2,1)} %own_ref.1), channel_id=1, source_target_pairs={{0,7},{1,0},{2,1},{3,2},{4,3},{5,4},{6,5},{7,6},{8,15},{9,8},{10,9... | collective-permute-start | bytes 3538952 | tf_op jit(solution)/shard_map/ppermute | solution.py:215
  40.0 24.5 %copy-start.2 = (s32[128]{0:T(128)S(1)}, s32[128]{0:T(128)}, u32[]{:S(2)}) copy-start(s32[128]{0:T(128)} %param.9) | copy-start | bytes 1540
  58.2 23.6 %all-to-all-start.1 = ((bf16[64,32,128]{2,1,0:T(8,128)(2,1)}), bf16[64,32,128]{2,1,0:T(8,128)(2,1)}, u32[]{:S(2)}, u32[]{:S(2)}) async-start(bf16[64,32,128]{2,1,0:T(8,128)(2,1)} %gather_fusion), calls=%async_computation.1 | async-start | bytes 1048576 | tf_op jit(solution)/shard_map/all_to_all | solution.py:238
  66.5 24.3 %collective-permute-start.6 = (bf16[2,384,384]{2,1,0:T(8,128)(2,1)}, bf16[2,384,384]{2,1,0:T(8,128)(2,1)}, u32[]{:S(2)}, u32[]{:S(2)}) collective-permute-start(bf16[2,384,384]{2,1,0:T(8,128)(2,1)} %pick.2), channel_id=1, source_target_pairs={{0,1},{1,2},{2,3},{3,4},{4,5},{5,6},{6,7},{7,0},{8,9},{9,10},{10,1... | collective-permute-start | bytes 1769480 | tf_op jit(solution)/shard_map/ppermute | solution.py:215
  71.5 19.3 %collective-permute-start.7 = (bf16[2,384,384]{2,1,0:T(8,128)(2,1)}, bf16[2,384,384]{2,1,0:T(8,128)(2,1)}, u32[]{:S(2)}, u32[]{:S(2)}) collective-permute-start(bf16[2,384,384]{2,1,0:T(8,128)(2,1)} %pick.3), channel_id=1, source_target_pairs={{0,7},{1,0},{2,1},{3,2},{4,3},{5,4},{6,5},{7,6},{8,15},{9,8},{10,9... | collective-permute-start | bytes 1769480 | tf_op jit(solution)/shard_map/ppermute | solution.py:215
  96.1 42.8 %copy-start.1 = (s32[64,3]{0,1:T(4,128)S(1)}, s32[64,3]{0,1:T(4,128)}, u32[]{:S(2)}) copy-start(s32[64,3]{0,1:T(4,128)} %param.8) | copy-start | bytes 2308

commit v8 on v7

--- a/solution.py
+++ b/solution.py
@@ -71,7 +71,7 @@
                 target[pl.ds(row, 128), term * 384 : term * 384 + 384] = product[kk, :, half].reshape(128, 384)
         return carry
 
-    lax.fori_loop(0, 8, left_group, 0, unroll=2)
+    lax.fori_loop(0, 8, left_group, 0, unroll=4)
     for copy in copies:
         copy.wait()
 
@@ -209,17 +209,51 @@
     )(right)
 
 
+def route_kernel(table_ref, slot_ref, psi_ref, out_ref, left_ref, source_ref):
+    def clear(owner, carry):
+        source_ref[owner] = 0
+        left_ref[owner] = 0
+        return carry
+
+    def enter(block, carry):
+        @pl.when(table_ref[2, block] == slot_ref[0])
+        def _():
+            owner = table_ref[1, block]
+            source_ref[owner] = block
+            left_ref[owner] = table_ref[0, block]
+
+        return carry
+
+    def move(owner, carry):
+        out_ref[owner] = psi_ref[source_ref[owner]]
+        return carry
+
+    lax.fori_loop(0, 64, clear, 0, unroll=8)
+    lax.fori_loop(0, 64, enter, 0, unroll=8)
+    lax.fori_loop(0, 64, move, 0, unroll=4)
+
+
+def route(table, slot, psi):
+    vmem = pl.BlockSpec(memory_space=pltpu.VMEM)
+    smem = pl.BlockSpec(memory_space=pltpu.SMEM)
+    return pl.pallas_call(
+        route_kernel,
+        out_shape=[jax.ShapeDtypeStruct((64, 32, 384), BF16), jax.ShapeDtypeStruct((64,), jnp.int32)],
+        in_specs=[smem, smem, vmem],
+        out_specs=[vmem, smem],
+        scratch_shapes=[pltpu.SMEM((64,), jnp.int32)],
+        compiler_params=pltpu.CompilerParams(vmem_limit_bytes=8 << 20),
+        name="route",
+    )(table, slot, psi)
+
+
 def per_device(psi, left, right, left_table, right_table):
     me = lax.axis_index("op")
     slot, half = (me >> 1) & 1, me & 1
     hop = lambda value, step: lax.ppermute(value, "op", [(i, (i + step) % 8) for i in range(8)])
 
-    match = (left_table[:, 1:2] == jnp.arange(64)[None, :]) & (left_table[:, 2:3] == slot)
-    source = jnp.sum(jnp.where(match, jnp.arange(64)[:, None], 0), axis=0)
-    left_of = jnp.sum(jnp.where(match, left_table[:, :1], 0), axis=0)
-    psi_there = lax.all_to_all(
-        psi.at[source].get(mode="promise_in_bounds"), "sec", split_axis=0, concat_axis=0, tiled=True
-    )
+    psi_here, left_of = route(left_table.T, slot.reshape(1), psi)
+    psi_there = lax.all_to_all(psi_here, "sec", split_axis=0, concat_axis=0, tiled=True)
 
     dense = left.reshape(16, 2, 2, 16, 32).transpose(0, 3, 2, 1, 4).reshape(16, 16, 128)
     before, after, two_before, two_after = hop(dense, 1), hop(dense, -1), hop(dense, 2), hop(dense, -2)

time: 141 us -> 144 us (1.021)
  Pallas kernels: 19.2 us -> 20.8 us
  blocking collectives: 42.8 us -> 44.3 us
    unnamed x6 -> x16, local copies, waits for them, and re-layouts: 0.02 us -> 4.15 us
    pallas_call x0 -> x1, Pallas kernels: none -> 2.54 us  [route(): pl.pallas_call(route_kernel, out_shape=[jax.ShapeDtypeStruct((64, 32, 384...]
    gather x1 -> x0, local copies, waits for them, and re-layouts: 1.89 us -> none  [per_device(): psi.at[source].get(mode='promise_in_bounds')]
    all_to_all x1, blocking collectives: 42.8 us -> 44.3 us  [per_device(): lax.all_to_all(pieces.reshape(512, 3, 2, 128), ('sec', 'op'), split_axis=...]
  transfers between devices with their start and end apart: 10 -> 10, of which waited for: 2 -> 2; matrix products, arithmetic and copies ran while one was open for 3% -> 2% of each run, Pallas kernels for 9% -> 8%
where the time goes in v8:
time: 144 us; the launch traced here: 143 us
  starting transfers between devices  47.8 us (33%)
  blocking collectives  44.3 us (31%)
  waiting for transfers between devices  22.7 us (16%)
  Pallas kernels  20.8 us (14%)
  local copies, waits for them, and re-layouts  6.27 us (4%)
    all_to_all x1, blocking collectives, per_device(): lax.all_to_all(pieces.reshape(512, 3, 2, 128), ('sec', 'op'), split_axis=...  44.3 us
    ppermute x8, starting transfers between devices, per_device(): lax.ppermute(value, 'op', [(i, (i + step) % 8) for i in range(8)])  26.7 us
    all_to_all x1, waiting for transfers between devices, per_device(): lax.all_to_all(psi_here, 'sec', split_axis=0, concat_axis=0, tiled=True)  17.4 us
    all_to_all x1, starting transfers between devices, per_device(): lax.all_to_all(psi_here, 'sec', split_axis=0, concat_axis=0, tiled=True)  15 us
    pallas_call x1, Pallas kernels, contract(): pl.pallas_call(first_kernel, out_shape=[jax.ShapeDtypeStruct((1024, 384),...  8.17 us
    all_to_all x1, starting transfers between devices, per_device(): lax.all_to_all(left_here, 'sec', split_axis=0, concat_axis=0, tiled=True)  6.12 us
    all_to_all x1, waiting for transfers between devices, per_device(): lax.all_to_all(left_here, 'sec', split_axis=0, concat_axis=0, tiled=True)  5.29 us
    pallas_call x1, Pallas kernels, contract(): pl.pallas_call(last_kernel, out_shape=jax.ShapeDtypeStruct((3072, 128), B...  5.24 us
  transfers between devices with their start and end apart: 10, of which 2 were waited for; matrix products, arithmetic and copies ran while one was open for 2% of the time, Pallas kernels for 8%

profile of v8, /device:TPU:1, one launch (start us, length us, event | category | flops | bytes accessed | tf_op | source)
XLA Modules:
  0.0 142.9 jit_solution(14040488166001936914)
XLA Ops:
  0.0 1.4 copy-done
  1.4 0.7 copy-done.1
  2.1 2.5 %route.1 = (bf16[64,32,384]{2,1,0:T(8,128)(2,1)}, s32[64]{0:T(128)S(1)}) custom-call(s32[3,64]{1,0:T(4,128)S(1)} %bitcast.11, s32[1]{0:T(128)} %bitcast.3.slot_ref, bf16[64,32,384]{2,1,0:T(8,128)(2,1)S(1)} %copy-done), custom_call_target="tpu_custom_call" | custom-call | tf_op jit(solution)/shard_map/route/pallas_call | solution.py:239
  4.6 15.0 %all-to-all-start = ((bf16[64,32,384]{2,1,0:T(8,128)(2,1)}), bf16[64,32,384]{2,1,0:T(8,128)(2,1)S(1)}, u32[]{:S(2)}, u32[]{:S(2)}) async-start(bf16[64,32,384]{2,1,0:T(8,128)(2,1)} %get-tuple-element.12), calls=%async_computation | async-start | bytes 3145728 | tf_op jit(solution)/shard_map/all_to_all | solution.py:256
  20.1 4.2 %collective-permute-start.2 = (bf16[16,16,128]{2,1,0:T(8,128)(2,1)S(1)}, bf16[16,16,128]{2,1,0:T(8,128)(2,1)S(1)}, u32[]{:S(2)}, u32[]{:S(2)}) collective-permute-start(bf16[16,16,128]{2,1,0:T(8,128)(2,1)S(1)} %reshape.23), channel_id=1, source_target_pairs={{0,2},{1,3},{2,4},{3,5},{4,6},{5,7},{6,0},{7,1},{8,10},{9,11},{10,... | collective-permute-start | bytes 196616 | tf_op jit(solution)/shard_map/ppermute | solution.py:253
  24.3 3.6 %collective-permute-start.3 = (bf16[16,16,128]{2,1,0:T(8,128)(2,1)S(1)}, bf16[16,16,128]{2,1,0:T(8,128)(2,1)S(1)}, u32[]{:S(2)}, u32[]{:S(2)}) collective-permute-start(bf16[16,16,128]{2,1,0:T(8,128)(2,1)S(1)} %reshape.23), channel_id=1, source_target_pairs={{0,6},{1,7},{2,0},{3,1},{4,2},{5,3},{6,4},{7,5},{8,14},{9,15},{10,... | collective-permute-start | bytes 196616 | tf_op jit(solution)/shard_map/ppermute | solution.py:253
  27.9 3.5 %collective-permute-start.1 = (bf16[16,16,128]{2,1,0:T(8,128)(2,1)S(1)}, bf16[16,16,128]{2,1,0:T(8,128)(2,1)S(1)}, u32[]{:S(2)}, u32[]{:S(2)}) collective-permute-start(bf16[16,16,128]{2,1,0:T(8,128)(2,1)S(1)} %reshape.23), channel_id=1, source_target_pairs={{0,7},{1,0},{2,1},{3,2},{4,3},{5,4},{6,5},{7,6},{8,15},{9,8},{10,9... | collective-permute-start | bytes 196616 | tf_op jit(solution)/shard_map/ppermute | solution.py:253
  31.4 1.9 %collective-permute-start = (bf16[16,16,128]{2,1,0:T(8,128)(2,1)S(1)}, bf16[16,16,128]{2,1,0:T(8,128)(2,1)S(1)}, u32[]{:S(2)}, u32[]{:S(2)}) collective-permute-start(bf16[16,16,128]{2,1,0:T(8,128)(2,1)S(1)} %reshape.23), channel_id=1, source_target_pairs={{0,1},{1,2},{2,3},{3,4},{4,5},{5,6},{6,7},{7,0},{8,9},{9,10},{10,1... | collective-permute-start | bytes 196616 | tf_op jit(solution)/shard_map/ppermute | solution.py:253
  33.3 2.7 %collective-permute-start.4 = (bf16[2,2,384,384]{3,2,1,0:T(8,128)(2,1)}, bf16[2,2,384,384]{3,2,1,0:T(8,128)(2,1)S(1)}, u32[]{:S(2)}, u32[]{:S(2)}) collective-permute-start(bf16[2,2,384,384]{3,2,1,0:T(8,128)(2,1)} %own_ref.1), channel_id=1, source_target_pairs={{0,1},{1,2},{2,3},{3,4},{4,5},{5,6},{6,7},{7,0},{8,9},{9,10},{10,1... | collective-permute-start | bytes 3538952 | tf_op jit(solution)/shard_map/ppermute | solution.py:253
  36.1 3.8 %collective-permute-start.5 = (bf16[2,2,384,384]{3,2,1,0:T(8,128)(2,1)}, bf16[2,2,384,384]{3,2,1,0:T(8,128)(2,1)}, u32[]{:S(2)}, u32[]{:S(2)}) collective-permute-start(bf16[2,2,384,384]{3,2,1,0:T(8,128)(2,1)} %own_ref.1), channel_id=1, source_target_pairs={{0,7},{1,0},{2,1},{3,2},{4,3},{5,4},{6,5},{7,6},{8,15},{9,8},{10,9... | collective-permute-start | bytes 3538952 | tf_op jit(solution)/shard_map/ppermute | solution.py:253
  40.6 1.4 gather_fusion
  42.0 17.4 %all-to-all-done.psi_ref = bf16[64,32,384]{2,1,0:T(8,128)(2,1)S(1)} async-done(((bf16[64,32,384]{2,1,0:T(8,128)(2,1)}), bf16[64,32,384]{2,1,0:T(8,128)(2,1)S(1)}, u32[]{:S(2)}, u32[]{:S(2)}) %all-to-all-start) | async-done | bytes 1572896 | tf_op jit(solution)/shard_map/all_to_all | solution.py:256
  59.4 6.1 %all-to-all-start.1 = ((bf16[64,32,128]{2,1,0:T(8,128)(2,1)}), bf16[64,32,128]{2,1,0:T(8,128)(2,1)S(1)}, u32[]{:S(2)}, u32[]{:S(2)}) async-start(bf16[64,32,128]{2,1,0:T(8,128)(2,1)} %gather_fusion), calls=%async_computation.1 | async-start | bytes 1048576 | tf_op jit(solution)/shard_map/all_to_all | solution.py:272
  65.7 1.0 copy-done.3
  66.8 1.8 %pick.2 = bf16[2,384,384]{2,1,0:T(8,128)(2,1)} custom-call(bf16[2,2,384,384]{3,2,1,0:T(8,128)(2,1)} %copy-done.3), custom_call_target="tpu_custom_call" | custom-call | tf_op jit(solution)/shard_map/pick/pallas_call | solution.py:201
  68.6 3.2 %collective-permute-start.6 = (bf16[2,384,384]{2,1,0:T(8,128)(2,1)}, bf16[2,384,384]{2,1,0:T(8,128)(2,1)S(1)}, u32[]{:S(2)}, u32[]{:S(2)}) collective-permute-start(bf16[2,384,384]{2,1,0:T(8,128)(2,1)} %pick.2), channel_id=1, source_target_pairs={{0,1},{1,2},{2,3},{3,4},{4,5},{5,6},{6,7},{7,0},{8,9},{9,10},{10,1... | collective-permute-start | bytes 1769480 | tf_op jit(solution)/shard_map/ppermute | solution.py:253
  71.8 1.8 %pick.3 = bf16[2,384,384]{2,1,0:T(8,128)(2,1)} custom-call(bf16[2,2,384,384]{3,2,1,0:T(8,128)(2,1)} %collective-permute-done.5.after_ref.right_ref), custom_call_target="tpu_custom_call" | custom-call | tf_op jit(solution)/shard_map/pick/pallas_call | solution.py:201
  73.6 3.8 %collective-permute-start.7 = (bf16[2,384,384]{2,1,0:T(8,128)(2,1)}, bf16[2,384,384]{2,1,0:T(8,128)(2,1)S(1)}, u32[]{:S(2)}, u32[]{:S(2)}) collective-permute-start(bf16[2,384,384]{2,1,0:T(8,128)(2,1)} %pick.3), channel_id=1, source_target_pairs={{0,7},{1,0},{2,1},{3,2},{4,3},{5,4},{6,5},{7,6},{8,15},{9,8},{10,9... | collective-permute-start | bytes 1769480 | tf_op jit(solution)/shard_map/ppermute | solution.py:253
  77.6 5.3 %all-to-all-done.1.left_ref = bf16[64,32,128]{2,1,0:T(8,128)(2,1)S(1)} async-done(((bf16[64,32,128]{2,1,0:T(8,128)(2,1)}), bf16[64,32,128]{2,1,0:T(8,128)(2,1)S(1)}, u32[]{:S(2)}, u32[]{:S(2)}) %all-to-all-start.1) | async-done | bytes 524320 | tf_op jit(solution)/shard_map/all_to_all | solution.py:272
  82.9 8.2 %contract_first.1 = (f32[1024,384]{1,0:T(8,128)S(1)}, bf16[1024,768]{1,0:T(8,128)(2,1)S(1)}) custom-call(s32[64]{0:T(128)S(1)} %fusion.sector_ref, bf16[64,32,384]{2,1,0:T(8,128)(2,1)S(1)} %all-to-all-done.psi_ref, bf16[64,32,128]{2,1,0:T(8,128)(2,1)S(1)} %all-to-all-done.1.left_ref, bf16[2,2,384,384]{3,2,1,0:T(8,128)(2,1)} %own_ref.1, ...), custom_call_target="tpu_custom_call" | custom-call | flops 6000000000 | bytes 9000000 | tf_op jit(solution)/shard_map/contract_first/pallas_call | solution.py:136
  91.1 0.8 copy-done.6
  92.1 5.2 %contract_last.1 = bf16[3072,128]{1,0:T(8,128)(2,1)S(1)} custom-call(s32[64]{0:T(128)S(1)} %fusion.sector_ref, f32[1024,384]{1,0:T(8,128)S(1)} %get-tuple-element.15.sum_ref, bf16[1024,768]{1,0:T(8,128)(2,1)S(1)} %get-tuple-element.16.last_ref, bf16[2,384,384]{2,1,0:T(8,128)(2,1)} %copy-done.6, bf16[2,384,384]{2,1,0:T(8,128)(2,1)} %copy-done.7), custom_call_target="tpu_custom_call" | custom-call | flops 2000000000 | bytes 5000000 | tf_op jit(solution)/shard_map/contract_last/pallas_call | solution.py:150
  97.4 44.3 %all_to_all.15 = bf16[512,3,2,128]{3,2,1,0:T(2,128)(2,1)S(1)} all-to-all(bf16[512,3,2,128]{3,2,1,0:T(2,128)(2,1)S(1)} %bitcast.10), channel_id=1, replica_groups=mesh['sec'=64,'op'=8] {'sec','op'}, dimensions={0} | all-to-all | bytes 1572864 | tf_op jit(solution)/shard_map/all_to_all | solution.py:282
  141.7 1.3 collect.1
  (33 shorter events, 1.7 us)
Async XLA Ops:
  0.0 1.4 copy-start
  1.4 0.7 copy-start.1
  4.6 15.0 %copy-start.4 = (bf16[16,2,32,32]{3,2,1,0:T(8,128)(2,1)S(1)}, bf16[16,2,32,32]{3,2,1,0:T(8,128)(2,1)}, u32[]{:S(2)}) copy-start(bf16[16,2,32,32]{3,2,1,0:T(8,128)(2,1)} %param.6) | copy-start | bytes 196612
  4.6 54.8 %all-to-all-start = ((bf16[64,32,384]{2,1,0:T(8,128)(2,1)}), bf16[64,32,384]{2,1,0:T(8,128)(2,1)S(1)}, u32[]{:S(2)}, u32[]{:S(2)}) async-start(bf16[64,32,384]{2,1,0:T(8,128)(2,1)} %get-tuple-element.12), calls=%async_computation | async-start | bytes 3145728 | tf_op jit(solution)/shard_map/all_to_all | solution.py:256
  20.1 16.1 %collective-permute-start.2 = (bf16[16,16,128]{2,1,0:T(8,128)(2,1)S(1)}, bf16[16,16,128]{2,1,0:T(8,128)(2,1)S(1)}, u32[]{:S(2)}, u32[]{:S(2)}) collective-permute-start(bf16[16,16,128]{2,1,0:T(8,128)(2,1)S(1)} %reshape.23), channel_id=1, source_target_pairs={{0,2},{1,3},{2,4},{3,5},{4,6},{5,7},{6,0},{7,1},{8,10},{9,11},{10,... | collective-permute-start | bytes 196616 | tf_op jit(solution)/shard_map/ppermute | solution.py:253
  24.3 15.8 %collective-permute-start.3 = (bf16[16,16,128]{2,1,0:T(8,128)(2,1)S(1)}, bf16[16,16,128]{2,1,0:T(8,128)(2,1)S(1)}, u32[]{:S(2)}, u32[]{:S(2)}) collective-permute-start(bf16[16,16,128]{2,1,0:T(8,128)(2,1)S(1)} %reshape.23), channel_id=1, source_target_pairs={{0,6},{1,7},{2,0},{3,1},{4,2},{5,3},{6,4},{7,5},{8,14},{9,15},{10,... | collective-permute-start | bytes 196616 | tf_op jit(solution)/shard_map/ppermute | solution.py:253
  27.9 12.4 %collective-permute-start.1 = (bf16[16,16,128]{2,1,0:T(8,128)(2,1)S(1)}, bf16[16,16,128]{2,1,0:T(8,128)(2,1)S(1)}, u32[]{:S(2)}, u32[]{:S(2)}) collective-permute-start(bf16[16,16,128]{2,1,0:T(8,128)(2,1)S(1)} %reshape.23), channel_id=1, source_target_pairs={{0,7},{1,0},{2,1},{3,2},{4,3},{5,4},{6,5},{7,6},{8,15},{9,8},{10,9... | collective-permute-start | bytes 196616 | tf_op jit(solution)/shard_map/ppermute | solution.py:253
  31.4 9.0 %collective-permute-start = (bf16[16,16,128]{2,1,0:T(8,128)(2,1)S(1)}, bf16[16,16,128]{2,1,0:T(8,128)(2,1)S(1)}, u32[]{:S(2)}, u32[]{:S(2)}) collective-permute-start(bf16[16,16,128]{2,1,0:T(8,128)(2,1)S(1)} %reshape.23), channel_id=1, source_target_pairs={{0,1},{1,2},{2,3},{3,4},{4,5},{5,6},{6,7},{7,0},{8,9},{9,10},{10,1... | collective-permute-start | bytes 196616 | tf_op jit(solution)/shard_map/ppermute | solution.py:253
  33.3 32.4 %collective-permute-start.4 = (bf16[2,2,384,384]{3,2,1,0:T(8,128)(2,1)}, bf16[2,2,384,384]{3,2,1,0:T(8,128)(2,1)S(1)}, u32[]{:S(2)}, u32[]{:S(2)}) collective-permute-start(bf16[2,2,384,384]{3,2,1,0:T(8,128)(2,1)} %own_ref.1), channel_id=1, source_target_pairs={{0,1},{1,2},{2,3},{3,4},{4,5},{5,6},{6,7},{7,0},{8,9},{9,10},{10,1... | collective-permute-start | bytes 3538952 | tf_op jit(solution)/shard_map/ppermute | solution.py:253
  36.1 35.7 %collective-permute-start.5 = (bf16[2,2,384,384]{3,2,1,0:T(8,128)(2,1)}, bf16[2,2,384,384]{3,2,1,0:T(8,128)(2,1)}, u32[]{:S(2)}, u32[]{:S(2)}) collective-permute-start(bf16[2,2,384,384]{3,2,1,0:T(8,128)(2,1)} %own_ref.1), channel_id=1, source_target_pairs={{0,7},{1,0},{2,1},{3,2},{4,3},{5,4},{6,5},{7,6},{8,15},{9,8},{10,9... | collective-permute-start | bytes 3538952 | tf_op jit(solution)/shard_map/ppermute | solution.py:253
  40.3 25.3 %copy-start.5 = (s32[128]{0:T(128)S(1)}, s32[128]{0:T(128)}, u32[]{:S(2)}) copy-start(s32[128]{0:T(128)} %param.9) | copy-start | bytes 1540
  59.4 23.5 %all-to-all-start.1 = ((bf16[64,32,128]{2,1,0:T(8,128)(2,1)}), bf16[64,32,128]{2,1,0:T(8,128)(2,1)S(1)}, u32[]{:S(2)}, u32[]{:S(2)}) async-start(bf16[64,32,128]{2,1,0:T(8,128)(2,1)} %gather_fusion), calls=%async_computation.1 | async-start | bytes 1048576 | tf_op jit(solution)/shard_map/all_to_all | solution.py:272
  65.7 1.0 copy-start.3
  68.6 22.5 %collective-permute-start.6 = (bf16[2,384,384]{2,1,0:T(8,128)(2,1)}, bf16[2,384,384]{2,1,0:T(8,128)(2,1)S(1)}, u32[]{:S(2)}, u32[]{:S(2)}) collective-permute-start(bf16[2,384,384]{2,1,0:T(8,128)(2,1)} %pick.2), channel_id=1, source_target_pairs={{0,1},{1,2},{2,3},{3,4},{4,5},{5,6},{6,7},{7,0},{8,9},{9,10},{10,1... | collective-permute-start | bytes 1769480 | tf_op jit(solution)/shard_map/ppermute | solution.py:253
  73.6 17.5 %collective-permute-start.7 = (bf16[2,384,384]{2,1,0:T(8,128)(2,1)}, bf16[2,384,384]{2,1,0:T(8,128)(2,1)S(1)}, u32[]{:S(2)}, u32[]{:S(2)}) collective-permute-start(bf16[2,384,384]{2,1,0:T(8,128)(2,1)} %pick.3), channel_id=1, source_target_pairs={{0,7},{1,0},{2,1},{3,2},{4,3},{5,4},{6,5},{7,6},{8,15},{9,8},{10,9... | collective-permute-start | bytes 1769480 | tf_op jit(solution)/shard_map/ppermute | solution.py:253
  91.1 0.8 copy-start.6
  91.1 1.0 copy-start.7
  97.4 44.3 %copy-start.2 = (s32[64,3]{0,1:T(4,128)S(1)}, s32[64,3]{0,1:T(4,128)}, u32[]{:S(2)}) copy-start(s32[64,3]{0,1:T(4,128)} %param.8) | copy-start | bytes 2308
